TPU v7x, 32 devices: a whole 2x2x4 slice. The times are simulated.
32 devices in a mesh: leaf: 8 (over z, y), grp: 4 (over x, core).
Axes of the slice: x: 2, y: 2, z: 4, core: 2. Of those that a mesh axis runs over, the one named last changes fastest.
Arguments:
- leaf_rhs: float32 [8, 8, 128, 512], P('leaf', 'grp'), may hold values from -6 to 6
- leaf_inv: float32 [8, 8, 128, 128], P('leaf', 'grp')
- coupling: float32 [8, 8, 128, 128], P('leaf', 'grp'), may hold values from -0.1875 to 0.1875
- pattern: int32 [8, 8], P('leaf', 'grp'), may hold values 0 or 1
- sep_rhs: float32 [8, 128, 512], P('leaf'), may hold values from -6 to 6
- sep_inv: float32 [8, 128, 128], P('leaf')
- chain_link: float32 [8, 128, 128], P('leaf'), may hold values from -0.4375 to 0.4375
Outputs:
- leaf_solution: float32 [8, 8, 128, 512], P('leaf', 'grp')
- sep_solution: float32 [8, 128, 512], P('leaf', None, 'grp')
All inputs are finite; a program needn't handle non-finite values. No bound on the sum of `pattern` on one device may be relied on, other than what follows from the above.
Results may differ from a plain program's by a relative error of at most 0.0003.
Values sent between devices are 32-bit elements; how exact they have to be, the bound alone decides.
No kernel may reach another device: no remote copies, remote signals or barrier semaphores. Data moves between devices by JAX's collectives and lax.ppermute only.
A program may use at most 192 MiB of HBM per device.

v0:
```python
import jax
import jax.numpy as jnp
from jax import lax
from jax.sharding import PartitionSpec as P

HIGH = lax.Precision.HIGHEST


def entering(part, axis, combine, identity, reverse):
    count = lax.axis_size(axis)
    place = lax.axis_index(axis)
    ahead = count - 1 - place if reverse else place
    gathered = jax.tree.map(lambda a: lax.all_gather(a, axis), part)
    state = jax.tree.map(lambda a, e: jnp.zeros_like(a) + jnp.asarray(e, a.dtype), part, identity)

    def one(turn, state):
        source = count - 1 - turn if reverse else turn
        return combine(
            state, jax.tree.map(lambda a: lax.dynamic_index_in_dim(a, source, 0, False), gathered)
        )

    return lax.fori_loop(0, ahead, one, state)


def compose(earlier, later):
    first_map, first_off = earlier
    second_map, second_off = later
    joined = jnp.matmul(second_map, first_map, precision=HIGH)
    shifted = jnp.matmul(second_map, first_off, precision=HIGH) + second_off
    return (joined, shifted)


def shards(leaf_rhs, leaf_inv, coupling, pattern, sep_rhs, sep_inv, chain_link):
    leaf_y = jnp.einsum("kij,kjr->kir", leaf_inv[0], leaf_rhs[0], precision=HIGH)
    present = pattern[0].astype(jnp.float32)[:, None, None]
    partial_sum = jnp.einsum("kij,kjr->ir", coupling[0] * present, leaf_y, precision=HIGH)
    inverse = sep_inv[0]
    link = chain_link[0]
    update = lax.psum_scatter(partial_sum, "grp", scatter_dimension=1, tiled=True)
    width_cols = update.shape[1]
    offset = lax.axis_index("grp") * width_cols
    rhs = lax.dynamic_slice_in_dim(sep_rhs[0], offset, width_cols, 1)
    order = inverse.shape[0]
    eye = jnp.eye(order, dtype=jnp.float32)
    start_off = jnp.zeros(update.shape, jnp.float32)
    step_map = -jnp.matmul(inverse, link, precision=HIGH)
    step_off = jnp.matmul(inverse, rhs - update, precision=HIGH)
    before = entering((step_map, step_off), "leaf", compose, (eye, start_off), False)
    sep_y = jnp.matmul(step_map, before[1], precision=HIGH) + step_off
    back_map = step_map.T
    back_off = -jnp.matmul(back_map, sep_y, precision=HIGH)
    after = entering((back_map, back_off), "leaf", compose, (eye, start_off), True)
    solved = jnp.matmul(inverse.T, sep_y - after[1], precision=HIGH)
    full_solved = lax.all_gather(solved, "grp", axis=1, tiled=True)
    back = jnp.einsum("kji,jr->kir", coupling[0], full_solved, precision=HIGH)
    leaf_solution = jnp.einsum("kji,kjr->kir", leaf_inv[0], leaf_y - present * back, precision=HIGH)
    return (leaf_solution[None], solved[None])


def solution(mesh):
    in_specs = (
        P("leaf", "grp", None, None),
        P("leaf", "grp", None, None),
        P("leaf", "grp", None, None),
        P("leaf", "grp"),
        P("leaf", None, None),
        P("leaf", None, None),
        P("leaf", None, None),
    )
    out_specs = (P("leaf", "grp", None, None), P("leaf", None, "grp"))
    return jax.shard_map(shards, mesh=mesh, in_specs=in_specs, out_specs=out_specs, check_vma=False)
```

profile of v0, /device:TPU:0, one launch (start us, length us, event | category | flops | bytes accessed | tf_op | source)
XLA Modules:
  0.0 160.9 jit_solution(8537445943247184277)
XLA Ops:
  7.2 0.7 convert_bitcast_fusion
  7.9 0.3 copy-done
  8.2 1.5 fusion.8
  9.8 1.1 convolution_bitcast_fusion.1
  10.9 0.8 copy-done.1
  12.0 33.0 %all-gather.2 = f32[1024,128]{0,1:T(8,128)S(1)} all-gather(f32[128,128]{0,1:T(8,128)S(1)} %bitcast.82), channel_id=4, replica_groups=mesh['leaf'=8,'grp'=4] {'leaf'}, dimensions={0}, use_global_device_ids=true | all-gather | bytes 589824 | tf_op jit(solution)/shard_map/all_gather | solution.py:13
  45.2 31.3 %all-gather = f32[1024,128]{1,0:T(8,128)S(1)} all-gather(f32[128,128]{1,0:T(8,128)S(1)} %convolution_negate_fusion.1), channel_id=2, replica_groups=mesh['leaf'=8,'grp'=4] {'leaf'}, dimensions={0}, use_global_device_ids=true | all-gather | bytes 589824 | tf_op jit(solution)/shard_map/all_gather | solution.py:13
  76.5 1.2 convolution_bitcast_fusion.2
  77.6 31.4 %all-gather.1 = f32[1024,128]{0,1:T(8,128)S(1)} all-gather(f32[128,128]{0,1:T(8,128)S(1)} %convolution_bitcast_fusion.2), channel_id=3, replica_groups=mesh['leaf'=8,'grp'=4] {'leaf'}, dimensions={0}, use_global_device_ids=true | all-gather | bytes 589824 | tf_op jit(solution)/shard_map/all_gather | solution.py:13
  109.2 0.3 convolution_add_fusion.2
  109.5 0.3 convolution_negate_fusion
  109.8 32.7 %all-gather.3 = f32[1024,128]{1,0:T(8,128)S(1)} all-gather(f32[128,128]{1,0:T(8,128)S(1)} %convolution_negate_fusion), channel_id=5, replica_groups=mesh['leaf'=8,'grp'=4] {'leaf'}, dimensions={0}, use_global_device_ids=true | all-gather | bytes 589824 | tf_op jit(solution)/shard_map/all_gather | solution.py:13
  142.6 1.7 %while.27 = (s32[]{:T(128)}, f32[128,128]{1,0:T(8,128)S(1)}, s32[]{:T(128)}, f32[8,128,128]{2,1,0:T(8,128)S(1)}, f32[8,128,128]{2,1,0:T(8,128)S(1)}, /*index=5*/s32[]{:T(128)}, s32[]{:T(128)}, s32[]{:T(128)}, s32[]{:T(128)}) while((s32[]{:T(128)}, f32[128,128]{1,0:T(8,128)S(1)}, s32[]{:T(128)}, f32[8,128,128]{2,1,0:T(8,128)S(1)}, ...), condition=%wide.region_4.5_spmd, body=%wide.region_3.4_spmd.sunk | while | flops 25182212 | bytes 394379 | solution.py:22
  142.6 0.2 convolution_add_fusion.6
  142.8 0.2 convolution_add_fusion.6
  143.1 0.2 convolution_add_fusion.6
  143.8 0.2 convolution_add_fusion.6
  144.4 0.2 fusion.15
  144.6 5.8 %all_gather.35 = f32[128,512]{0,1:T(8,128)S(1)} all-gather(f32[128,128]{0,1:T(8,128)S(1)} %bitcast.87), channel_id=1, replica_groups=mesh['leaf'=8,'grp'=4] {'grp'}, dimensions={1}, use_global_device_ids=true | all-gather | bytes 327680 | tf_op jit(solution)/shard_map/all_gather | solution.py:54
  150.4 0.6 fusion.7
  151.1 0.3 copy-done.2
  151.3 1.0 convolution_bitcast_fusion
  152.3 1.0 copy.14
  153.3 0.7 copy.15
  (27 shorter events, 1.5 us)
Async XLA Ops:
  7.2 1.1 copy-start
  7.2 69.3 %reduce-scatter.2.cloned.1.call-start = ((), (), s32[]{:S(2)}) async-start(), calls=%async_computation.1 | async-start | bytes 327680 | tf_op jit(solution)/shard_map/reduce_scatter | solution.py:39
  8.2 1.5 copy-start.3
  10.9 0.8 copy-start.1
  10.9 0.9 copy-start.4
  150.4 0.9 copy-start.2
Sparse Core Ops, SparseCore 0:
  11.1 22.7 reduce-scatter.1
where the time goes:
time: 161 us
  blocking collectives  134 us (83%)
  between operations  14.2 us (9%)
  matrix products  7.86 us (5%)
  local copies, waits for them, and re-layouts  3.67 us (2%)
    all_gather x4, blocking collectives, entering(): gathered = jax.tree.map(lambda a: lax.all_gather(a, axis), part)  128 us
    all_gather x1, blocking collectives, shards(): full_solved = lax.all_gather(solved, 'grp', axis=1, tiled=True)  5.79 us
  transfers between devices with their start and end apart: 1, of which 0 were waited for; matrix products, arithmetic and copies ran while one was open for 0% of the time, Pallas kernels for 0%

commit v1 on v0

v1 whole, which is shorter than its diff:
```python
import jax
import jax.numpy as jnp
from jax import lax
from jax.experimental import pallas as pl
from jax.experimental.pallas import tpu as pltpu
from jax.sharding import PartitionSpec as P

HIGH = lax.Precision.HIGHEST
F32 = jnp.float32
VMEM = pl.BlockSpec(memory_space=pltpu.VMEM)
SMEM = pl.BlockSpec(memory_space=pltpu.SMEM)


def dot(a, b):
    return jnp.dot(a, b, precision=HIGH, preferred_element_type=F32)


def dot_ta(a, b):
    return lax.dot_general(
        a, b, (((0,), (0,)), ((), ())), precision=HIGH, preferred_element_type=F32
    )


def dot_tb(a, b):
    return lax.dot_general(
        a, b, (((1,), (1,)), ((), ())), precision=HIGH, preferred_element_type=F32
    )


def shaped(*shape):
    return jax.ShapeDtypeStruct(shape, F32)


def call(body, outs, flops, moved, *args):
    return pl.pallas_call(
        body,
        out_shape=outs,
        in_specs=[SMEM if a.dtype == jnp.int32 else VMEM for a in args],
        out_specs=jax.tree.map(lambda _: VMEM, outs),
        cost_estimate=pl.CostEstimate(flops=flops, bytes_accessed=moved, transcendentals=0),
        compiler_params=pltpu.CompilerParams(vmem_limit_bytes=48 << 20),
    )(*args)


def map_rows(place, inverse, link, out):
    rows = out.shape[0]
    start = pl.multiple_of(place[1] * rows, rows)
    out[...] = -dot(inverse[0, pl.ds(start, rows), :], link[0])


def partial_sums(place, pattern, rhs, leaf_inv, coupling, inverse, kept, sent, down):
    count, order = down.shape[0], down.shape[1]
    groups = kept.shape[0] * 2
    for k in range(count):
        present = pattern[0, k].astype(F32)
        mixed = dot(coupling[0, k] * present, leaf_inv[0, k])
        down[k] = dot(inverse[0], mixed)
    width = kept.shape[2]
    for slot in range(groups):
        start = pl.multiple_of((place[1] ^ slot) * width, width)
        total = dot(down[0], rhs[0, 0, :, pl.ds(start, width)])
        for k in range(1, count):
            total += dot(down[k], rhs[0, k, :, pl.ds(start, width)])
        (sent if slot % 2 else kept)[slot // 2] = total


def leaf_base(rhs, leaf_inv, base):
    for k in range(base.shape[0]):
        base[k] = dot_ta(leaf_inv[0, k], dot(leaf_inv[0, k], rhs[0, k]))


def own_columns(place, rhs, inverse, out):
    width = out.shape[1]
    start = pl.multiple_of(place[1] * width, width)
    out[...] = dot(inverse[0], rhs[0, :, pl.ds(start, width)])


def operator_row(place, maps, row, held):
    groups, sections, rows, order = maps.shape
    me, mine = place[0], place[1]
    diagonal = (
        lax.broadcasted_iota(jnp.int32, (order, order), 0)
        == lax.broadcasted_iota(jnp.int32, (order, order), 1)
    ).astype(F32)

    def slot_of(quarter):
        far = quarter ^ mine
        index, bit, low = 0, groups // 2, 1
        while bit:
            index = index + (far // bit) % 2 * low
            bit, low = bit // 2, low * 2
        return index

    def load(section):
        return jnp.concatenate(
            [maps[slot_of(q), section ^ me] for q in range(groups)], axis=0
        )

    held[0] = diagonal * (me == 0).astype(F32)

    @pl.loop(1, sections, unroll=sections <= 8)
    def _(section):
        reached = dot_tb(held[section - 1], load(section))
        held[section] = reached + diagonal * (me == section).astype(F32)

    row[sections - 1] = held[sections - 1]

    @pl.loop(0, sections - 1, unroll=sections <= 8)
    def _(turn):
        section = sections - 2 - turn
        row[section] = held[section] + dot(row[section + 1], load(section + 1))


def apply_row(row, offsets, out):
    total = dot(row[0], offsets[0])
    for section in range(1, row.shape[0]):
        total += dot(row[section], offsets[section])
    out[...] = total


def finish(place, base, down, inverse, spread, leaves, solved):
    groups, width = spread.shape[0], spread.shape[2]
    for j in range(groups):
        for k in range(base.shape[0]):
            cols = slice(j * width, (j + 1) * width)
            leaves[0, k, :, cols] = base[k, :, cols] - dot_ta(down[k], spread[j])
    solved[0] = dot_ta(inverse[0], spread[place[1]])


def swap(value, axis, bit):
    count = lax.axis_size(axis)
    return lax.ppermute(value, axis, [(i, i ^ bit) for i in range(count)])


def shards(leaf_rhs, leaf_inv, coupling, pattern, sep_rhs, sep_inv, chain_link):
    sections, groups = lax.axis_size("leaf"), lax.axis_size("grp")
    count, order, columns = leaf_rhs.shape[1:]
    width = columns // groups
    place = jnp.stack([lax.axis_index("leaf"), lax.axis_index("grp")]).astype(jnp.int32)
    cube = 2 * order**3

    maps = call(
        map_rows, shaped(order // groups, order), cube // groups, 3 * order * order * 4,
        place, sep_inv, chain_link,
    )[None]
    bit = 1
    while bit < sections:
        maps = jnp.concatenate([maps, swap(maps, "leaf", bit)], axis=0)
        bit *= 2
    maps = maps[None]
    bit = groups // 2
    while bit:
        maps = jnp.concatenate([maps, swap(maps, "grp", bit)], axis=0)
        bit //= 2
    row = pl.pallas_call(
        operator_row,
        out_shape=shaped(sections, order, order),
        in_specs=[SMEM, VMEM],
        out_specs=VMEM,
        scratch_shapes=[pltpu.VMEM((sections, order, order), F32)],
        cost_estimate=pl.CostEstimate(
            flops=2 * sections * cube, bytes_accessed=2 * maps.size * 4, transcendentals=0
        ),
        compiler_params=pltpu.CompilerParams(vmem_limit_bytes=48 << 20),
    )(place, maps)

    half = shaped(groups // 2, order, width)
    kept, sent, down = call(
        partial_sums,
        (half, half, shaped(count, order, order)),
        (2 * count + groups * count) * cube,
        3 * leaf_rhs.size * 4,
        place, pattern, leaf_rhs, leaf_inv, coupling, sep_inv,
    )
    own = call(
        own_columns, shaped(order, width), cube, 3 * order * order * 4, place, sep_rhs, sep_inv
    )
    bit = 1
    while bit < groups:
        total = kept + swap(sent, "grp", bit)
        kept, sent = total[0::2], total[1::2]
        bit *= 2
    offset = own - total[0]
    offsets = lax.all_to_all(
        jnp.broadcast_to(offset, (sections, order, width)), "leaf", 0, 0, tiled=True
    )
    base = call(
        leaf_base, shaped(count, order, columns), 8 * count * cube, 3 * leaf_rhs.size * 4,
        leaf_rhs, leaf_inv,
    )
    carried = call(
        apply_row, shaped(order, width), sections * cube, 2 * row.size * 4, row, offsets
    )
    spread = lax.all_gather(carried, "grp")
    return call(
        finish,
        (shaped(1, count, order, columns), shaped(1, order, width)),
        (4 * count + 1) * cube,
        3 * leaf_rhs.size * 4,
        place, base, down, sep_inv, spread,
    )


def solution(mesh):
    in_specs = (
        P("leaf", "grp", None, None),
        P("leaf", "grp", None, None),
        P("leaf", "grp", None, None),
        P("leaf", "grp"),
        P("leaf", None, None),
        P("leaf", None, None),
        P("leaf", None, None),
    )
    out_specs = (P("leaf", "grp", None, None), P("leaf", None, "grp"))
    return jax.shard_map(shards, mesh=mesh, in_specs=in_specs, out_specs=out_specs, check_vma=False)
```

time: 161 us -> 57.6 us (0.36)
  blocking collectives: 134 us -> 5.93 us
  waiting for transfers between devices: 0.02 us -> 18.5 us
  starting transfers between devices: 0.04 us -> 15.7 us
  between operations: 14.2 us -> 0.8 us
  Pallas kernels: 0 us -> 11.1 us
  matrix products: 7.86 us -> 0 us
    all_gather x5 -> x1, blocking collectives: 134 us -> 5.93 us  [shards(): spread = lax.all_gather(carried, 'grp')]
    ppermute x0 -> x7, waiting for transfers between devices: none -> 18.5 us  [swap(): return lax.ppermute(value, axis, [(i, i ^ bit) for i in range(count)])]
    pallas_call x0 -> x7, Pallas kernels: none -> 11.1 us  [the longest x6 7.02 us: call(): pl.pallas_call(body, out_shape=outs, in_specs=[SMEM if a.dtype == jnp.int...]
    ppermute x0 -> x7, starting transfers between devices: none -> 10.8 us  [swap(): return lax.ppermute(value, axis, [(i, i ^ bit) for i in range(count)])]
    dot_general x16 -> x0, matrix products: 7.86 us -> none  [the longest x1 1.51 us: shards(): jnp.einsum('kij,kjr->kir', leaf_inv[0], leaf_rhs[0], precision=HIGH)]
    all_to_all x0 -> x1, starting transfers between devices: none -> 4.88 us  [shards(): lax.all_to_all(jnp.broadcast_to(offset, (sections, order, width)), 'leaf'...]
    unnamed x12 -> x20, local copies, waits for them, and re-layouts: 3.14 us -> 4.28 us
  transfers between devices with their start and end apart: 1 -> 8, of which waited for: 0 -> 4; matrix products, arithmetic and copies ran while one was open for 0% -> 2% of each run, Pallas kernels for 0% -> 12%
where the time goes in v1:
time: 57.6 us; the launch traced here: 57.3 us
  waiting for transfers between devices  18.5 us (32%)
  starting transfers between devices  15.7 us (27%)
  Pallas kernels  11.1 us (19%)
  blocking collectives  5.93 us (10%)
  local copies, waits for them, and re-layouts  5.12 us (9%)
  between operations  0.8 us (1%)
    ppermute x7, waiting for transfers between devices, swap(): return lax.ppermute(value, axis, [(i, i ^ bit) for i in range(count)])  18.5 us
    ppermute x7, starting transfers between devices, swap(): return lax.ppermute(value, axis, [(i, i ^ bit) for i in range(count)])  10.8 us
    pallas_call x6, Pallas kernels, call(): pl.pallas_call(body, out_shape=outs, in_specs=[SMEM if a.dtype == jnp.int...  7.02 us
    all_gather x1, blocking collectives, shards(): spread = lax.all_gather(carried, 'grp')  5.93 us
    all_to_all x1, starting transfers between devices, shards(): lax.all_to_all(jnp.broadcast_to(offset, (sections, order, width)), 'leaf'...  4.88 us
    unnamed x20, local copies, waits for them, and re-layouts  4.28 us
    pallas_call x1, Pallas kernels, shards(): pl.pallas_call(operator_row, out_shape=shaped(sections, order, order), in...  4.07 us
  transfers between devices with their start and end apart: 8, of which 4 were waited for; matrix products, arithmetic and copies ran while one was open for 2% of the time, Pallas kernels for 12%

profile of v1, /device:TPU:0, one launch (start us, length us, event | category | flops | bytes accessed | tf_op | source)
XLA Modules:
  0.0 57.3 jit_solution(16151101030885790206)
XLA Ops:
  0.7 0.6 copy-done.9
  1.3 1.0 %copy-done = f32[1,2,128,512]{3,2,1,0:T(8,128)S(1)} copy-done((f32[1,2,128,512]{3,2,1,0:T(8,128)S(1)}, f32[1,2,128,512]{3,2,1,0:T(8,128)}, u32[]{:S(2)}) %copy-start) | copy-done | bytes 524312
  2.3 0.8 %copy-done.2 = f32[1,128,128]{2,1,0:T(8,128)S(1)} copy-done((f32[1,128,128]{2,1,0:T(8,128)S(1)}, f32[1,128,128]{2,1,0:T(8,128)}, u32[]{:S(2)}) %copy-start.2) | copy-done | bytes 65560
  3.2 0.9 %copy-done.4 = f32[1,2,128,128]{3,2,1,0:T(8,128)S(1)} copy-done((f32[1,2,128,128]{3,2,1,0:T(8,128)S(1)}, f32[1,2,128,128]{3,2,1,0:T(8,128)}, u32[]{:S(2)}) %copy-start.4) | copy-done | bytes 131096
  4.1 0.9 %copy-done.7 = f32[1,2,128,128]{3,2,1,0:T(8,128)S(1)} copy-done((f32[1,2,128,128]{3,2,1,0:T(8,128)S(1)}, f32[1,2,128,128]{3,2,1,0:T(8,128)}, u32[]{:S(2)}) %copy-start.7) | copy-done | bytes 131096
  5.0 1.6 %shard_map.87 = (f32[2,128,128]{2,1,0:T(8,128)S(1)}, f32[2,128,128]{2,1,0:T(8,128)S(1)}, f32[2,128,128]{2,1,0:T(8,128)S(1)}) custom-call(s32[2]{0:T(128)S(1)} %pad_add_fusion.place, s32[1,2]{1,0:T(1,128)S(1)} %copy-done.9, f32[1,2,128,512]{3,2,1,0:T(8,128)S(1)} %copy-done, f32[1,2,128,128]{3,2,1,0:T(8,128)S(1)} %copy-done.4, ...), custom_call_target="tpu_custom_call" | custom-call | flops 50331648 | bytes 1572864 | tf_op jit(solution)/shard_map/pallas_call | solution.py:35
  6.6 0.5 collective-permute-start.5
  7.2 0.7 %shard_map.88 = f32[32,128]{1,0:T(8,128)S(1)} custom-call(s32[2]{0:T(128)S(1)} %pad_add_fusion.place, f32[1,128,128]{2,1,0:T(8,128)S(1)} %copy-done.2, f32[1,128,128]{2,1,0:T(8,128)S(1)} %copy-done.8), custom_call_target="tpu_custom_call" | custom-call | flops 1048576 | bytes 196608 | tf_op jit(solution)/shard_map/pallas_call | solution.py:35
  7.9 2.5 %collective-permute-start = (f32[1,32,128]{2,1,0:T(8,128)S(1)}, f32[1,32,128]{2,1,0:T(8,128)S(1)}, u32[]{:S(2)}, u32[]{:S(2)}) collective-permute-start(f32[1,32,128]{2,1,0:T(8,128)S(1)} %bitcast.11), channel_id=1, source_target_pairs={{0,4},{4,0},{8,12},{12,8},{16,20},{20,16},{24,28},{28,24},{1,5},{5... | collective-permute-start | bytes 49160 | tf_op jit(solution)/shard_map/ppermute | solution.py:132
  10.4 0.7 %shard_map.90 = f32[128,128]{1,0:T(8,128)S(1)} custom-call(s32[2]{0:T(128)S(1)} %pad_add_fusion.place, f32[1,128,512]{2,1,0:T(8,128)S(1)} %copy-done.6, f32[1,128,128]{2,1,0:T(8,128)S(1)} %copy-done.2), custom_call_target="tpu_custom_call" | custom-call | flops 4194304 | bytes 196608 | tf_op jit(solution)/shard_map/pallas_call | solution.py:35
  11.2 1.6 %collective-permute-start.6 = (f32[1,128,128]{2,1,0:T(8,128)S(1)}, f32[1,128,128]{2,1,0:T(8,128)S(1)}, u32[]{:S(2)}, u32[]{:S(2)}) collective-permute-start(f32[1,128,128]{2,1,0:T(8,128)S(1)} %slice.11), channel_id=1, source_target_pairs={{0,2},{1,3},{2,0},{3,1},{4,6},{5,7},{6,4},{7,5},{8,10},{9,11},{10,... | collective-permute-start | bytes 196616 | tf_op jit(solution)/shard_map/ppermute | solution.py:132
  12.8 1.6 %collective-permute-start.1 = (f32[2,32,128]{2,1,0:T(8,128)S(1)}, f32[2,32,128]{2,1,0:T(8,128)S(1)}, u32[]{:S(2)}, u32[]{:S(2)}) collective-permute-start(f32[2,32,128]{2,1,0:T(8,128)S(1)} %pad_maximum_fusion.3), channel_id=1, source_target_pairs={{0,8},{4,12},{8,0},{12,4},{16,24},{20,28},{24,16},{28,20},{1,9},{5... | collective-permute-start | bytes 98312 | tf_op jit(solution)/shard_map/ppermute | solution.py:132
  14.4 1.2 %collective-permute-done.6 = f32[1,128,128]{2,1,0:T(8,128)S(1)} collective-permute-done((f32[1,128,128]{2,1,0:T(8,128)S(1)}, f32[1,128,128]{2,1,0:T(8,128)S(1)}, u32[]{:S(2)}, u32[]{:S(2)}) %collective-permute-start.6) | collective-permute-done | bytes 65568 | tf_op jit(solution)/shard_map/ppermute | solution.py:132
  15.6 0.8 %broadcast_in_dim.11 = f32[8,128,128]{2,1,0:T(8,128)} broadcast(f32[128,128]{1,0:T(8,128)S(1)} %fusion.1), dimensions={1,2} | broadcast | bytes 589824 | tf_op jit(solution)/shard_map/broadcast_in_dim | solution.py:185
  16.4 4.9 %all-to-all-start = ((f32[8,128,128]{2,1,0:T(8,128)}), f32[8,128,128]{2,1,0:T(8,128)S(1)}, u32[]{:S(2)}, u32[]{:S(2)}) async-start(f32[8,128,128]{2,1,0:T(8,128)} %broadcast_in_dim.11), calls=%async_computation | async-start | bytes 1048576 | tf_op jit(solution)/shard_map/all_to_all | solution.py:184
  21.3 3.0 %collective-permute-start.2 = (f32[4,32,128]{2,1,0:T(8,128)S(1)}, f32[4,32,128]{2,1,0:T(8,128)S(1)}, u32[]{:S(2)}, u32[]{:S(2)}) collective-permute-start(f32[4,32,128]{2,1,0:T(8,128)S(1)} %pad_maximum_fusion.2), channel_id=1, source_target_pairs={{0,16},{4,20},{8,24},{12,28},{16,0},{20,4},{24,8},{28,12},{1,17},{... | collective-permute-start | bytes 196616 | tf_op jit(solution)/shard_map/ppermute | solution.py:132
  24.3 13.6 %collective-permute-done.2 = f32[4,32,128]{2,1,0:T(8,128)S(1)} collective-permute-done((f32[4,32,128]{2,1,0:T(8,128)S(1)}, f32[4,32,128]{2,1,0:T(8,128)S(1)}, u32[]{:S(2)}, u32[]{:S(2)}) %collective-permute-start.2) | collective-permute-done | bytes 65568 | tf_op jit(solution)/shard_map/ppermute | solution.py:132
  37.9 1.6 %collective-permute-start.3 = (f32[1,8,32,128]{3,2,1,0:T(8,128)S(1)}, f32[1,8,32,128]{3,2,1,0:T(8,128)S(1)}, u32[]{:S(2)}, u32[]{:S(2)}) collective-permute-start(f32[1,8,32,128]{3,2,1,0:T(8,128)S(1)} %maximum_bitcast_fusion), channel_id=1, source_target_pairs={{0,2},{1,3},{2,0},{3,1},{4,6},{5,7},{6,4},{7,5},{8,10},{9,11},{10,... | collective-permute-start | bytes 393224 | tf_op jit(solution)/shard_map/ppermute | solution.py:132
  39.4 3.5 %collective-permute-done.3 = f32[1,8,32,128]{3,2,1,0:T(8,128)S(1)} collective-permute-done((f32[1,8,32,128]{3,2,1,0:T(8,128)S(1)}, f32[1,8,32,128]{3,2,1,0:T(8,128)S(1)}, u32[]{:S(2)}, u32[]{:S(2)}) %collective-permute-start.3) | collective-permute-done | bytes 131104 | tf_op jit(solution)/shard_map/ppermute | solution.py:132
  43.0 1.3 %shard_map.86.base = f32[2,128,512]{2,1,0:T(8,128)S(1)} custom-call(f32[1,2,128,512]{3,2,1,0:T(8,128)S(1)} %copy-done.1, f32[1,2,128,128]{3,2,1,0:T(8,128)S(1)} %copy-done.5), custom_call_target="tpu_custom_call" | custom-call | flops 67108864 | bytes 1572864 | tf_op jit(solution)/shard_map/pallas_call | solution.py:35
  44.6 4.1 %shard_map.89.row = f32[8,128,128]{2,1,0:T(8,128)S(1)} custom-call(s32[2]{0:T(128)S(1)} %pad_add_fusion.place, f32[4,8,32,128]{3,2,1,0:T(8,128)S(1)} %pad_maximum_fusion.maps), custom_call_target="tpu_custom_call" | custom-call | flops 67108864 | bytes 1048576 | tf_op jit(solution)/shard_map/pallas_call | solution.py:155
  48.6 0.6 %shard_map.91 = f32[128,128]{1,0:T(8,128)S(1)} custom-call(f32[8,128,128]{2,1,0:T(8,128)S(1)} %shard_map.89.row, f32[8,128,128]{2,1,0:T(8,128)S(1)} %all-to-all-done.offsets), custom_call_target="tpu_custom_call" | custom-call | flops 33554432 | bytes 1048576 | tf_op jit(solution)/shard_map/pallas_call | solution.py:35
  49.3 5.9 %all-gather = f32[512,128]{1,0:T(8,128)S(1)} all-gather(f32[128,128]{1,0:T(8,128)S(1)} %shard_map.91), channel_id=2, replica_groups=mesh['leaf'=8,'grp'=4] {'grp'}, dimensions={0}, use_global_device_ids=true | all-gather | bytes 327680 | tf_op jit(solution)/shard_map/all_gather | solution.py:194
  55.2 2.1 %shard_map.92 = (f32[1,2,128,512]{3,2,1,0:T(8,128)}, f32[1,128,128]{2,1,0:T(8,128)}) custom-call(s32[2]{0:T(128)S(1)} %pad_add_fusion.place, f32[2,128,512]{2,1,0:T(8,128)S(1)} %shard_map.86.base, f32[2,128,128]{2,1,0:T(8,128)S(1)} %get-tuple-element.5.down, f32[1,128,128]{2,1,0:T(8,128)S(1)} %copy-done.3, f32[4,128,128]{2,1,0:T(8,128)S(1)} %bitcast.10), custom_call_target="tpu_custom_call" | custom-call | flops 37748736 | bytes 1572864 | tf_op jit(solution)/shard_map/pallas_call | solution.py:35
  (30 shorter events, 0.5 us)
Async XLA Ops:
  0.6 0.7 %copy-start.9 = (s32[1,2]{1,0:T(1,128)S(1)}, s32[1,2]{1,0:T(1,128)}, u32[]{:S(2)}) copy-start(s32[1,2]{1,0:T(1,128)} %pattern.1) | copy-start | bytes 28
  1.3 1.0 %copy-start = (f32[1,2,128,512]{3,2,1,0:T(8,128)S(1)}, f32[1,2,128,512]{3,2,1,0:T(8,128)}, u32[]{:S(2)}) copy-start(f32[1,2,128,512]{3,2,1,0:T(8,128)} %rhs.4) | copy-start | bytes 1572868
  2.3 0.8 %copy-start.2 = (f32[1,128,128]{2,1,0:T(8,128)S(1)}, f32[1,128,128]{2,1,0:T(8,128)}, u32[]{:S(2)}) copy-start(f32[1,128,128]{2,1,0:T(8,128)} %inverse.7) | copy-start | bytes 196612
  3.2 0.9 %copy-start.4 = (f32[1,2,128,128]{3,2,1,0:T(8,128)S(1)}, f32[1,2,128,128]{3,2,1,0:T(8,128)}, u32[]{:S(2)}) copy-start(f32[1,2,128,128]{3,2,1,0:T(8,128)} %leaf_inv.3) | copy-start | bytes 393220
  4.1 0.9 %copy-start.7 = (f32[1,2,128,128]{3,2,1,0:T(8,128)S(1)}, f32[1,2,128,128]{3,2,1,0:T(8,128)}, u32[]{:S(2)}) copy-start(f32[1,2,128,128]{3,2,1,0:T(8,128)} %coupling.1) | copy-start | bytes 393220
  5.0 2.2 %copy-start.8 = (f32[1,128,128]{2,1,0:T(8,128)S(1)}, f32[1,128,128]{2,1,0:T(8,128)}, u32[]{:S(2)}) copy-start(f32[1,128,128]{2,1,0:T(8,128)} %link.1) | copy-start | bytes 196612
  5.0 5.4 %copy-start.6 = (f32[1,128,512]{2,1,0:T(8,128)S(1)}, f32[1,128,512]{2,1,0:T(8,128)}, u32[]{:S(2)}) copy-start(f32[1,128,512]{2,1,0:T(8,128)} %rhs.5) | copy-start | bytes 786436
  6.6 4.5 %collective-permute-start.5 = (f32[2,128,128]{2,1,0:T(8,128)S(1)}, f32[2,128,128]{2,1,0:T(8,128)S(1)}, u32[]{:S(2)}, u32[]{:S(2)}) collective-permute-start(f32[2,128,128]{2,1,0:T(8,128)S(1)} %get-tuple-element.7), channel_id=1, source_target_pairs={{0,1},{1,0},{2,3},{3,2},{4,5},{5,4},{6,7},{7,6},{8,9},{9,8},{10,11... | collective-permute-start | bytes 393224 | tf_op jit(solution)/shard_map/ppermute | solution.py:132
  7.9 4.9 %collective-permute-start = (f32[1,32,128]{2,1,0:T(8,128)S(1)}, f32[1,32,128]{2,1,0:T(8,128)S(1)}, u32[]{:S(2)}, u32[]{:S(2)}) collective-permute-start(f32[1,32,128]{2,1,0:T(8,128)S(1)} %bitcast.11), channel_id=1, source_target_pairs={{0,4},{4,0},{8,12},{12,8},{16,20},{20,16},{24,28},{28,24},{1,5},{5... | collective-permute-start | bytes 49160 | tf_op jit(solution)/shard_map/ppermute | solution.py:132
  11.2 4.3 %collective-permute-start.6 = (f32[1,128,128]{2,1,0:T(8,128)S(1)}, f32[1,128,128]{2,1,0:T(8,128)S(1)}, u32[]{:S(2)}, u32[]{:S(2)}) collective-permute-start(f32[1,128,128]{2,1,0:T(8,128)S(1)} %slice.11), channel_id=1, source_target_pairs={{0,2},{1,3},{2,0},{3,1},{4,6},{5,7},{6,4},{7,5},{8,10},{9,11},{10,... | collective-permute-start | bytes 196616 | tf_op jit(solution)/shard_map/ppermute | solution.py:132
  12.8 8.5 %collective-permute-start.1 = (f32[2,32,128]{2,1,0:T(8,128)S(1)}, f32[2,32,128]{2,1,0:T(8,128)S(1)}, u32[]{:S(2)}, u32[]{:S(2)}) collective-permute-start(f32[2,32,128]{2,1,0:T(8,128)S(1)} %pad_maximum_fusion.3), channel_id=1, source_target_pairs={{0,8},{4,12},{8,0},{12,4},{16,24},{20,28},{24,16},{28,20},{1,9},{5... | collective-permute-start | bytes 98312 | tf_op jit(solution)/shard_map/ppermute | solution.py:132
  16.4 32.2 %all-to-all-start = ((f32[8,128,128]{2,1,0:T(8,128)}), f32[8,128,128]{2,1,0:T(8,128)S(1)}, u32[]{:S(2)}, u32[]{:S(2)}) async-start(f32[8,128,128]{2,1,0:T(8,128)} %broadcast_in_dim.11), calls=%async_computation | async-start | bytes 1048576 | tf_op jit(solution)/shard_map/all_to_all | solution.py:184
  21.3 21.7 %copy-start.1 = (f32[1,2,128,512]{3,2,1,0:T(8,128)S(1)}, f32[1,2,128,512]{3,2,1,0:T(8,128)}, u32[]{:S(2)}) copy-start(f32[1,2,128,512]{3,2,1,0:T(8,128)} %rhs.4) | copy-start | bytes 1572868
  21.3 16.5 %collective-permute-start.2 = (f32[4,32,128]{2,1,0:T(8,128)S(1)}, f32[4,32,128]{2,1,0:T(8,128)S(1)}, u32[]{:S(2)}, u32[]{:S(2)}) collective-permute-start(f32[4,32,128]{2,1,0:T(8,128)S(1)} %pad_maximum_fusion.2), channel_id=1, source_target_pairs={{0,16},{4,20},{8,24},{12,28},{16,0},{20,4},{24,8},{28,12},{1,17},{... | collective-permute-start | bytes 196616 | tf_op jit(solution)/shard_map/ppermute | solution.py:132
  37.8 5.2 %copy-start.5 = (f32[1,2,128,128]{3,2,1,0:T(8,128)S(1)}, f32[1,2,128,128]{3,2,1,0:T(8,128)}, u32[]{:S(2)}) copy-start(f32[1,2,128,128]{3,2,1,0:T(8,128)} %leaf_inv.3) | copy-start | bytes 393220
  37.9 5.0 %collective-permute-start.3 = (f32[1,8,32,128]{3,2,1,0:T(8,128)S(1)}, f32[1,8,32,128]{3,2,1,0:T(8,128)S(1)}, u32[]{:S(2)}, u32[]{:S(2)}) collective-permute-start(f32[1,8,32,128]{3,2,1,0:T(8,128)S(1)} %maximum_bitcast_fusion), channel_id=1, source_target_pairs={{0,2},{1,3},{2,0},{3,1},{4,6},{5,7},{6,4},{7,5},{8,10},{9,11},{10,... | collective-permute-start | bytes 393224 | tf_op jit(solution)/shard_map/ppermute | solution.py:132
  42.9 1.6 %collective-permute-start.4 = (f32[2,8,32,128]{3,2,1,0:T(8,128)S(1)}, f32[2,8,32,128]{3,2,1,0:T(8,128)S(1)}, u32[]{:S(2)}, u32[]{:S(2)}) collective-permute-start(f32[2,8,32,128]{3,2,1,0:T(8,128)S(1)} %pad_maximum_fusion.1), channel_id=1, source_target_pairs={{0,1},{1,0},{2,3},{3,2},{4,5},{5,4},{6,7},{7,6},{8,9},{9,8},{10,11... | collective-permute-start | bytes 786440 | tf_op jit(solution)/shard_map/ppermute | solution.py:132
  49.2 5.9 %copy-start.3 = (f32[1,128,128]{2,1,0:T(8,128)S(1)}, f32[1,128,128]{2,1,0:T(8,128)}, u32[]{:S(2)}) copy-start(f32[1,128,128]{2,1,0:T(8,128)} %inverse.7) | copy-start | bytes 196612

commit v2 on v1

v2 whole, which is shorter than its diff:
```python
import jax
import jax.numpy as jnp
from jax import lax
from jax.experimental import pallas as pl
from jax.experimental.pallas import tpu as pltpu
from jax.sharding import PartitionSpec as P

HIGH = lax.Precision.HIGHEST
F32 = jnp.float32
VMEM = pl.BlockSpec(memory_space=pltpu.VMEM)
HBM = pl.BlockSpec(memory_space=pltpu.HBM)


def dot(a, b):
    return jnp.dot(a, b, precision=HIGH, preferred_element_type=F32)


def dot_ta(a, b):
    return lax.dot_general(
        a, b, (((0,), (0,)), ((), ())), precision=HIGH, preferred_element_type=F32
    )


def dot_tb(a, b):
    return lax.dot_general(
        a, b, (((1,), (1,)), ((), ())), precision=HIGH, preferred_element_type=F32
    )


def shaped(*shape):
    return jax.ShapeDtypeStruct(shape, F32)


def call(body, outs, flops, moved, *args, held=(), far=0):
    args = [pltpu.with_memory_space_constraint(a, pltpu.HBM) for a in args[:far]] + list(args[far:])
    return pl.pallas_call(
        body,
        out_shape=outs,
        in_specs=[HBM] * far + [VMEM] * (len(args) - far),
        out_specs=jax.tree.map(lambda _: VMEM, outs),
        scratch_shapes=held,
        cost_estimate=pl.CostEstimate(flops=flops, bytes_accessed=moved, transcendentals=0),
        compiler_params=pltpu.CompilerParams(vmem_limit_bytes=48 << 20),
    )(*args)


def landing(args):
    holds = [
        (pltpu.SMEM if a.dtype == jnp.int32 else pltpu.VMEM)(a.shape, a.dtype) for a in args
    ]
    return holds + [pltpu.SemaphoreType.DMA((len(args),))]


def fetch(sources, targets, sems):
    copies = [
        pltpu.make_async_copy(a, b, sems.at[i]) for i, (a, b) in enumerate(zip(sources, targets))
    ]
    for copy in copies:
        copy.start()
    return copies


def begin(*refs):
    sources, (maps, kept, sent, down) = refs[:6], refs[6:10]
    targets, sems = refs[10:16], refs[16]
    inverse, link, pattern, leaf_inv, coupling, rhs = targets
    copies = fetch(sources, targets, sems)
    group = lax.axis_index("grp")
    count, order = down.shape[0], down.shape[1]
    groups, width, rows = kept.shape[0] * 2, kept.shape[2], maps.shape[0]
    copies[0].wait()
    copies[1].wait()
    start = pl.multiple_of(group * rows, rows)
    maps[...] = -dot(inverse[0, pl.ds(start, rows), :], link[0])
    for copy in copies[2:5]:
        copy.wait()
    for k in range(count):
        present = pattern[0, k].astype(F32)
        mixed = dot(coupling[0, k] * present, leaf_inv[0, k])
        down[k] = dot(inverse[0], mixed)
    copies[5].wait()
    for slot in range(groups):
        start = pl.multiple_of((group ^ slot) * width, width)
        total = dot(down[0], rhs[0, 0, :, pl.ds(start, width)])
        for k in range(1, count):
            total += dot(down[k], rhs[0, k, :, pl.ds(start, width)])
        (sent if slot % 2 else kept)[slot // 2] = total


def leaf_base(rhs_far, inv_far, base, rhs, leaf_inv, sems):
    copies = fetch((rhs_far, inv_far), (rhs, leaf_inv), sems)
    for copy in copies:
        copy.wait()
    for k in range(base.shape[0]):
        base[k] = dot_ta(leaf_inv[0, k], dot(leaf_inv[0, k], rhs[0, k]))


def own_columns(rhs_far, inverse_far, out, rhs, inverse, sems):
    width = out.shape[1]
    start = pl.multiple_of(lax.axis_index("grp") * width, width)
    copies = fetch((rhs_far, inverse_far), (rhs, inverse), sems)
    for copy in copies:
        copy.wait()
    out[...] = dot(inverse[0], rhs[0, :, pl.ds(start, width)])


def operator_row(maps, row, held):
    groups, sections, rows, order = maps.shape
    me, mine = lax.axis_index("leaf"), lax.axis_index("grp")
    diagonal = (
        lax.broadcasted_iota(jnp.int32, (order, order), 0)
        == lax.broadcasted_iota(jnp.int32, (order, order), 1)
    ).astype(F32)

    def slot_of(far, size):
        index, bit, low = 0, size // 2, 1
        while bit:
            index = index + (far // bit) % 2 * low
            bit, low = bit // 2, low * 2
        return index

    def load(section):
        spot = slot_of(section ^ me, sections)
        return jnp.concatenate(
            [maps[slot_of(q ^ mine, groups), spot] for q in range(groups)], axis=0
        )

    held[0] = diagonal * (me == 0).astype(F32)

    @pl.loop(1, sections, unroll=sections <= 8)
    def _(section):
        reached = dot_tb(held[section - 1], load(section))
        held[section] = reached + diagonal * (me == section).astype(F32)

    row[sections - 1] = held[sections - 1]

    @pl.loop(0, sections - 1, unroll=sections <= 8)
    def _(turn):
        section = sections - 2 - turn
        row[section] = held[section] + dot(row[section + 1], load(section + 1))


def apply_row(row, offsets, out):
    total = dot(row[0], offsets[0])
    for section in range(1, row.shape[0]):
        total += dot(row[section], offsets[section])
    out[...] = total


def finish(base, down, inverse, spread, leaves, solved):
    groups, width = spread.shape[0], spread.shape[2]
    for j in range(groups):
        for k in range(base.shape[0]):
            cols = slice(j * width, (j + 1) * width)
            leaves[0, k, :, cols] = base[k, :, cols] - dot_ta(down[k], spread[j])
    solved[0] = dot_ta(inverse[0], spread[lax.axis_index("grp")])


def swap(value, axis, bit):
    count = lax.axis_size(axis)
    return lax.ppermute(value, axis, [(i, i ^ bit) for i in range(count)])


def shards(leaf_rhs, leaf_inv, coupling, pattern, sep_rhs, sep_inv, chain_link):
    sections, groups = lax.axis_size("leaf"), lax.axis_size("grp")
    count, order, columns = leaf_rhs.shape[1:]
    width = columns // groups
    cube = 2 * order**3

    half = shaped(groups // 2, order, width)
    first = (sep_inv, chain_link, pattern, leaf_inv, coupling, leaf_rhs)
    maps, kept, sent, down = call(
        begin,
        (shaped(order // groups, order), half, half, shaped(count, order, order)),
        (2 * count + groups * count + 1) * cube,
        2 * leaf_rhs.size * 4,
        *first, held=landing(first), far=6,
    )
    maps = maps[None]
    rounds = [("leaf", 2**i) for i in reversed(range((sections - 1).bit_length()))]

    own = call(
        own_columns, shaped(order, width), cube, 3 * order * order * 4, sep_rhs, sep_inv,
        held=landing((sep_rhs, sep_inv)), far=2,
    )
    bit = 1
    while bit < groups:
        total = kept + swap(sent, "grp", bit)
        kept, sent = total[0::2], total[1::2]
        bit *= 2
    offset = own - total[0]

    for axis, bit in rounds[:-1]:
        maps = jnp.concatenate([maps, swap(maps, axis, bit)], axis=0)
    maps, offset = lax.optimization_barrier((maps, offset))
    for axis, bit in rounds[-1:]:
        maps = jnp.concatenate([maps, swap(maps, axis, bit)], axis=0)
    maps = maps[None]
    bit = groups // 2
    while bit:
        maps = jnp.concatenate([maps, swap(maps, "grp", bit)], axis=0)
        bit //= 2
    row = call(
        operator_row, shaped(sections, order, order), 2 * sections * cube, 2 * maps.size * 4,
        maps, held=[pltpu.VMEM((sections, order, order), F32)],
    )

    offsets = lax.all_to_all(
        jnp.broadcast_to(offset, (sections, order, width)), "leaf", 0, 0, tiled=True
    )
    base = call(
        leaf_base, shaped(count, order, columns), 8 * count * cube, 3 * leaf_rhs.size * 4,
        leaf_rhs, leaf_inv, held=landing((leaf_rhs, leaf_inv)), far=2,
    )
    carried = call(
        apply_row, shaped(order, width), sections * cube, 2 * row.size * 4, row, offsets
    )
    spread = lax.all_gather(carried, "grp")
    return call(
        finish,
        (shaped(1, count, order, columns), shaped(1, order, width)),
        (4 * count + 1) * cube,
        3 * leaf_rhs.size * 4,
        base, down, sep_inv, spread,
    )


def solution(mesh):
    in_specs = (
        P("leaf", "grp", None, None),
        P("leaf", "grp", None, None),
        P("leaf", "grp", None, None),
        P("leaf", "grp"),
        P("leaf", None, None),
        P("leaf", None, None),
        P("leaf", None, None),
    )
    out_specs = (P("leaf", "grp", None, None), P("leaf", None, "grp"))
    return jax.shard_map(shards, mesh=mesh, in_specs=in_specs, out_specs=out_specs, check_vma=False)
```

time: 57.6 us -> 47 us (0.82)
  waiting for transfers between devices: 18.5 us -> 11.1 us
  local copies, waits for them, and re-layouts: 5.12 us -> 0.84 us
    ppermute x7, waiting for transfers between devices: 18.5 us -> 11.1 us  [swap(): return lax.ppermute(value, axis, [(i, i ^ bit) for i in range(count)])]
    unnamed x20 -> x2, local copies, waits for them, and re-layouts: 4.28 us -> 0.01 us
    pallas_call x7 -> x6, Pallas kernels: 11.1 us -> 11.4 us  [call(): pl.pallas_call(body, out_shape=outs, in_specs=[HBM] * far + [VMEM] * (len...]
  transfers between devices with their start and end apart: 8 -> 8, of which waited for: 4 -> 4; matrix products, arithmetic and copies ran while one was open for 2% -> 0% of each run, Pallas kernels for 12% -> 15%
where the time goes in v2:
time: 47 us; the launch traced here: 46.5 us
  starting transfers between devices  16.1 us (34%)
  Pallas kernels  11.4 us (24%)
  waiting for transfers between devices  11.1 us (24%)
  blocking collectives  6.14 us (13%)
  local copies, waits for them, and re-layouts  0.84 us (2%)
  between operations  0.76 us (2%)
    pallas_call x6, Pallas kernels, call(): pl.pallas_call(body, out_shape=outs, in_specs=[HBM] * far + [VMEM] * (len...  11.4 us
    ppermute x7, starting transfers between devices, swap(): return lax.ppermute(value, axis, [(i, i ^ bit) for i in range(count)])  11.2 us
    ppermute x7, waiting for transfers between devices, swap(): return lax.ppermute(value, axis, [(i, i ^ bit) for i in range(count)])  11.1 us
    all_gather x1, blocking collectives, shards(): spread = lax.all_gather(carried, 'grp')  6.14 us
    all_to_all x1, starting transfers between devices, shards(): lax.all_to_all(jnp.broadcast_to(offset, (sections, order, width)), 'leaf'...  4.88 us
  transfers between devices with their start and end apart: 8, of which 4 were waited for; matrix products, arithmetic and copies ran while one was open for 0% of the time, Pallas kernels for 15%

profile of v2, /device:TPU:0, one launch (start us, length us, event | category | flops | bytes accessed | tf_op | source)
XLA Modules:
  0.0 46.5 jit_solution(17972458211259698453)
XLA Ops:
  0.6 2.2 %shard_map.87 = (f32[32,128]{1,0:T(8,128)S(1)}, f32[2,128,128]{2,1,0:T(8,128)S(1)}, f32[2,128,128]{2,1,0:T(8,128)S(1)}, f32[2,128,128]{2,1,0:T(8,128)S(1)}) custom-call(f32[1,128,128]{2,1,0:T(8,128)} %inverse.1, f32[1,128,128]{2,1,0:T(8,128)} %refs_1_.1, s32[1,2]{1,0:T(1,128)} %refs_2_.1, f32[1,2,128,128]{3,2,1,0:T(8,128)} %refs_3_.1, ...), custom_call_target="tpu_custom_call" | custom-call | flops 54525952 | bytes 1048576 | tf_op jit(solution)/shard_map/pallas_call | solution.py:36
  2.9 4.1 %collective-permute-start = (f32[1,32,128]{2,1,0:T(8,128)S(1)}, f32[1,32,128]{2,1,0:T(8,128)S(1)}, u32[]{:S(2)}, u32[]{:S(2)}) collective-permute-start(f32[1,32,128]{2,1,0:T(8,128)S(1)} %bitcast.9), channel_id=1, source_target_pairs={{0,16},{4,20},{8,24},{12,28},{16,0},{20,4},{24,8},{28,12},{1,17},{... | collective-permute-start | bytes 49160 | tf_op jit(solution)/shard_map/ppermute | solution.py:161
  7.0 0.0 collective-permute-start.2
  7.0 1.7 %collective-permute-done = f32[1,32,128]{2,1,0:T(8,128)S(1)} collective-permute-done((f32[1,32,128]{2,1,0:T(8,128)S(1)}, f32[1,32,128]{2,1,0:T(8,128)S(1)}, u32[]{:S(2)}, u32[]{:S(2)}) %collective-permute-start) | collective-permute-done | bytes 16416 | tf_op jit(solution)/shard_map/ppermute | solution.py:161
  8.7 1.9 %collective-permute-start.1 = (f32[2,32,128]{2,1,0:T(8,128)S(1)}, f32[2,32,128]{2,1,0:T(8,128)S(1)}, u32[]{:S(2)}, u32[]{:S(2)}) collective-permute-start(f32[2,32,128]{2,1,0:T(8,128)S(1)} %pad_maximum_fusion.3), channel_id=1, source_target_pairs={{0,8},{4,12},{8,0},{12,4},{16,24},{20,28},{24,16},{28,20},{1,9},{5... | collective-permute-start | bytes 98312 | tf_op jit(solution)/shard_map/ppermute | solution.py:161
  10.6 1.2 %shard_map.88 = f32[128,128]{1,0:T(8,128)S(1)} custom-call(f32[1,128,512]{2,1,0:T(8,128)} %rhs_far.3, f32[1,128,128]{2,1,0:T(8,128)} %inverse.1), custom_call_target="tpu_custom_call" | custom-call | flops 4194304 | bytes 196608 | tf_op jit(solution)/shard_map/pallas_call | solution.py:36
  11.8 0.0 collective-permute-done.2
  11.8 1.6 %collective-permute-start.3 = (f32[1,128,128]{2,1,0:T(8,128)S(1)}, f32[1,128,128]{2,1,0:T(8,128)S(1)}, u32[]{:S(2)}, u32[]{:S(2)}) collective-permute-start(f32[1,128,128]{2,1,0:T(8,128)S(1)} %slice.11), channel_id=1, source_target_pairs={{0,2},{1,3},{2,0},{3,1},{4,6},{5,7},{6,4},{7,5},{8,10},{9,11},{10,... | collective-permute-start | bytes 196616 | tf_op jit(solution)/shard_map/ppermute | solution.py:161
  13.4 2.8 %collective-permute-done.3 = f32[1,128,128]{2,1,0:T(8,128)S(1)} collective-permute-done((f32[1,128,128]{2,1,0:T(8,128)S(1)}, f32[1,128,128]{2,1,0:T(8,128)S(1)}, u32[]{:S(2)}, u32[]{:S(2)}) %collective-permute-start.3) | collective-permute-done | bytes 65568 | tf_op jit(solution)/shard_map/ppermute | solution.py:161
  16.2 0.8 %broadcast_in_dim.11 = f32[8,128,128]{2,1,0:T(8,128)} broadcast(f32[128,128]{1,0:T(8,128)S(1)} %fusion.1), dimensions={1,2} | broadcast | bytes 589824 | tf_op jit(solution)/shard_map/broadcast_in_dim | solution.py:209
  17.0 4.9 %all-to-all-start = ((f32[8,128,128]{2,1,0:T(8,128)}), f32[8,128,128]{2,1,0:T(8,128)S(1)}, u32[]{:S(2)}, u32[]{:S(2)}) async-start(f32[8,128,128]{2,1,0:T(8,128)} %broadcast_in_dim.11), calls=%async_computation | async-start | bytes 1048576 | tf_op jit(solution)/shard_map/all_to_all | solution.py:208
  21.9 2.0 %collective-permute-start.4 = (f32[4,32,128]{2,1,0:T(8,128)S(1)}, f32[4,32,128]{2,1,0:T(8,128)S(1)}, u32[]{:S(2)}, u32[]{:S(2)}) collective-permute-start(f32[4,32,128]{2,1,0:T(8,128)S(1)} %pad_maximum_fusion.2), channel_id=1, source_target_pairs={{0,4},{4,0},{8,12},{12,8},{16,20},{20,16},{24,28},{28,24},{1,5},{5... | collective-permute-start | bytes 196616 | tf_op jit(solution)/shard_map/ppermute | solution.py:161
  23.9 3.1 %collective-permute-done.4 = f32[4,32,128]{2,1,0:T(8,128)S(1)} collective-permute-done((f32[4,32,128]{2,1,0:T(8,128)S(1)}, f32[4,32,128]{2,1,0:T(8,128)S(1)}, u32[]{:S(2)}, u32[]{:S(2)}) %collective-permute-start.4) | collective-permute-done | bytes 65568 | tf_op jit(solution)/shard_map/ppermute | solution.py:161
  27.1 1.6 %collective-permute-start.5 = (f32[1,8,32,128]{3,2,1,0:T(8,128)S(1)}, f32[1,8,32,128]{3,2,1,0:T(8,128)S(1)}, u32[]{:S(2)}, u32[]{:S(2)}) collective-permute-start(f32[1,8,32,128]{3,2,1,0:T(8,128)S(1)} %maximum_bitcast_fusion), channel_id=1, source_target_pairs={{0,2},{1,3},{2,0},{3,1},{4,6},{5,7},{6,4},{7,5},{8,10},{9,11},{10,... | collective-permute-start | bytes 393224 | tf_op jit(solution)/shard_map/ppermute | solution.py:161
  28.6 3.5 %collective-permute-done.5 = f32[1,8,32,128]{3,2,1,0:T(8,128)S(1)} collective-permute-done((f32[1,8,32,128]{3,2,1,0:T(8,128)S(1)}, f32[1,8,32,128]{3,2,1,0:T(8,128)S(1)}, u32[]{:S(2)}, u32[]{:S(2)}) %collective-permute-start.5) | collective-permute-done | bytes 131104 | tf_op jit(solution)/shard_map/ppermute | solution.py:161
  32.1 0.1 collective-permute-start.6
  32.2 2.4 %shard_map.86.base = f32[2,128,512]{2,1,0:T(8,128)S(1)} custom-call(f32[1,2,128,512]{3,2,1,0:T(8,128)} %refs_5_.1, f32[1,2,128,128]{3,2,1,0:T(8,128)} %refs_3_.1), custom_call_target="tpu_custom_call" | custom-call | flops 67108864 | bytes 1572864 | tf_op jit(solution)/shard_map/pallas_call | solution.py:36
  34.6 0.0 collective-permute-done.6
  34.6 3.5 %shard_map.89.row = f32[8,128,128]{2,1,0:T(8,128)S(1)} custom-call(f32[4,8,32,128]{3,2,1,0:T(8,128)S(1)} %pad_maximum_fusion.maps), custom_call_target="tpu_custom_call" | custom-call | flops 67108864 | bytes 1048576 | tf_op jit(solution)/shard_map/pallas_call | solution.py:36
  38.2 0.0 all-to-all-done.offsets
  38.2 0.6 %shard_map.90 = f32[128,128]{1,0:T(8,128)S(1)} custom-call(f32[8,128,128]{2,1,0:T(8,128)S(1)} %shard_map.89.row, f32[8,128,128]{2,1,0:T(8,128)S(1)} %all-to-all-done.offsets), custom_call_target="tpu_custom_call" | custom-call | flops 33554432 | bytes 1048576 | tf_op jit(solution)/shard_map/pallas_call | solution.py:36
  38.8 0.0 copy-start
  38.8 6.1 %all-gather = f32[512,128]{1,0:T(8,128)S(1)} all-gather(f32[128,128]{1,0:T(8,128)S(1)} %shard_map.90), channel_id=2, replica_groups=mesh['leaf'=8,'grp'=4] {'grp'}, dimensions={0}, use_global_device_ids=true | all-gather | bytes 327680 | tf_op jit(solution)/shard_map/all_gather | solution.py:218
  45.0 1.5 %shard_map.91 = (f32[1,2,128,512]{3,2,1,0:T(8,128)}, f32[1,128,128]{2,1,0:T(8,128)}) custom-call(f32[2,128,512]{2,1,0:T(8,128)S(1)} %shard_map.86.base, f32[2,128,128]{2,1,0:T(8,128)S(1)} %get-tuple-element.8.down, f32[1,128,128]{2,1,0:T(8,128)S(1)} %copy-done, f32[4,128,128]{2,1,0:T(8,128)S(1)} %bitcast.8), custom_call_target="tpu_custom_call" | custom-call | flops 37748736 | bytes 1572864 | tf_op jit(solution)/shard_map/pallas_call | solution.py:36
  (10 shorter events, 0.1 us)
Async XLA Ops:
  2.9 5.8 %collective-permute-start = (f32[1,32,128]{2,1,0:T(8,128)S(1)}, f32[1,32,128]{2,1,0:T(8,128)S(1)}, u32[]{:S(2)}, u32[]{:S(2)}) collective-permute-start(f32[1,32,128]{2,1,0:T(8,128)S(1)} %bitcast.9), channel_id=1, source_target_pairs={{0,16},{4,20},{8,24},{12,28},{16,0},{20,4},{24,8},{28,12},{1,17},{... | collective-permute-start | bytes 49160 | tf_op jit(solution)/shard_map/ppermute | solution.py:161
  7.0 4.8 %collective-permute-start.2 = (f32[2,128,128]{2,1,0:T(8,128)S(1)}, f32[2,128,128]{2,1,0:T(8,128)S(1)}, u32[]{:S(2)}, u32[]{:S(2)}) collective-permute-start(f32[2,128,128]{2,1,0:T(8,128)S(1)} %get-tuple-element.11), channel_id=1, source_target_pairs={{0,1},{1,0},{2,3},{3,2},{4,5},{5,4},{6,7},{7,6},{8,9},{9,8},{10,11... | collective-permute-start | bytes 393224 | tf_op jit(solution)/shard_map/ppermute | solution.py:161
  8.7 4.7 %collective-permute-start.1 = (f32[2,32,128]{2,1,0:T(8,128)S(1)}, f32[2,32,128]{2,1,0:T(8,128)S(1)}, u32[]{:S(2)}, u32[]{:S(2)}) collective-permute-start(f32[2,32,128]{2,1,0:T(8,128)S(1)} %pad_maximum_fusion.3), channel_id=1, source_target_pairs={{0,8},{4,12},{8,0},{12,4},{16,24},{20,28},{24,16},{28,20},{1,9},{5... | collective-permute-start | bytes 98312 | tf_op jit(solution)/shard_map/ppermute | solution.py:161
  11.8 4.3 %collective-permute-start.3 = (f32[1,128,128]{2,1,0:T(8,128)S(1)}, f32[1,128,128]{2,1,0:T(8,128)S(1)}, u32[]{:S(2)}, u32[]{:S(2)}) collective-permute-start(f32[1,128,128]{2,1,0:T(8,128)S(1)} %slice.11), channel_id=1, source_target_pairs={{0,2},{1,3},{2,0},{3,1},{4,6},{5,7},{6,4},{7,5},{8,10},{9,11},{10,... | collective-permute-start | bytes 196616 | tf_op jit(solution)/shard_map/ppermute | solution.py:161
  17.0 21.2 %all-to-all-start = ((f32[8,128,128]{2,1,0:T(8,128)}), f32[8,128,128]{2,1,0:T(8,128)S(1)}, u32[]{:S(2)}, u32[]{:S(2)}) async-start(f32[8,128,128]{2,1,0:T(8,128)} %broadcast_in_dim.11), calls=%async_computation | async-start | bytes 1048576 | tf_op jit(solution)/shard_map/all_to_all | solution.py:208
  21.9 5.2 %collective-permute-start.4 = (f32[4,32,128]{2,1,0:T(8,128)S(1)}, f32[4,32,128]{2,1,0:T(8,128)S(1)}, u32[]{:S(2)}, u32[]{:S(2)}) collective-permute-start(f32[4,32,128]{2,1,0:T(8,128)S(1)} %pad_maximum_fusion.2), channel_id=1, source_target_pairs={{0,4},{4,0},{8,12},{12,8},{16,20},{20,16},{24,28},{28,24},{1,5},{5... | collective-permute-start | bytes 196616 | tf_op jit(solution)/shard_map/ppermute | solution.py:161
  27.1 5.0 %collective-permute-start.5 = (f32[1,8,32,128]{3,2,1,0:T(8,128)S(1)}, f32[1,8,32,128]{3,2,1,0:T(8,128)S(1)}, u32[]{:S(2)}, u32[]{:S(2)}) collective-permute-start(f32[1,8,32,128]{3,2,1,0:T(8,128)S(1)} %maximum_bitcast_fusion), channel_id=1, source_target_pairs={{0,2},{1,3},{2,0},{3,1},{4,6},{5,7},{6,4},{7,5},{8,10},{9,11},{10,... | collective-permute-start | bytes 393224 | tf_op jit(solution)/shard_map/ppermute | solution.py:161
  32.1 2.5 %collective-permute-start.6 = (f32[2,8,32,128]{3,2,1,0:T(8,128)S(1)}, f32[2,8,32,128]{3,2,1,0:T(8,128)S(1)}, u32[]{:S(2)}, u32[]{:S(2)}) collective-permute-start(f32[2,8,32,128]{3,2,1,0:T(8,128)S(1)} %pad_maximum_fusion.1), channel_id=1, source_target_pairs={{0,1},{1,0},{2,3},{3,2},{4,5},{5,4},{6,7},{7,6},{8,9},{9,8},{10,11... | collective-permute-start | bytes 786440 | tf_op jit(solution)/shard_map/ppermute | solution.py:161
  38.8 6.2 %copy-start = (f32[1,128,128]{2,1,0:T(8,128)S(1)}, f32[1,128,128]{2,1,0:T(8,128)}, u32[]{:S(2)}) copy-start(f32[1,128,128]{2,1,0:T(8,128)} %inverse.1) | copy-start | bytes 196612

commit v3 on v2

v3 whole, which is shorter than its diff:
```python
import jax
import jax.numpy as jnp
from jax import lax
from jax.experimental import pallas as pl
from jax.experimental.pallas import tpu as pltpu
from jax.sharding import PartitionSpec as P

HIGH = lax.Precision.HIGHEST
F32 = jnp.float32
VMEM = pl.BlockSpec(memory_space=pltpu.VMEM)
HBM = pl.BlockSpec(memory_space=pltpu.HBM)


def dot(a, b):
    return jnp.dot(a, b, precision=HIGH, preferred_element_type=F32)


def dot_ta(a, b):
    return lax.dot_general(
        a, b, (((0,), (0,)), ((), ())), precision=HIGH, preferred_element_type=F32
    )


def dot_tb(a, b):
    return lax.dot_general(
        a, b, (((1,), (1,)), ((), ())), precision=HIGH, preferred_element_type=F32
    )


def shaped(*shape):
    return jax.ShapeDtypeStruct(shape, F32)


def call(body, outs, flops, moved, *args, held=(), far=0, out_specs=None):
    args = [pltpu.with_memory_space_constraint(a, pltpu.HBM) for a in args[:far]] + list(args[far:])
    return pl.pallas_call(
        body,
        out_shape=outs,
        in_specs=[HBM] * far + [VMEM] * (len(args) - far),
        out_specs=out_specs or jax.tree.map(lambda _: VMEM, outs),
        scratch_shapes=held,
        cost_estimate=pl.CostEstimate(flops=flops, bytes_accessed=moved, transcendentals=0),
        compiler_params=pltpu.CompilerParams(vmem_limit_bytes=48 << 20),
    )(*args)


def landing(*args):
    holds = [
        (pltpu.SMEM if a.dtype == jnp.int32 else pltpu.VMEM)(a.shape, a.dtype) for a in args
    ]
    return holds + [pltpu.SemaphoreType.DMA((len(args),))]


def fetch(sources, targets, sems):
    copies = [
        pltpu.make_async_copy(a, b, sems.at[i]) for i, (a, b) in enumerate(zip(sources, targets))
    ]
    for copy in copies:
        copy.start()
    return copies


def columns_of(block, width):
    return pl.ds(pl.multiple_of(block * width, width), width)


def map_half(inverse_far, link_far, out, inverse, link, sems):
    copies = fetch((inverse_far, link_far), (inverse, link), sems)
    rows = out.shape[1]
    start = pl.multiple_of((lax.axis_index("grp") & 1) * rows, rows)
    for copy in copies:
        copy.wait()
    out[0] = -dot(inverse[0, pl.ds(start, rows), :], link[0])


def begin(*refs):
    sources, outs = refs[:5], refs[5:-6]
    down, slots = outs[0], outs[1:]
    targets, sems = refs[-6:-1], refs[-1]
    inverse, pattern, leaf_inv, coupling, rhs = targets
    copies = fetch(sources, targets, sems)
    group = lax.axis_index("grp")
    count, width = down.shape[0], slots[0].shape[1]
    for copy in copies[:4]:
        copy.wait()
    for k in range(count):
        present = pattern[0, k].astype(F32)
        mixed = dot(coupling[0, k] * present, leaf_inv[0, k])
        down[k] = dot(inverse[0], mixed)
    copies[4].wait()
    for slot in reversed(range(len(slots))):
        cols = columns_of(group ^ slot, width)
        total = dot(down[0], rhs[0, 0, :, cols])
        for k in range(1, count):
            total += dot(down[k], rhs[0, k, :, cols])
        slots[slot][...] = total


def leaf_base(rhs_far, inv_far, base, rhs, leaf_inv, sems):
    copies = fetch((rhs_far, inv_far), (rhs, leaf_inv), sems)
    for copy in copies:
        copy.wait()
    for k in range(base.shape[0]):
        base[k] = dot_ta(leaf_inv[0, k], dot(leaf_inv[0, k], rhs[0, k]))


def own_columns(rhs_far, inverse_far, out, rhs, inverse, sems):
    copies = fetch((rhs_far, inverse_far), (rhs, inverse), sems)
    for copy in copies:
        copy.wait()
    out[...] = dot(inverse[0], rhs[0, :, columns_of(lax.axis_index("grp"), out.shape[1])])


def operator_rows(mine, mine_rest, other, other_rest, held, maps):
    sections, both, order = held.shape
    rows = order // 2
    me, half = lax.axis_index("leaf"), lax.axis_index("grp") & 1
    near = pl.ds(pl.multiple_of(half * rows, rows), rows)
    rest = pl.ds(pl.multiple_of((1 - half) * rows, rows), rows)

    @pl.loop(0, sections // 2, unroll=sections <= 8)
    def _(i):
        maps[2 * i ^ me, near] = mine[i]
        maps[2 * i ^ me, rest] = mine_rest[i]
        maps[2 * i ^ 1 ^ me, near] = other[i]
        maps[2 * i ^ 1 ^ me, rest] = other_rest[i]

    line = lax.broadcasted_iota(jnp.int32, (both, order), 0)
    column = lax.broadcasted_iota(jnp.int32, (both, order), 1)
    target = jnp.where(line < order, me, me ^ 1)
    ones = jnp.where((line & (order - 1)) == column, target, -1)

    held[0] = (ones == 0).astype(F32)

    @pl.loop(1, sections, unroll=sections <= 8)
    def _(section):
        held[section] = dot_tb(held[section - 1], maps[section]) + (ones == section).astype(F32)

    @pl.loop(0, sections - 1, unroll=sections <= 8)
    def _(turn):
        section = sections - 2 - turn
        held[section] += dot(held[section + 1], maps[section + 1])


def apply_rows(which, *refs):
    held, parts, out = refs[0], refs[1:-1], refs[-1]
    order = held.shape[2]
    rows = slice(which * order, (which + 1) * order)
    me = lax.axis_index("leaf")
    size = parts[0].shape[0]
    total = None
    for p, part in enumerate(parts):
        for i in range(size):
            piece = dot(held[2 * (p * size + i) ^ me, rows], part[i])
            total = piece if total is None else total + piece
    out[...] = total


def leaf_piece(slot, base, down, carried, out):
    width = out.shape[2]
    for k in range(out.shape[0]):
        cols = columns_of(lax.axis_index("grp") ^ slot, width)
        out[k] = base[k, :, cols] - dot_ta(down[k], carried[...])


def own_piece(inverse_far, base, down, carried, out, solved, inverse, sems):
    copies = fetch((inverse_far,), (inverse,), sems)
    leaf_piece(0, base, down, carried, out)
    copies[0].wait()
    solved[0] = dot_ta(inverse[0], carried[...])


def last_piece(*refs):
    (base, down, carried), done = refs[:3], refs[3:-3]
    leaves, piece, sems = refs[-3:]
    width = piece.shape[2]
    group, slot = lax.axis_index("grp"), len(done)

    def put(i, source):
        target = leaves.at[0, :, :, columns_of(group ^ i, width)]
        return pltpu.make_async_copy(source, target, sems.at[i])

    copies = [put(i, source) for i, source in enumerate(done)]
    for copy in copies:
        copy.start()
    leaf_piece(slot, base, down, carried, piece)
    copies.append(put(slot, piece))
    copies[slot].start()
    for copy in copies:
        copy.wait()


def swap(value, axis, bit):
    count = lax.axis_size(axis)
    return lax.ppermute(value, axis, [(i, i ^ bit) for i in range(count)])


def gather_pairs(value):
    bit, sections = 2, lax.axis_size("leaf")
    parts = [value]
    while bit < sections:
        if len(parts) > 1:
            value = jnp.concatenate(parts, axis=0)
        masks = [bit] if 2 * bit >= sections else [bit, 2 * bit, 3 * bit]
        parts = [value] + [swap(value, "leaf", m) for m in masks]
        bit *= 4 if len(masks) > 1 else 2
    return parts


def after(value, *others):
    return lax.optimization_barrier((value,) + others)[0]


def shards(leaf_rhs, leaf_inv, coupling, pattern, sep_rhs, sep_inv, chain_link):
    sections, groups = lax.axis_size("leaf"), lax.axis_size("grp")
    count, order, columns = leaf_rhs.shape[1:]
    width = columns // groups
    cube = 2 * order**3
    block = shaped(order, width)
    block_bytes = order * width * 4

    half = call(
        map_half, shaped(1, order // 2, order), cube // 2, 3 * block_bytes,
        sep_inv, chain_link, held=landing(sep_inv, chain_link), far=2,
    )
    map_parts = gather_pairs(half)

    first = (sep_inv, pattern, leaf_inv, coupling, leaf_rhs)
    down, *slots = call(
        begin,
        (shaped(count, order, order),) + (block,) * groups,
        (2 * count + groups * count) * cube,
        2 * leaf_rhs.size * 4,
        *first, held=landing(*first), far=5,
    )
    slots = dict(enumerate(slots))
    bit = 1
    while bit < groups:
        arrived = {m: swap(slots[m + bit], "grp", bit) for m in reversed(range(0, groups, 2 * bit))}
        if 2 * bit == groups:
            own = call(
                own_columns, block, cube, 3 * block_bytes, sep_rhs, sep_inv,
                held=landing(sep_rhs, sep_inv), far=2,
            )
            slots[0] = own - slots[0]
            offset = slots[0] - arrived[0]
        else:
            slots = {m: slots[m] + arrived[m] for m in arrived}
        bit *= 2

    mine = jnp.concatenate(map_parts, axis=0)
    mine_rest = swap(mine, "grp", 1)
    other = swap(mine, "leaf", 1)
    other_rest = swap(other, "grp", 1)
    rows = call(
        operator_rows, shaped(sections, 2 * order, order), 4 * sections * cube,
        4 * sections * block_bytes, mine, mine_rest, other, other_rest,
        held=[pltpu.VMEM((sections, order, order), F32)],
    )

    base = call(
        leaf_base, shaped(count, order, columns), 8 * count * cube, 3 * leaf_rhs.size * 4,
        leaf_rhs, leaf_inv, held=landing(leaf_rhs, leaf_inv), far=2,
    )

    offsets = gather_pairs(offset[None])

    def applied(which):
        return call(
            lambda *refs: apply_rows(which, *refs), block, sections // 2 * cube,
            sections * block_bytes, rows, *offsets,
        )

    theirs = applied(1)
    carried = {0: swap(theirs, "leaf", 1)}
    carried[0] = applied(0) + carried[0]

    for m in range(1, groups):
        low = m & -m
        carried[m] = swap(carried[m ^ low], "grp", low)
    piece = shaped(count, order, width)
    own_leaves, solved = call(
        own_piece, (piece, shaped(1, order, width)), (count + 1) * cube, 6 * block_bytes,
        sep_inv, base, down, carried[0], held=landing(sep_inv), far=1,
    )
    done = [own_leaves]
    for m in range(1, groups - 1):
        done.append(
            call(
                lambda *refs, m=m: leaf_piece(m, *refs), piece, count * cube, 6 * block_bytes,
                base, down, carried[m],
            )
        )
    leaves = call(
        last_piece, shaped(1, count, order, columns), count * cube,
        2 * leaf_rhs.size * 4, base, down, carried[groups - 1], *done,
        held=[pltpu.VMEM((count, order, width), F32), pltpu.SemaphoreType.DMA((groups,))],
        out_specs=HBM,
    )
    return leaves, solved


def solution(mesh):
    in_specs = (
        P("leaf", "grp", None, None),
        P("leaf", "grp", None, None),
        P("leaf", "grp", None, None),
        P("leaf", "grp"),
        P("leaf", None, None),
        P("leaf", None, None),
        P("leaf", None, None),
    )
    out_specs = (P("leaf", "grp", None, None), P("leaf", None, "grp"))
    return jax.shard_map(shards, mesh=mesh, in_specs=in_specs, out_specs=out_specs, check_vma=False)
```

time: 47 us -> 43.3 us (0.921)
  blocking collectives: 6.14 us -> 0 us
  Pallas kernels: 11.4 us -> 15.1 us
  local copies, waits for them, and re-layouts: 0.84 us -> 0 us
  starting transfers between devices: 16.1 us -> 15.6 us
    all_gather x1 -> x0, blocking collectives: 6.14 us -> none  [shards(): spread = lax.all_gather(carried, 'grp')]
    all_to_all x1 -> x0, starting transfers between devices: 4.88 us -> none  [shards(): lax.all_to_all(jnp.broadcast_to(offset, (sections, order, width)), 'leaf'...]
    ppermute x7 -> x16, starting transfers between devices: 11.2 us -> 15.6 us  [swap(): return lax.ppermute(value, axis, [(i, i ^ bit) for i in range(count)])]
    pallas_call x6 -> x11, Pallas kernels: 11.4 us -> 15.1 us  [call(): pl.pallas_call(body, out_shape=outs, in_specs=[HBM] * far + [VMEM] * (len...]
    broadcast_in_dim x1 -> x0, local copies, waits for them, and re-layouts: 0.83 us -> none  [shards(): jnp.broadcast_to(offset, (sections, order, width))]
    ppermute x7 -> x16, waiting for transfers between devices: 11.1 us -> 11.4 us  [swap(): return lax.ppermute(value, axis, [(i, i ^ bit) for i in range(count)])]
  transfers between devices with their start and end apart: 8 -> 16, of which waited for: 4 -> 6; matrix products, arithmetic and copies ran while one was open for 0% -> 0% of each run, Pallas kernels for 15% -> 29%
where the time goes in v3:
time: 43.3 us; the launch traced here: 43 us
  starting transfers between devices  15.6 us (36%)
  Pallas kernels  15.1 us (35%)
  waiting for transfers between devices  11.4 us (26%)
  between operations  0.81 us (2%)
    ppermute x16, starting transfers between devices, swap(): return lax.ppermute(value, axis, [(i, i ^ bit) for i in range(count)])  15.6 us
    pallas_call x11, Pallas kernels, call(): pl.pallas_call(body, out_shape=outs, in_specs=[HBM] * far + [VMEM] * (len...  15.1 us
    ppermute x16, waiting for transfers between devices, swap(): return lax.ppermute(value, axis, [(i, i ^ bit) for i in range(count)])  11.4 us
  transfers between devices with their start and end apart: 16, of which 6 were waited for; matrix products, arithmetic and copies ran while one was open for 0% of the time, Pallas kernels for 29%

profile of v3, /device:TPU:0, one launch (start us, length us, event | category | flops | bytes accessed | tf_op | source)
XLA Modules:
  0.0 43.0 jit_solution(17251452369388142467)
XLA Ops:
  0.6 1.1 %shard_map.88 = f32[1,64,128]{2,1,0:T(8,128)S(1)} custom-call(f32[1,128,128]{2,1,0:T(8,128)} %inverse_far.5, f32[1,128,128]{2,1,0:T(8,128)} %link_far.1), custom_call_target="tpu_custom_call" | custom-call | flops 2097152 | bytes 196608 | tf_op jit(solution)/shard_map/pallas_call | solution.py:36
  1.7 3.1 %collective-permute-start = (f32[1,64,128]{2,1,0:T(8,128)S(1)}, f32[1,64,128]{2,1,0:T(8,128)S(1)}, u32[]{:S(2)}, u32[]{:S(2)}) collective-permute-start(f32[1,64,128]{2,1,0:T(8,128)S(1)} %shard_map.88), channel_id=1, source_target_pairs={{0,8},{4,12},{8,0},{12,4},{16,24},{20,28},{24,16},{28,20},{1,9},{5... | collective-permute-start | bytes 98312 | tf_op jit(solution)/shard_map/ppermute | solution.py:195
  4.8 2.6 %collective-permute-start.1 = (f32[1,64,128]{2,1,0:T(8,128)S(1)}, f32[1,64,128]{2,1,0:T(8,128)S(1)}, u32[]{:S(2)}, u32[]{:S(2)}) collective-permute-start(f32[1,64,128]{2,1,0:T(8,128)S(1)} %shard_map.88), channel_id=1, source_target_pairs={{0,16},{4,20},{8,24},{12,28},{16,0},{20,4},{24,8},{28,12},{1,17},{... | collective-permute-start | bytes 98312 | tf_op jit(solution)/shard_map/ppermute | solution.py:195
  7.4 2.2 %shard_map.87 = (f32[2,128,128]{2,1,0:T(8,128)S(1)}, f32[128,128]{1,0:T(8,128)S(1)}, f32[128,128]{1,0:T(8,128)S(1)}, f32[128,128]{1,0:T(8,128)S(1)}, f32[128,128]{1,0:T(8,128)S(1)}) custom-call(f32[1,128,128]{2,1,0:T(8,128)} %inverse_far.5, s32[1,2]{1,0:T(1,128)} %refs_1_.1, f32[1,2,128,128]{3,2,1,0:T(8,128)} %refs_2_.1, f32[1,2,128,128]{3,2,1,0:T(8,128)} %refs_3_.1, ...), custom_call_target="tpu_custom_call" | custom-call | flops 50331648 | bytes 1048576 | tf_op jit(solution)/shard_map/pallas_call | solution.py:36
  9.6 0.6 %collective-permute-done.1 = f32[1,64,128]{2,1,0:T(8,128)S(1)} collective-permute-done((f32[1,64,128]{2,1,0:T(8,128)S(1)}, f32[1,64,128]{2,1,0:T(8,128)S(1)}, u32[]{:S(2)}, u32[]{:S(2)}) %collective-permute-start.1) | collective-permute-done | bytes 32800 | tf_op jit(solution)/shard_map/ppermute | solution.py:195
  10.2 2.9 %collective-permute-done.2 = f32[1,64,128]{2,1,0:T(8,128)S(1)} collective-permute-done((f32[1,64,128]{2,1,0:T(8,128)S(1)}, f32[1,64,128]{2,1,0:T(8,128)S(1)}, u32[]{:S(2)}, u32[]{:S(2)}) %collective-permute-start.2) | collective-permute-done | bytes 32800 | tf_op jit(solution)/shard_map/ppermute | solution.py:195
  13.1 1.6 %collective-permute-start.4 = (f32[4,64,128]{2,1,0:T(8,128)S(1)}, f32[4,64,128]{2,1,0:T(8,128)S(1)}, u32[]{:S(2)}, u32[]{:S(2)}) collective-permute-start(f32[4,64,128]{2,1,0:T(8,128)S(1)} %pad_maximum_fusion.mine), channel_id=1, source_target_pairs={{0,4},{4,0},{8,12},{12,8},{16,20},{20,16},{24,28},{28,24},{1,5},{5... | collective-permute-start | bytes 393224 | tf_op jit(solution)/shard_map/ppermute | solution.py:195
  14.7 0.5 %collective-permute-start.6 = (f32[128,128]{1,0:T(8,128)S(1)}, f32[128,128]{1,0:T(8,128)S(1)}, u32[]{:S(2)}, u32[]{:S(2)}) collective-permute-start(f32[128,128]{1,0:T(8,128)S(1)} %get-tuple-element.11), channel_id=1, source_target_pairs={{0,1},{1,0},{2,3},{3,2},{4,5},{5,4},{6,7},{7,6},{8,9},{9,8},{10,11... | collective-permute-start | bytes 196616 | tf_op jit(solution)/shard_map/ppermute | solution.py:195
  15.2 0.7 %collective-permute-done.7 = f32[128,128]{1,0:T(8,128)S(1)} collective-permute-done((f32[128,128]{1,0:T(8,128)S(1)}, f32[128,128]{1,0:T(8,128)S(1)}, u32[]{:S(2)}, u32[]{:S(2)}) %collective-permute-start.7) | collective-permute-done | bytes 65568 | tf_op jit(solution)/shard_map/ppermute | solution.py:195
  16.0 1.6 %collective-permute-start.8 = (f32[128,128]{1,0:T(8,128)S(1)}, f32[128,128]{1,0:T(8,128)S(1)}, u32[]{:S(2)}, u32[]{:S(2)}) collective-permute-start(f32[128,128]{1,0:T(8,128)S(1)} %add.10), channel_id=1, source_target_pairs={{0,2},{1,3},{2,0},{3,1},{4,6},{5,7},{6,4},{7,5},{8,10},{9,11},{10,... | collective-permute-start | bytes 196616 | tf_op jit(solution)/shard_map/ppermute | solution.py:195
  17.5 1.2 %shard_map.90 = f32[128,128]{1,0:T(8,128)S(1)} custom-call(f32[1,128,512]{2,1,0:T(8,128)} %rhs_far.3, f32[1,128,128]{2,1,0:T(8,128)} %inverse_far.5), custom_call_target="tpu_custom_call" | custom-call | flops 4194304 | bytes 196608 | tf_op jit(solution)/shard_map/pallas_call | solution.py:36
  18.8 0.5 %collective-permute-start.5 = (f32[4,64,128]{2,1,0:T(8,128)S(1)}, f32[4,64,128]{2,1,0:T(8,128)S(1)}, u32[]{:S(2)}, u32[]{:S(2)}) collective-permute-start(f32[4,64,128]{2,1,0:T(8,128)S(1)} %collective-permute-done.4.other), channel_id=1, source_target_pairs={{0,1},{1,0},{2,3},{3,2},{4,5},{5,4},{6,7},{7,6},{8,9},{9,8},{10,11... | collective-permute-start | bytes 393224 | tf_op jit(solution)/shard_map/ppermute | solution.py:195
  19.3 1.0 %collective-permute-done.8 = f32[128,128]{1,0:T(8,128)S(1)} collective-permute-done((f32[128,128]{1,0:T(8,128)S(1)}, f32[128,128]{1,0:T(8,128)S(1)}, u32[]{:S(2)}, u32[]{:S(2)}) %collective-permute-start.8) | collective-permute-done | bytes 65568 | tf_op jit(solution)/shard_map/ppermute | solution.py:195
  20.4 1.4 %collective-permute-start.11 = (f32[1,128,128]{2,1,0:T(8,128)S(1)}, f32[1,128,128]{2,1,0:T(8,128)S(1)}, u32[]{:S(2)}, u32[]{:S(2)}) collective-permute-start(f32[1,128,128]{2,1,0:T(8,128)S(1)} %subtract_bitcast_fusion.refs_1_), channel_id=1, source_target_pairs={{0,24},{4,28},{8,16},{12,20},{16,8},{20,12},{24,0},{28,4},{1,25},{... | collective-permute-start | bytes 196616 | tf_op jit(solution)/shard_map/ppermute | solution.py:195
  21.8 2.1 %collective-permute-start.9 = (f32[1,128,128]{2,1,0:T(8,128)S(1)}, f32[1,128,128]{2,1,0:T(8,128)S(1)}, u32[]{:S(2)}, u32[]{:S(2)}) collective-permute-start(f32[1,128,128]{2,1,0:T(8,128)S(1)} %subtract_bitcast_fusion.refs_1_), channel_id=1, source_target_pairs={{0,8},{4,12},{8,0},{12,4},{16,24},{20,28},{24,16},{28,20},{1,9},{5... | collective-permute-start | bytes 196616 | tf_op jit(solution)/shard_map/ppermute | solution.py:195
  23.9 4.2 %shard_map.89.refs_0_ = f32[8,256,128]{2,1,0:T(8,128)S(1)} custom-call(f32[4,64,128]{2,1,0:T(8,128)S(1)} %pad_maximum_fusion.mine, f32[4,64,128]{2,1,0:T(8,128)S(1)} %collective-permute-done.3.mine_rest, f32[4,64,128]{2,1,0:T(8,128)S(1)} %collective-permute-done.4.other, f32[4,64,128]{2,1,0:T(8,128)S(1)} %collective-permute-done.5.other_rest), custom_call_target="tpu_custom_call" | custom-call | flops 134217728 | bytes 2097152 | tf_op jit(solution)/shard_map/pallas_call | solution.py:36
  28.5 0.6 %collective-permute-start.12 = (f32[128,128]{1,0:T(8,128)S(1)}, f32[128,128]{1,0:T(8,128)S(1)}, u32[]{:S(2)}, u32[]{:S(2)}) collective-permute-start(f32[128,128]{1,0:T(8,128)S(1)} %shard_map.92), channel_id=1, source_target_pairs={{0,4},{4,0},{8,12},{12,8},{16,20},{20,16},{24,28},{28,24},{1,5},{5... | collective-permute-start | bytes 196616 | tf_op jit(solution)/shard_map/ppermute | solution.py:195
  29.1 0.4 shard_map.91
  29.4 3.4 %collective-permute-done.12 = f32[128,128]{1,0:T(8,128)S(1)} collective-permute-done((f32[128,128]{1,0:T(8,128)S(1)}, f32[128,128]{1,0:T(8,128)S(1)}, u32[]{:S(2)}, u32[]{:S(2)}) %collective-permute-start.12) | collective-permute-done | bytes 65568 | tf_op jit(solution)/shard_map/ppermute | solution.py:195
  32.8 1.6 %collective-permute-start.13 = (f32[128,128]{1,0:T(8,128)S(1)}, f32[128,128]{1,0:T(8,128)S(1)}, u32[]{:S(2)}, u32[]{:S(2)}) collective-permute-start(f32[128,128]{1,0:T(8,128)S(1)} %add.11.carried), channel_id=1, source_target_pairs={{0,2},{1,3},{2,0},{3,1},{4,6},{5,7},{6,4},{7,5},{8,10},{9,11},{10,... | collective-permute-start | bytes 196616 | tf_op jit(solution)/shard_map/ppermute | solution.py:195
  34.4 2.8 %collective-permute-done.13.refs_2_ = f32[128,128]{1,0:T(8,128)S(1)} collective-permute-done((f32[128,128]{1,0:T(8,128)S(1)}, f32[128,128]{1,0:T(8,128)S(1)}, u32[]{:S(2)}, u32[]{:S(2)}) %collective-permute-start.13) | collective-permute-done | bytes 65568 | tf_op jit(solution)/shard_map/ppermute | solution.py:195
  37.2 2.4 %shard_map.86.base.refs_0_ = f32[2,128,512]{2,1,0:T(8,128)S(1)} custom-call(f32[1,2,128,512]{3,2,1,0:T(8,128)} %refs_4_.1, f32[1,2,128,128]{3,2,1,0:T(8,128)} %refs_2_.1), custom_call_target="tpu_custom_call" | custom-call | flops 67108864 | bytes 1572864 | tf_op jit(solution)/shard_map/pallas_call | solution.py:36
  39.5 1.8 %shard_map.93 = (f32[2,128,128]{2,1,0:T(8,128)S(1)}, f32[1,128,128]{2,1,0:T(8,128)}) custom-call(f32[1,128,128]{2,1,0:T(8,128)} %inverse_far.5, f32[2,128,512]{2,1,0:T(8,128)S(1)} %shard_map.86.base.refs_0_, f32[2,128,128]{2,1,0:T(8,128)S(1)} %get-tuple-element.9.down.refs_1_, f32[128,128]{1,0:T(8,128)S(1)} %add.11.carried), custom_call_target="tpu_custom_call" | custom-call | flops 12582912 | bytes 393216 | tf_op jit(solution)/shard_map/pallas_call | solution.py:36
  42.0 1.0 %shard_map.96 = f32[1,2,128,512]{3,2,1,0:T(8,128)} custom-call(f32[2,128,512]{2,1,0:T(8,128)S(1)} %shard_map.86.base.refs_0_, f32[2,128,128]{2,1,0:T(8,128)S(1)} %get-tuple-element.9.down.refs_1_, f32[128,128]{1,0:T(8,128)S(1)} %collective-permute-done.14.refs_2_, f32[2,128,128]{2,1,0:T(8,128)S(1)} %get-tuple-element.14.refs_3_, ...), custom_call_target="tpu_custom_call" | custom-call | flops 8388608 | bytes 1048576 | tf_op jit(solution)/shard_map/pallas_call | solution.py:36
  (23 shorter events, 1.2 us)
Async XLA Ops:
  1.7 7.9 %collective-permute-start = (f32[1,64,128]{2,1,0:T(8,128)S(1)}, f32[1,64,128]{2,1,0:T(8,128)S(1)}, u32[]{:S(2)}, u32[]{:S(2)}) collective-permute-start(f32[1,64,128]{2,1,0:T(8,128)S(1)} %shard_map.88), channel_id=1, source_target_pairs={{0,8},{4,12},{8,0},{12,4},{16,24},{20,28},{24,16},{28,20},{1,9},{5... | collective-permute-start | bytes 98312 | tf_op jit(solution)/shard_map/ppermute | solution.py:195
  4.8 5.4 %collective-permute-start.1 = (f32[1,64,128]{2,1,0:T(8,128)S(1)}, f32[1,64,128]{2,1,0:T(8,128)S(1)}, u32[]{:S(2)}, u32[]{:S(2)}) collective-permute-start(f32[1,64,128]{2,1,0:T(8,128)S(1)} %shard_map.88), channel_id=1, source_target_pairs={{0,16},{4,20},{8,24},{12,28},{16,0},{20,4},{24,8},{28,12},{1,17},{... | collective-permute-start | bytes 98312 | tf_op jit(solution)/shard_map/ppermute | solution.py:195
  7.4 5.7 %collective-permute-start.2 = (f32[1,64,128]{2,1,0:T(8,128)S(1)}, f32[1,64,128]{2,1,0:T(8,128)S(1)}, u32[]{:S(2)}, u32[]{:S(2)}) collective-permute-start(f32[1,64,128]{2,1,0:T(8,128)S(1)} %shard_map.88), channel_id=1, source_target_pairs={{0,24},{4,28},{8,16},{12,20},{16,8},{20,12},{24,0},{28,4},{1,25},{... | collective-permute-start | bytes 98312 | tf_op jit(solution)/shard_map/ppermute | solution.py:195
  13.1 5.7 %collective-permute-start.4 = (f32[4,64,128]{2,1,0:T(8,128)S(1)}, f32[4,64,128]{2,1,0:T(8,128)S(1)}, u32[]{:S(2)}, u32[]{:S(2)}) collective-permute-start(f32[4,64,128]{2,1,0:T(8,128)S(1)} %pad_maximum_fusion.mine), channel_id=1, source_target_pairs={{0,4},{4,0},{8,12},{12,8},{16,20},{20,16},{24,28},{28,24},{1,5},{5... | collective-permute-start | bytes 393224 | tf_op jit(solution)/shard_map/ppermute | solution.py:195
  14.7 1.3 %collective-permute-start.7 = (f32[128,128]{1,0:T(8,128)S(1)}, f32[128,128]{1,0:T(8,128)S(1)}, u32[]{:S(2)}, u32[]{:S(2)}) collective-permute-start(f32[128,128]{1,0:T(8,128)S(1)} %get-tuple-element.13), channel_id=1, source_target_pairs={{0,1},{1,0},{2,3},{3,2},{4,5},{5,4},{6,7},{7,6},{8,9},{9,8},{10,11... | collective-permute-start | bytes 196616 | tf_op jit(solution)/shard_map/ppermute | solution.py:195
  14.7 4.6 %collective-permute-start.6 = (f32[128,128]{1,0:T(8,128)S(1)}, f32[128,128]{1,0:T(8,128)S(1)}, u32[]{:S(2)}, u32[]{:S(2)}) collective-permute-start(f32[128,128]{1,0:T(8,128)S(1)} %get-tuple-element.11), channel_id=1, source_target_pairs={{0,1},{1,0},{2,3},{3,2},{4,5},{5,4},{6,7},{7,6},{8,9},{9,8},{10,11... | collective-permute-start | bytes 196616 | tf_op jit(solution)/shard_map/ppermute | solution.py:195
  16.0 4.3 %collective-permute-start.8 = (f32[128,128]{1,0:T(8,128)S(1)}, f32[128,128]{1,0:T(8,128)S(1)}, u32[]{:S(2)}, u32[]{:S(2)}) collective-permute-start(f32[128,128]{1,0:T(8,128)S(1)} %add.10), channel_id=1, source_target_pairs={{0,2},{1,3},{2,0},{3,1},{4,6},{5,7},{6,4},{7,5},{8,10},{9,11},{10,... | collective-permute-start | bytes 196616 | tf_op jit(solution)/shard_map/ppermute | solution.py:195
  18.7 5.2 %collective-permute-start.3 = (f32[4,64,128]{2,1,0:T(8,128)S(1)}, f32[4,64,128]{2,1,0:T(8,128)S(1)}, u32[]{:S(2)}, u32[]{:S(2)}) collective-permute-start(f32[4,64,128]{2,1,0:T(8,128)S(1)} %pad_maximum_fusion.mine), channel_id=1, source_target_pairs={{0,1},{1,0},{2,3},{3,2},{4,5},{5,4},{6,7},{7,6},{8,9},{9,8},{10,11... | collective-permute-start | bytes 393224 | tf_op jit(solution)/shard_map/ppermute | solution.py:195
  18.8 5.1 %collective-permute-start.5 = (f32[4,64,128]{2,1,0:T(8,128)S(1)}, f32[4,64,128]{2,1,0:T(8,128)S(1)}, u32[]{:S(2)}, u32[]{:S(2)}) collective-permute-start(f32[4,64,128]{2,1,0:T(8,128)S(1)} %collective-permute-done.4.other), channel_id=1, source_target_pairs={{0,1},{1,0},{2,3},{3,2},{4,5},{5,4},{6,7},{7,6},{8,9},{9,8},{10,11... | collective-permute-start | bytes 393224 | tf_op jit(solution)/shard_map/ppermute | solution.py:195
  20.3 7.7 %collective-permute-start.10 = (f32[1,128,128]{2,1,0:T(8,128)S(1)}, f32[1,128,128]{2,1,0:T(8,128)S(1)}, u32[]{:S(2)}, u32[]{:S(2)}) collective-permute-start(f32[1,128,128]{2,1,0:T(8,128)S(1)} %subtract_bitcast_fusion.refs_1_), channel_id=1, source_target_pairs={{0,16},{4,20},{8,24},{12,28},{16,0},{20,4},{24,8},{28,12},{1,17},{... | collective-permute-start | bytes 196616 | tf_op jit(solution)/shard_map/ppermute | solution.py:195
  20.4 7.7 %collective-permute-start.11 = (f32[1,128,128]{2,1,0:T(8,128)S(1)}, f32[1,128,128]{2,1,0:T(8,128)S(1)}, u32[]{:S(2)}, u32[]{:S(2)}) collective-permute-start(f32[1,128,128]{2,1,0:T(8,128)S(1)} %subtract_bitcast_fusion.refs_1_), channel_id=1, source_target_pairs={{0,24},{4,28},{8,16},{12,20},{16,8},{20,12},{24,0},{28,4},{1,25},{... | collective-permute-start | bytes 196616 | tf_op jit(solution)/shard_map/ppermute | solution.py:195
  21.8 6.3 %collective-permute-start.9 = (f32[1,128,128]{2,1,0:T(8,128)S(1)}, f32[1,128,128]{2,1,0:T(8,128)S(1)}, u32[]{:S(2)}, u32[]{:S(2)}) collective-permute-start(f32[1,128,128]{2,1,0:T(8,128)S(1)} %subtract_bitcast_fusion.refs_1_), channel_id=1, source_target_pairs={{0,8},{4,12},{8,0},{12,4},{16,24},{20,28},{24,16},{28,20},{1,9},{5... | collective-permute-start | bytes 196616 | tf_op jit(solution)/shard_map/ppermute | solution.py:195
  28.5 4.3 %collective-permute-start.12 = (f32[128,128]{1,0:T(8,128)S(1)}, f32[128,128]{1,0:T(8,128)S(1)}, u32[]{:S(2)}, u32[]{:S(2)}) collective-permute-start(f32[128,128]{1,0:T(8,128)S(1)} %shard_map.92), channel_id=1, source_target_pairs={{0,4},{4,0},{8,12},{12,8},{16,20},{20,16},{24,28},{28,24},{1,5},{5... | collective-permute-start | bytes 196616 | tf_op jit(solution)/shard_map/ppermute | solution.py:195
  32.8 4.3 %collective-permute-start.13 = (f32[128,128]{1,0:T(8,128)S(1)}, f32[128,128]{1,0:T(8,128)S(1)}, u32[]{:S(2)}, u32[]{:S(2)}) collective-permute-start(f32[128,128]{1,0:T(8,128)S(1)} %add.11.carried), channel_id=1, source_target_pairs={{0,2},{1,3},{2,0},{3,1},{4,6},{5,7},{6,4},{7,5},{8,10},{9,11},{10,... | collective-permute-start | bytes 196616 | tf_op jit(solution)/shard_map/ppermute | solution.py:195
  34.4 7.3 %collective-permute-start.15 = (f32[128,128]{1,0:T(8,128)S(1)}, f32[128,128]{1,0:T(8,128)S(1)}, u32[]{:S(2)}, u32[]{:S(2)}) collective-permute-start(f32[128,128]{1,0:T(8,128)S(1)} %add.11.carried), channel_id=1, source_target_pairs={{0,1},{1,0},{2,3},{3,2},{4,5},{5,4},{6,7},{7,6},{8,9},{9,8},{10,11... | collective-permute-start | bytes 196616 | tf_op jit(solution)/shard_map/ppermute | solution.py:195
  37.2 4.8 %collective-permute-start.14 = (f32[128,128]{1,0:T(8,128)S(1)}, f32[128,128]{1,0:T(8,128)S(1)}, u32[]{:S(2)}, u32[]{:S(2)}) collective-permute-start(f32[128,128]{1,0:T(8,128)S(1)} %collective-permute-done.13.refs_2_), channel_id=1, source_target_pairs={{0,1},{1,0},{2,3},{3,2},{4,5},{5,4},{6,7},{7,6},{8,9},{9,8},{10,11... | collective-permute-start | bytes 196616 | tf_op jit(solution)/shard_map/ppermute | solution.py:195

commit v4 on v3

v4 whole, which is shorter than its diff:
```python
import jax
import jax.numpy as jnp
from jax import lax
from jax.experimental import pallas as pl
from jax.experimental.pallas import tpu as pltpu
from jax.sharding import PartitionSpec as P

HIGH = lax.Precision.HIGHEST
F32 = jnp.float32
BF16 = jnp.bfloat16
VMEM = pl.BlockSpec(memory_space=pltpu.VMEM)
HBM = pl.BlockSpec(memory_space=pltpu.HBM)


def dot(a, b):
    return jnp.dot(a, b, precision=HIGH, preferred_element_type=F32)


def dot_ta(a, b):
    return lax.dot_general(
        a, b, (((0,), (0,)), ((), ())), precision=HIGH, preferred_element_type=F32
    )


def split(x):
    high = x.astype(BF16)
    return high, (x - high.astype(F32)).astype(BF16)


def left(x):
    high, low = split(x)
    return jnp.concatenate([high, low, high], axis=1)


def right(x, axis=0):
    high, low = split(x)
    return jnp.concatenate([high, high, low], axis=axis)


def dot3(a, b):
    return jnp.dot(left(a), right(b), preferred_element_type=F32)


def dot3_tb(a, b):
    return lax.dot_general(
        left(a), right(b, 1), (((1,), (1,)), ((), ())), preferred_element_type=F32
    )


def shaped(*shape):
    return jax.ShapeDtypeStruct(shape, F32)


def call(body, outs, flops, moved, *args, held=(), far=0, out_specs=None):
    args = [pltpu.with_memory_space_constraint(a, pltpu.HBM) for a in args[:far]] + list(args[far:])
    return pl.pallas_call(
        body,
        out_shape=outs,
        in_specs=[HBM] * far + [VMEM] * (len(args) - far),
        out_specs=out_specs or jax.tree.map(lambda _: VMEM, outs),
        scratch_shapes=held,
        cost_estimate=pl.CostEstimate(flops=flops, bytes_accessed=moved, transcendentals=0),
        compiler_params=pltpu.CompilerParams(vmem_limit_bytes=48 << 20),
    )(*args)


def landing(*args):
    holds = [
        (pltpu.SMEM if a.dtype == jnp.int32 else pltpu.VMEM)(a.shape, a.dtype) for a in args
    ]
    return holds + [pltpu.SemaphoreType.DMA((len(args),))]


def fetch(sources, targets, sems):
    copies = [
        pltpu.make_async_copy(a, b, sems.at[i]) for i, (a, b) in enumerate(zip(sources, targets))
    ]
    for copy in copies:
        copy.start()
    return copies


def columns_of(block, width):
    return pl.ds(pl.multiple_of(block * width, width), width)


def begin(*refs):
    sources, outs = refs[:5], refs[5:-6]
    down, slots = outs[0], outs[1:]
    targets, sems = refs[-6:-1], refs[-1]
    inverse, pattern, leaf_inv, coupling, rhs = targets
    copies = fetch(sources, targets, sems)
    group = lax.axis_index("grp")
    count, width = down.shape[0], slots[0].shape[1]
    for copy in copies[:4]:
        copy.wait()
    for k in range(count):
        present = pattern[0, k].astype(F32)
        mixed = dot(coupling[0, k] * present, leaf_inv[0, k])
        down[k] = dot(inverse[0], mixed)
    copies[4].wait()
    for slot in reversed(range(len(slots))):
        cols = columns_of(group ^ slot, width)
        total = dot(down[0], rhs[0, 0, :, cols])
        for k in range(1, count):
            total += dot(down[k], rhs[0, k, :, cols])
        slots[slot][...] = total


def section_map(inverse, link, order_only, out):
    out[0] = -dot(inverse[0], link[0])


def leaf_base(rhs, leaf_inv, down, base, factors):
    order = down.shape[1]
    for k in range(base.shape[0]):
        gram = dot_ta(leaf_inv[0, k], leaf_inv[0, k])
        base[k] = dot(gram, rhs[0, k])
        factors[k * order : (k + 1) * order] = left(down[k].T)


def own_columns(rhs, inverse, out):
    out[...] = dot(inverse[0], rhs[0, :, columns_of(lax.axis_index("grp"), out.shape[1])])


def operator_rows(*refs):
    parts, (held, maps) = refs[:-2], refs[-2:]
    sections, both, order = held.shape
    me = lax.axis_index("leaf")
    size = parts[0].shape[0]
    half = len(parts) // 2

    @pl.loop(0, size, unroll=size <= 8)
    def _(i):
        for p in range(half):
            maps[2 * (p * size + i) ^ me] = parts[p][i]
            maps[2 * (p * size + i) ^ 1 ^ me] = parts[half + p][i]

    line = lax.broadcasted_iota(jnp.int32, (both, order), 0)
    column = lax.broadcasted_iota(jnp.int32, (both, order), 1)
    target = jnp.where(line < order, me, me ^ 1)
    ones = jnp.where((line & (order - 1)) == column, target, -1)

    held[0] = (ones == 0).astype(F32)

    @pl.loop(1, sections, unroll=sections <= 8)
    def _(section):
        held[section] = dot3_tb(held[section - 1], maps[section]) + (ones == section).astype(F32)

    @pl.loop(0, sections - 1, unroll=sections <= 8)
    def _(turn):
        section = sections - 2 - turn
        held[section] += dot3(held[section + 1], maps[section + 1])


def apply_rows(which, *refs):
    held, parts, out = refs[0], refs[1:-1], refs[-1]
    order = held.shape[2]
    rows = slice(which * order, (which + 1) * order)
    me = lax.axis_index("leaf")
    size = parts[0].shape[0]
    total = None
    for p, part in enumerate(parts):
        for i in range(size):
            piece = dot(held[2 * (p * size + i) ^ me, rows], part[i])
            total = piece if total is None else total + piece
    out[...] = total


def finish(base, factors, inverse, spread, leaves, solved, pieces, sems):
    groups, count, order, width = pieces.shape
    copies = []
    for j in range(groups):
        cols = slice(j * width, (j + 1) * width)
        taken = jnp.dot(factors[...], right(spread[j]), preferred_element_type=F32)
        for k in range(count):
            pieces[j, k] = base[k, :, cols] - taken[k * order : (k + 1) * order]
        copy = pltpu.make_async_copy(pieces.at[j], leaves.at[0, :, :, cols], sems.at[j])
        copy.start()
        copies.append(copy)
    solved[0] = dot_ta(inverse[0], spread[lax.axis_index("grp")])
    for copy in copies:
        copy.wait()


def swap(value, axis, bit):
    count = lax.axis_size(axis)
    return lax.ppermute(value, axis, [(i, i ^ bit) for i in range(count)])


def gather_pairs(value):
    bit, sections = 2, lax.axis_size("leaf")
    parts = [value]
    while bit < sections:
        if len(parts) > 1:
            value = jnp.concatenate(parts, axis=0)
        masks = [bit] if 2 * bit >= sections else [bit, 2 * bit, 3 * bit]
        parts = [value] + [swap(value, "leaf", m) for m in masks]
        bit *= 4 if len(masks) > 1 else 2
    return parts


def shards(leaf_rhs, leaf_inv, coupling, pattern, sep_rhs, sep_inv, chain_link):
    sections, groups = lax.axis_size("leaf"), lax.axis_size("grp")
    count, order, columns = leaf_rhs.shape[1:]
    width = columns // groups
    cube = 2 * order**3
    block = shaped(order, width)
    block_bytes = order * width * 4

    first = (sep_inv, pattern, leaf_inv, coupling, leaf_rhs)
    down, *slots = call(
        begin,
        (shaped(count, order, order),) + (block,) * groups,
        (2 * count + groups * count) * cube,
        2 * leaf_rhs.size * 4,
        *first, held=landing(*first), far=5,
    )
    step = call(
        section_map, shaped(1, order, order), cube, 3 * block_bytes,
        sep_inv, chain_link, down,
    )
    slots = dict(enumerate(slots))
    own = call(own_columns, block, cube, 3 * block_bytes, sep_rhs, sep_inv)
    bit = 1
    while bit < groups:
        ahead = {
            m: slots[m] + swap(slots[m + bit], "grp", bit)
            for m in reversed(range(2 * bit, groups, 2 * bit))
        }
        slots = {0: slots[0] + swap(slots[bit], "grp", bit), **ahead}
        bit *= 2
    maps = gather_pairs(step)
    others = [swap(part, "leaf", 1) for part in maps]
    offset = own - slots[0]
    offsets = gather_pairs(offset[None])
    rows = call(
        operator_rows, shaped(sections, 2 * order, order), 4 * sections * cube,
        4 * sections * block_bytes, *maps, *others,
        held=[pltpu.VMEM((sections, order, order), F32)],
    )

    base, factors = call(
        leaf_base,
        (shaped(count, order, columns), jax.ShapeDtypeStruct((count * order, 3 * order), BF16)),
        (groups + 1) * count * cube, 3 * leaf_rhs.size * 4, leaf_rhs, leaf_inv, down,
    )

    def applied(which):
        return call(
            lambda *refs: apply_rows(which, *refs), block, sections // 2 * cube,
            sections * block_bytes, rows, *offsets,
        )

    theirs = swap(applied(1), "leaf", 1)
    carried = applied(0) + theirs
    spread = lax.all_gather(carried, "grp")
    return call(
        finish, (shaped(1, count, order, columns), shaped(1, order, width)),
        (4 * count + 1) * cube, 3 * leaf_rhs.size * 4,
        base, factors, sep_inv, spread,
        held=[pltpu.VMEM((groups, count, order, width), F32), pltpu.SemaphoreType.DMA((groups,))],
        out_specs=(HBM, VMEM),
    )


def solution(mesh):
    in_specs = (
        P("leaf", "grp", None, None),
        P("leaf", "grp", None, None),
        P("leaf", "grp", None, None),
        P("leaf", "grp"),
        P("leaf", None, None),
        P("leaf", None, None),
        P("leaf", None, None),
    )
    out_specs = (P("leaf", "grp", None, None), P("leaf", None, "grp"))
    return jax.shard_map(shards, mesh=mesh, in_specs=in_specs, out_specs=out_specs, check_vma=False)
```

time: 43.3 us -> 38.5 us (0.89)
  Pallas kernels: 15.1 us -> 8.07 us
  blocking collectives: 0 us -> 5.79 us
  waiting for transfers between devices: 11.4 us -> 5.97 us
  starting transfers between devices: 15.6 us -> 17.7 us
    pallas_call x11 -> x8, Pallas kernels: 15.1 us -> 8.07 us  [call(): pl.pallas_call(body, out_shape=outs, in_specs=[HBM] * far + [VMEM] * (len...]
    all_gather x0 -> x1, blocking collectives: none -> 5.79 us  [shards(): spread = lax.all_gather(carried, 'grp')]
    ppermute x16 -> x14, waiting for transfers between devices: 11.4 us -> 5.97 us  [swap(): return lax.ppermute(value, axis, [(i, i ^ bit) for i in range(count)])]
    ppermute x16 -> x14, starting transfers between devices: 15.6 us -> 17.7 us  [swap(): return lax.ppermute(value, axis, [(i, i ^ bit) for i in range(count)])]
  transfers between devices with their start and end apart: 16 -> 14, of which waited for: 6 -> 5; matrix products, arithmetic and copies ran while one was open for 0% -> 0% of each run, Pallas kernels for 29% -> 10%
where the time goes in v4:
time: 38.5 us; the launch traced here: 38.4 us
  starting transfers between devices  17.7 us (46%)
  Pallas kernels  8.07 us (21%)
  waiting for transfers between devices  5.97 us (16%)
  blocking collectives  5.79 us (15%)
  between operations  0.75 us (2%)
    ppermute x14, starting transfers between devices, swap(): return lax.ppermute(value, axis, [(i, i ^ bit) for i in range(count)])  17.7 us
    pallas_call x8, Pallas kernels, call(): pl.pallas_call(body, out_shape=outs, in_specs=[HBM] * far + [VMEM] * (len...  8.07 us
    ppermute x14, waiting for transfers between devices, swap(): return lax.ppermute(value, axis, [(i, i ^ bit) for i in range(count)])  5.97 us
    all_gather x1, blocking collectives, shards(): spread = lax.all_gather(carried, 'grp')  5.79 us
  transfers between devices with their start and end apart: 14, of which 5 were waited for; matrix products, arithmetic and copies ran while one was open for 0% of the time, Pallas kernels for 10%

profile of v4, /device:TPU:0, one launch (start us, length us, event | category | flops | bytes accessed | tf_op | source)
XLA Modules:
  0.0 38.4 jit_solution(1191724380706654322)
XLA Ops:
  0.7 2.2 %shard_map.86 = (f32[2,128,128]{2,1,0:T(8,128)S(1)}, f32[128,128]{1,0:T(8,128)S(1)}, f32[128,128]{1,0:T(8,128)S(1)}, f32[128,128]{1,0:T(8,128)S(1)}, f32[128,128]{1,0:T(8,128)S(1)}) custom-call(f32[1,128,128]{2,1,0:T(8,128)} %inverse.5, s32[1,2]{1,0:T(1,128)} %refs_1_.1, f32[1,2,128,128]{3,2,1,0:T(8,128)} %leaf_inv.1, f32[1,2,128,128]{3,2,1,0:T(8,128)} %refs_3_.1, ...), custom_call_target="tpu_custom_call" | custom-call | flops 50331648 | bytes 1048576 | tf_op jit(solution)/shard_map/pallas_call | solution.py:56
  2.9 0.5 %collective-permute-start.8 = (f32[128,128]{1,0:T(8,128)S(1)}, f32[128,128]{1,0:T(8,128)S(1)}, u32[]{:S(2)}, u32[]{:S(2)}) collective-permute-start(f32[128,128]{1,0:T(8,128)S(1)} %get-tuple-element.15), channel_id=1, source_target_pairs={{0,1},{1,0},{2,3},{3,2},{4,5},{5,4},{6,7},{7,6},{8,9},{9,8},{10,11... | collective-permute-start | bytes 196616 | tf_op jit(solution)/shard_map/ppermute | solution.py:188
  3.4 0.2 shard_map.88.refs_0_
  3.6 4.7 %collective-permute-start.2 = (f32[1,128,128]{2,1,0:T(8,128)S(1)}, f32[1,128,128]{2,1,0:T(8,128)S(1)}, u32[]{:S(2)}, u32[]{:S(2)}) collective-permute-start(f32[1,128,128]{2,1,0:T(8,128)S(1)} %shard_map.88.refs_0_), channel_id=1, source_target_pairs={{0,24},{4,28},{8,16},{12,20},{16,8},{20,12},{24,0},{28,4},{1,25},{... | collective-permute-start | bytes 196616 | tf_op jit(solution)/shard_map/ppermute | solution.py:188
  8.3 0.6 %collective-permute-start = (f32[1,128,128]{2,1,0:T(8,128)S(1)}, f32[1,128,128]{2,1,0:T(8,128)S(1)}, u32[]{:S(2)}, u32[]{:S(2)}) collective-permute-start(f32[1,128,128]{2,1,0:T(8,128)S(1)} %shard_map.88.refs_0_), channel_id=1, source_target_pairs={{0,8},{4,12},{8,0},{12,4},{16,24},{20,28},{24,16},{28,20},{1,9},{5... | collective-permute-start | bytes 196616 | tf_op jit(solution)/shard_map/ppermute | solution.py:188
  9.0 1.7 %collective-permute-start.9 = (f32[128,128]{1,0:T(8,128)S(1)}, f32[128,128]{1,0:T(8,128)S(1)}, u32[]{:S(2)}, u32[]{:S(2)}) collective-permute-start(f32[128,128]{1,0:T(8,128)S(1)} %add.13), channel_id=1, source_target_pairs={{0,2},{1,3},{2,0},{3,1},{4,6},{5,7},{6,4},{7,5},{8,10},{9,11},{10,... | collective-permute-start | bytes 196616 | tf_op jit(solution)/shard_map/ppermute | solution.py:188
  10.7 0.2 shard_map.90
  10.9 0.3 collective-permute-done.2.refs_3_
  11.2 1.6 %collective-permute-start.3 = (f32[1,128,128]{2,1,0:T(8,128)S(1)}, f32[1,128,128]{2,1,0:T(8,128)S(1)}, u32[]{:S(2)}, u32[]{:S(2)}) collective-permute-start(f32[1,128,128]{2,1,0:T(8,128)S(1)} %shard_map.88.refs_0_), channel_id=1, source_target_pairs={{0,4},{4,0},{8,12},{12,8},{16,20},{20,16},{24,28},{28,24},{1,5},{5... | collective-permute-start | bytes 196616 | tf_op jit(solution)/shard_map/ppermute | solution.py:188
  12.8 1.6 %collective-permute-done.1.refs_2_ = f32[1,128,128]{2,1,0:T(8,128)S(1)} collective-permute-done((f32[1,128,128]{2,1,0:T(8,128)S(1)}, f32[1,128,128]{2,1,0:T(8,128)S(1)}, u32[]{:S(2)}, u32[]{:S(2)}) %collective-permute-start.1) | collective-permute-done | bytes 65568 | tf_op jit(solution)/shard_map/ppermute | solution.py:188
  14.4 1.5 %collective-permute-start.6 = (f32[1,128,128]{2,1,0:T(8,128)S(1)}, f32[1,128,128]{2,1,0:T(8,128)S(1)}, u32[]{:S(2)}, u32[]{:S(2)}) collective-permute-start(f32[1,128,128]{2,1,0:T(8,128)S(1)} %collective-permute-done.2.refs_3_), channel_id=1, source_target_pairs={{0,4},{4,0},{8,12},{12,8},{16,20},{20,16},{24,28},{28,24},{1,5},{5... | collective-permute-start | bytes 196616 | tf_op jit(solution)/shard_map/ppermute | solution.py:188
  15.9 0.5 %collective-permute-start.5 = (f32[1,128,128]{2,1,0:T(8,128)S(1)}, f32[1,128,128]{2,1,0:T(8,128)S(1)}, u32[]{:S(2)}, u32[]{:S(2)}) collective-permute-start(f32[1,128,128]{2,1,0:T(8,128)S(1)} %collective-permute-done.1.refs_2_), channel_id=1, source_target_pairs={{0,4},{4,0},{8,12},{12,8},{16,20},{20,16},{24,28},{28,24},{1,5},{5... | collective-permute-start | bytes 196616 | tf_op jit(solution)/shard_map/ppermute | solution.py:188
  16.4 1.5 %collective-permute-start.4 = (f32[1,128,128]{2,1,0:T(8,128)S(1)}, f32[1,128,128]{2,1,0:T(8,128)S(1)}, u32[]{:S(2)}, u32[]{:S(2)}) collective-permute-start(f32[1,128,128]{2,1,0:T(8,128)S(1)} %collective-permute-done.refs_1_), channel_id=1, source_target_pairs={{0,4},{4,0},{8,12},{12,8},{16,20},{20,16},{24,28},{28,24},{1,5},{5... | collective-permute-start | bytes 196616 | tf_op jit(solution)/shard_map/ppermute | solution.py:188
  18.0 2.5 %collective-permute-start.12 = (f32[1,128,128]{2,1,0:T(8,128)S(1)}, f32[1,128,128]{2,1,0:T(8,128)S(1)}, u32[]{:S(2)}, u32[]{:S(2)}) collective-permute-start(f32[1,128,128]{2,1,0:T(8,128)S(1)} %subtract_bitcast_fusion.refs_1_), channel_id=1, source_target_pairs={{0,24},{4,28},{8,16},{12,20},{16,8},{20,12},{24,0},{28,4},{1,25},{... | collective-permute-start | bytes 196616 | tf_op jit(solution)/shard_map/ppermute | solution.py:188
  20.5 1.9 %collective-permute-start.10 = (f32[1,128,128]{2,1,0:T(8,128)S(1)}, f32[1,128,128]{2,1,0:T(8,128)S(1)}, u32[]{:S(2)}, u32[]{:S(2)}) collective-permute-start(f32[1,128,128]{2,1,0:T(8,128)S(1)} %subtract_bitcast_fusion.refs_1_), channel_id=1, source_target_pairs={{0,8},{4,12},{8,0},{12,4},{16,24},{20,28},{24,16},{28,20},{1,9},{5... | collective-permute-start | bytes 196616 | tf_op jit(solution)/shard_map/ppermute | solution.py:188
  22.4 1.9 %shard_map.89.refs_0_ = f32[8,256,128]{2,1,0:T(8,128)S(1)} custom-call(f32[1,128,128]{2,1,0:T(8,128)S(1)} %shard_map.88.refs_0_, f32[1,128,128]{2,1,0:T(8,128)S(1)} %collective-permute-done.refs_1_, f32[1,128,128]{2,1,0:T(8,128)S(1)} %collective-permute-done.1.refs_2_, f32[1,128,128]{2,1,0:T(8,128)S(1)} %collective-permute-done.2.refs_3_, ...), custom_call_target="tpu_custom_call" | custom-call | flops 134217728 | bytes 2097152 | tf_op jit(solution)/shard_map/pallas_call | solution.py:56
  24.5 1.6 %collective-permute-done.11.refs_3_ = f32[1,128,128]{2,1,0:T(8,128)S(1)} collective-permute-done((f32[1,128,128]{2,1,0:T(8,128)S(1)}, f32[1,128,128]{2,1,0:T(8,128)S(1)}, u32[]{:S(2)}, u32[]{:S(2)}) %collective-permute-start.11) | collective-permute-done | bytes 65568 | tf_op jit(solution)/shard_map/ppermute | solution.py:188
  26.1 0.4 shard_map.92
  26.5 0.6 %collective-permute-start.13 = (f32[128,128]{1,0:T(8,128)S(1)}, f32[128,128]{1,0:T(8,128)S(1)}, u32[]{:S(2)}, u32[]{:S(2)}) collective-permute-start(f32[128,128]{1,0:T(8,128)S(1)} %shard_map.92), channel_id=1, source_target_pairs={{0,4},{4,0},{8,12},{12,8},{16,20},{20,16},{24,28},{28,24},{1,5},{5... | collective-permute-start | bytes 196616 | tf_op jit(solution)/shard_map/ppermute | solution.py:188
  27.2 1.1 %shard_map.87 = (f32[2,128,512]{2,1,0:T(8,128)S(1)}, bf16[256,384]{1,0:T(8,128)(2,1)S(1)}) custom-call(f32[1,2,128,512]{3,2,1,0:T(8,128)S(1)} %copy-done, f32[1,2,128,128]{3,2,1,0:T(8,128)S(1)} %copy-done.2, f32[2,128,128]{2,1,0:T(8,128)S(1)} %get-tuple-element.9.down.order_only), custom_call_target="tpu_custom_call" | custom-call | flops 41943040 | bytes 1572864 | tf_op jit(solution)/shard_map/pallas_call | solution.py:56
  28.2 0.4 shard_map.91
  28.6 2.2 %collective-permute-done.13 = f32[128,128]{1,0:T(8,128)S(1)} collective-permute-done((f32[128,128]{1,0:T(8,128)S(1)}, f32[128,128]{1,0:T(8,128)S(1)}, u32[]{:S(2)}, u32[]{:S(2)}) %collective-permute-start.13) | collective-permute-done | bytes 65568 | tf_op jit(solution)/shard_map/ppermute | solution.py:188
  30.9 5.8 %all-gather = f32[512,128]{1,0:T(8,128)S(1)} all-gather(f32[128,128]{1,0:T(8,128)S(1)} %add.15), channel_id=2, replica_groups=mesh['leaf'=8,'grp'=4] {'grp'}, dimensions={0}, use_global_device_ids=true | all-gather | bytes 327680 | tf_op jit(solution)/shard_map/all_gather | solution.py:257
  36.6 1.7 %shard_map.93 = (f32[1,2,128,512]{3,2,1,0:T(8,128)}, f32[1,128,128]{2,1,0:T(8,128)}) custom-call(f32[2,128,512]{2,1,0:T(8,128)S(1)} %get-tuple-element.10.base, bf16[256,384]{1,0:T(8,128)(2,1)S(1)} %get-tuple-element.11.factors, f32[1,128,128]{2,1,0:T(8,128)S(1)} %copy-done.1, f32[4,128,128]{2,1,0:T(8,128)S(1)} %bitcast.3), custom_call_target="tpu_custom_call" | custom-call | flops 37748736 | bytes 1572864 | tf_op jit(solution)/shard_map/pallas_call | solution.py:56
  (26 shorter events, 0.2 us)
Async XLA Ops:
  0.6 2.8 %copy-start.1 = (f32[1,128,128]{2,1,0:T(8,128)S(1)}, f32[1,128,128]{2,1,0:T(8,128)}, u32[]{:S(2)}) copy-start(f32[1,128,128]{2,1,0:T(8,128)} %inverse.5) | copy-start | bytes 196612
  0.6 2.7 %copy-start.4 = (f32[1,128,128]{2,1,0:T(8,128)S(1)}, f32[1,128,128]{2,1,0:T(8,128)}, u32[]{:S(2)}) copy-start(f32[1,128,128]{2,1,0:T(8,128)} %link.1) | copy-start | bytes 196612
  2.9 6.1 %collective-permute-start.8 = (f32[128,128]{1,0:T(8,128)S(1)}, f32[128,128]{1,0:T(8,128)S(1)}, u32[]{:S(2)}, u32[]{:S(2)}) collective-permute-start(f32[128,128]{1,0:T(8,128)S(1)} %get-tuple-element.15), channel_id=1, source_target_pairs={{0,1},{1,0},{2,3},{3,2},{4,5},{5,4},{6,7},{7,6},{8,9},{9,8},{10,11... | collective-permute-start | bytes 196616 | tf_op jit(solution)/shard_map/ppermute | solution.py:188
  3.4 7.3 %copy-start.3 = (f32[1,128,512]{2,1,0:T(8,128)S(1)}, f32[1,128,512]{2,1,0:T(8,128)}, u32[]{:S(2)}) copy-start(f32[1,128,512]{2,1,0:T(8,128)} %rhs.3) | copy-start | bytes 786436
  3.6 7.6 %collective-permute-start.2 = (f32[1,128,128]{2,1,0:T(8,128)S(1)}, f32[1,128,128]{2,1,0:T(8,128)S(1)}, u32[]{:S(2)}, u32[]{:S(2)}) collective-permute-start(f32[1,128,128]{2,1,0:T(8,128)S(1)} %shard_map.88.refs_0_), channel_id=1, source_target_pairs={{0,24},{4,28},{8,16},{12,20},{16,8},{20,12},{24,0},{28,4},{1,25},{... | collective-permute-start | bytes 196616 | tf_op jit(solution)/shard_map/ppermute | solution.py:188
  8.3 6.1 %collective-permute-start.1 = (f32[1,128,128]{2,1,0:T(8,128)S(1)}, f32[1,128,128]{2,1,0:T(8,128)S(1)}, u32[]{:S(2)}, u32[]{:S(2)}) collective-permute-start(f32[1,128,128]{2,1,0:T(8,128)S(1)} %shard_map.88.refs_0_), channel_id=1, source_target_pairs={{0,16},{4,20},{8,24},{12,28},{16,0},{20,4},{24,8},{28,12},{1,17},{... | collective-permute-start | bytes 196616 | tf_op jit(solution)/shard_map/ppermute | solution.py:188
  8.3 7.6 %collective-permute-start = (f32[1,128,128]{2,1,0:T(8,128)S(1)}, f32[1,128,128]{2,1,0:T(8,128)S(1)}, u32[]{:S(2)}, u32[]{:S(2)}) collective-permute-start(f32[1,128,128]{2,1,0:T(8,128)S(1)} %shard_map.88.refs_0_), channel_id=1, source_target_pairs={{0,8},{4,12},{8,0},{12,4},{16,24},{20,28},{24,16},{28,20},{1,9},{5... | collective-permute-start | bytes 196616 | tf_op jit(solution)/shard_map/ppermute | solution.py:188
  8.9 7.5 %collective-permute-start.7 = (f32[128,128]{1,0:T(8,128)S(1)}, f32[128,128]{1,0:T(8,128)S(1)}, u32[]{:S(2)}, u32[]{:S(2)}) collective-permute-start(f32[128,128]{1,0:T(8,128)S(1)} %get-tuple-element.13), channel_id=1, source_target_pairs={{0,1},{1,0},{2,3},{3,2},{4,5},{5,4},{6,7},{7,6},{8,9},{9,8},{10,11... | collective-permute-start | bytes 196616 | tf_op jit(solution)/shard_map/ppermute | solution.py:188
  9.0 9.0 %collective-permute-start.9 = (f32[128,128]{1,0:T(8,128)S(1)}, f32[128,128]{1,0:T(8,128)S(1)}, u32[]{:S(2)}, u32[]{:S(2)}) collective-permute-start(f32[128,128]{1,0:T(8,128)S(1)} %add.13), channel_id=1, source_target_pairs={{0,2},{1,3},{2,0},{3,1},{4,6},{5,7},{6,4},{7,5},{8,10},{9,11},{10,... | collective-permute-start | bytes 196616 | tf_op jit(solution)/shard_map/ppermute | solution.py:188
  11.2 9.3 %collective-permute-start.3 = (f32[1,128,128]{2,1,0:T(8,128)S(1)}, f32[1,128,128]{2,1,0:T(8,128)S(1)}, u32[]{:S(2)}, u32[]{:S(2)}) collective-permute-start(f32[1,128,128]{2,1,0:T(8,128)S(1)} %shard_map.88.refs_0_), channel_id=1, source_target_pairs={{0,4},{4,0},{8,12},{12,8},{16,20},{20,16},{24,28},{28,24},{1,5},{5... | collective-permute-start | bytes 196616 | tf_op jit(solution)/shard_map/ppermute | solution.py:188
  14.4 6.1 %collective-permute-start.6 = (f32[1,128,128]{2,1,0:T(8,128)S(1)}, f32[1,128,128]{2,1,0:T(8,128)S(1)}, u32[]{:S(2)}, u32[]{:S(2)}) collective-permute-start(f32[1,128,128]{2,1,0:T(8,128)S(1)} %collective-permute-done.2.refs_3_), channel_id=1, source_target_pairs={{0,4},{4,0},{8,12},{12,8},{16,20},{20,16},{24,28},{28,24},{1,5},{5... | collective-permute-start | bytes 196616 | tf_op jit(solution)/shard_map/ppermute | solution.py:188
  15.9 6.5 %collective-permute-start.5 = (f32[1,128,128]{2,1,0:T(8,128)S(1)}, f32[1,128,128]{2,1,0:T(8,128)S(1)}, u32[]{:S(2)}, u32[]{:S(2)}) collective-permute-start(f32[1,128,128]{2,1,0:T(8,128)S(1)} %collective-permute-done.1.refs_2_), channel_id=1, source_target_pairs={{0,4},{4,0},{8,12},{12,8},{16,20},{20,16},{24,28},{28,24},{1,5},{5... | collective-permute-start | bytes 196616 | tf_op jit(solution)/shard_map/ppermute | solution.py:188
  16.4 6.0 %collective-permute-start.4 = (f32[1,128,128]{2,1,0:T(8,128)S(1)}, f32[1,128,128]{2,1,0:T(8,128)S(1)}, u32[]{:S(2)}, u32[]{:S(2)}) collective-permute-start(f32[1,128,128]{2,1,0:T(8,128)S(1)} %collective-permute-done.refs_1_), channel_id=1, source_target_pairs={{0,4},{4,0},{8,12},{12,8},{16,20},{20,16},{24,28},{28,24},{1,5},{5... | collective-permute-start | bytes 196616 | tf_op jit(solution)/shard_map/ppermute | solution.py:188
  18.0 6.6 %collective-permute-start.12 = (f32[1,128,128]{2,1,0:T(8,128)S(1)}, f32[1,128,128]{2,1,0:T(8,128)S(1)}, u32[]{:S(2)}, u32[]{:S(2)}) collective-permute-start(f32[1,128,128]{2,1,0:T(8,128)S(1)} %subtract_bitcast_fusion.refs_1_), channel_id=1, source_target_pairs={{0,24},{4,28},{8,16},{12,20},{16,8},{20,12},{24,0},{28,4},{1,25},{... | collective-permute-start | bytes 196616 | tf_op jit(solution)/shard_map/ppermute | solution.py:188
  20.5 5.6 %collective-permute-start.11 = (f32[1,128,128]{2,1,0:T(8,128)S(1)}, f32[1,128,128]{2,1,0:T(8,128)S(1)}, u32[]{:S(2)}, u32[]{:S(2)}) collective-permute-start(f32[1,128,128]{2,1,0:T(8,128)S(1)} %subtract_bitcast_fusion.refs_1_), channel_id=1, source_target_pairs={{0,16},{4,20},{8,24},{12,28},{16,0},{20,4},{24,8},{28,12},{1,17},{... | collective-permute-start | bytes 196616 | tf_op jit(solution)/shard_map/ppermute | solution.py:188
  20.5 5.6 %collective-permute-start.10 = (f32[1,128,128]{2,1,0:T(8,128)S(1)}, f32[1,128,128]{2,1,0:T(8,128)S(1)}, u32[]{:S(2)}, u32[]{:S(2)}) collective-permute-start(f32[1,128,128]{2,1,0:T(8,128)S(1)} %subtract_bitcast_fusion.refs_1_), channel_id=1, source_target_pairs={{0,8},{4,12},{8,0},{12,4},{16,24},{20,28},{24,16},{28,20},{1,9},{5... | collective-permute-start | bytes 196616 | tf_op jit(solution)/shard_map/ppermute | solution.py:188
  24.4 2.8 %copy-start = (f32[1,2,128,512]{3,2,1,0:T(8,128)S(1)}, f32[1,2,128,512]{3,2,1,0:T(8,128)}, u32[]{:S(2)}) copy-start(f32[1,2,128,512]{3,2,1,0:T(8,128)} %rhs.2) | copy-start | bytes 1572868
  24.4 2.8 %copy-start.2 = (f32[1,2,128,128]{3,2,1,0:T(8,128)S(1)}, f32[1,2,128,128]{3,2,1,0:T(8,128)}, u32[]{:S(2)}) copy-start(f32[1,2,128,128]{3,2,1,0:T(8,128)} %leaf_inv.1) | copy-start | bytes 393220
  26.5 4.3 %collective-permute-start.13 = (f32[128,128]{1,0:T(8,128)S(1)}, f32[128,128]{1,0:T(8,128)S(1)}, u32[]{:S(2)}, u32[]{:S(2)}) collective-permute-start(f32[128,128]{1,0:T(8,128)S(1)} %shard_map.92), channel_id=1, source_target_pairs={{0,4},{4,0},{8,12},{12,8},{16,20},{20,16},{24,28},{28,24},{1,5},{5... | collective-permute-start | bytes 196616 | tf_op jit(solution)/shard_map/ppermute | solution.py:188

commit v5 on v4

--- a/solution.py
+++ b/solution.py
@@ -99,12 +99,16 @@
         mixed = dot(coupling[0, k] * present, leaf_inv[0, k])
         down[k] = dot(inverse[0], mixed)
     copies[4].wait()
-    for slot in reversed(range(len(slots))):
-        cols = columns_of(group ^ slot, width)
-        total = dot(down[0], rhs[0, 0, :, cols])
-        for k in range(1, count):
-            total += dot(down[k], rhs[0, k, :, cols])
-        slots[slot][...] = total
+    joined = left(jnp.concatenate([down[k] for k in range(count)], axis=1))
+    for first in reversed(range(0, len(slots), 2)):
+        pair = [columns_of(group ^ slot, width) for slot in range(first, first + 2)]
+        stacked = jnp.concatenate(
+            [jnp.concatenate([rhs[0, k, :, cols] for cols in pair], axis=1) for k in range(count)],
+            axis=0,
+        )
+        total = jnp.dot(joined, right(stacked), preferred_element_type=F32)
+        slots[first][...] = total[:, :width]
+        slots[first + 1][...] = total[:, width:]
 
 
 def section_map(inverse, link, order_only, out):
@@ -127,14 +131,16 @@
     parts, (held, maps) = refs[:-2], refs[-2:]
     sections, both, order = held.shape
     me = lax.axis_index("leaf")
-    size = parts[0].shape[0]
-    half = len(parts) // 2
-
-    @pl.loop(0, size, unroll=size <= 8)
-    def _(i):
-        for p in range(half):
-            maps[2 * (p * size + i) ^ me] = parts[p][i]
-            maps[2 * (p * size + i) ^ 1 ^ me] = parts[half + p][i]
+    at = 0
+    for part in parts:
+        size, begun = part.shape[0], at
+
+        @pl.loop(0, size, unroll=size <= 8)
+        def _(i):
+            spot = i + begun
+            maps[(2 * spot if begun < sections // 2 else 2 * spot + 1 - sections) ^ me] = part[i]
+
+        at += size
 
     line = lax.broadcasted_iota(jnp.int32, (both, order), 0)
     column = lax.broadcasted_iota(jnp.int32, (both, order), 1)
@@ -153,8 +159,8 @@
         held[section] += dot3(held[section + 1], maps[section + 1])
 
 
-def apply_rows(which, *refs):
-    held, parts, out = refs[0], refs[1:-1], refs[-1]
+def apply_rows(which, held, order_only, *refs):
+    parts, out = refs[:-1], refs[-1]
     order = held.shape[2]
     rows = slice(which * order, (which + 1) * order)
     me = lax.axis_index("leaf")
@@ -167,18 +173,39 @@
     out[...] = total
 
 
-def finish(base, factors, inverse, spread, leaves, solved, pieces, sems):
-    groups, count, order, width = pieces.shape
-    copies = []
-    for j in range(groups):
-        cols = slice(j * width, (j + 1) * width)
-        taken = jnp.dot(factors[...], right(spread[j]), preferred_element_type=F32)
-        for k in range(count):
-            pieces[j, k] = base[k, :, cols] - taken[k * order : (k + 1) * order]
-        copy = pltpu.make_async_copy(pieces.at[j], leaves.at[0, :, :, cols], sems.at[j])
+def leaf_blocks(slots, base, factors, spread, out):
+    count, order = base.shape[:2]
+    width = spread.shape[2]
+    for first in range(0, len(slots), 2):
+        ready = range(first, min(first + 2, len(slots)))
+        stacked = jnp.concatenate([spread[i] for i in ready], axis=1)
+        taken = jnp.dot(factors[...], right(stacked), preferred_element_type=F32)
+        for i in ready:
+            cols = columns_of(lax.axis_index("grp") ^ slots[i], width)
+            near = slice((i - first) * width, (i - first + 1) * width)
+            for k in range(count):
+                out[i, k] = base[k, :, cols] - taken[k * order : (k + 1) * order, near]
+
+
+def early_blocks(slots, base, factors, inverse, spread, out, solved):
+    leaf_blocks(slots, base, factors, spread, out)
+    solved[0] = dot_ta(inverse[0], spread[0])
+
+
+def late_blocks(early, late, base, factors, spread, done, leaves, fresh, sems):
+    width = spread.shape[2]
+
+    def put(i, slot, source):
+        target = leaves.at[0, :, :, columns_of(lax.axis_index("grp") ^ slot, width)]
+        return pltpu.make_async_copy(source, target, sems.at[i])
+
+    copies = [put(i, slot, done.at[i]) for i, slot in enumerate(early)]
+    for copy in copies:
         copy.start()
-        copies.append(copy)
-    solved[0] = dot_ta(inverse[0], spread[lax.axis_index("grp")])
+    leaf_blocks(late, base, factors, spread, fresh)
+    for i, slot in enumerate(late):
+        copies.append(put(len(early) + i, slot, fresh.at[i]))
+        copies[-1].start()
     for copy in copies:
         copy.wait()
 
@@ -231,7 +258,10 @@
         slots = {0: slots[0] + swap(slots[bit], "grp", bit), **ahead}
         bit *= 2
     maps = gather_pairs(step)
-    others = [swap(part, "leaf", 1) for part in maps]
+    middle = len(maps) // 2
+    others = [
+        swap(jnp.concatenate(pair, axis=0), "leaf", 1) for pair in (maps[:middle], maps[middle:]) if pair
+    ]
     offset = own - slots[0]
     offsets = gather_pairs(offset[None])
     rows = call(
@@ -246,22 +276,36 @@
         (groups + 1) * count * cube, 3 * leaf_rhs.size * 4, leaf_rhs, leaf_inv, down,
     )
 
-    def applied(which):
+    def applied(which, order_only):
         return call(
             lambda *refs: apply_rows(which, *refs), block, sections // 2 * cube,
-            sections * block_bytes, rows, *offsets,
+            sections * block_bytes, rows, order_only, *offsets,
         )
 
-    theirs = swap(applied(1), "leaf", 1)
-    carried = applied(0) + theirs
-    spread = lax.all_gather(carried, "grp")
-    return call(
-        finish, (shaped(1, count, order, columns), shaped(1, order, width)),
-        (4 * count + 1) * cube, 3 * leaf_rhs.size * 4,
-        base, factors, sep_inv, spread,
-        held=[pltpu.VMEM((groups, count, order, width), F32), pltpu.SemaphoreType.DMA((groups,))],
-        out_specs=(HBM, VMEM),
-    )
+    theirs = swap(applied(1, down), "leaf", 1)
+    carried = applied(0, factors) + theirs
+    spread, slots, bit = carried[None], [0], groups // 2
+    while bit > 1:
+        spread = jnp.concatenate([spread, swap(spread, "grp", bit)], axis=0)
+        slots = slots + [slot ^ bit for slot in slots]
+        bit //= 2
+    late = [slot ^ 1 for slot in slots]
+    arrived = swap(spread, "grp", 1)
+    done, solved = call(
+        lambda *refs: early_blocks(slots, *refs),
+        (shaped(len(slots), count, order, width), shaped(1, order, width)),
+        (len(slots) * count + 1) * cube, 4 * leaf_rhs.size, base, factors, sep_inv, spread,
+    )
+    leaves = call(
+        lambda *refs: late_blocks(slots, late, *refs), shaped(1, count, order, columns),
+        len(late) * count * cube, 8 * leaf_rhs.size, base, factors, arrived, done,
+        held=[
+            pltpu.VMEM((len(late), count, order, width), F32),
+            pltpu.SemaphoreType.DMA((groups,)),
+        ],
+        out_specs=HBM,
+    )
+    return leaves, solved
 
 
 def solution(mesh):

time: 38.5 us -> 36.5 us (0.948)
  blocking collectives: 5.79 us -> 0 us
  waiting for transfers between devices: 5.97 us -> 10.6 us
  starting transfers between devices: 17.7 us -> 16.9 us
    all_gather x1 -> x0, blocking collectives: 5.79 us -> none  [shards(): spread = lax.all_gather(carried, 'grp')]
    ppermute x14, waiting for transfers between devices: 5.97 us -> 10.6 us  [swap(): return lax.ppermute(value, axis, [(i, i ^ bit) for i in range(count)])]
    ppermute x14, starting transfers between devices: 17.7 us -> 16.9 us  [swap(): return lax.ppermute(value, axis, [(i, i ^ bit) for i in range(count)])]
    pallas_call x8 -> x9, Pallas kernels: 8.07 us -> 8 us  [call(): pl.pallas_call(body, out_shape=outs, in_specs=[HBM] * far + [VMEM] * (len...]
  transfers between devices with their start and end apart: 14 -> 14, of which waited for: 5 -> 7; matrix products, arithmetic and copies ran while one was open for 0% -> 0% of each run, Pallas kernels for 10% -> 13%
where the time goes in v5:
time: 36.5 us; the launch traced here: 36.3 us
  starting transfers between devices  16.9 us (46%)
  waiting for transfers between devices  10.6 us (29%)
  Pallas kernels  8 us (22%)
  between operations  0.79 us (2%)
    ppermute x14, starting transfers between devices, swap(): return lax.ppermute(value, axis, [(i, i ^ bit) for i in range(count)])  16.9 us
    ppermute x14, waiting for transfers between devices, swap(): return lax.ppermute(value, axis, [(i, i ^ bit) for i in range(count)])  10.6 us
    pallas_call x9, Pallas kernels, call(): pl.pallas_call(body, out_shape=outs, in_specs=[HBM] * far + [VMEM] * (len...  8 us
  transfers between devices with their start and end apart: 14, of which 7 were waited for; matrix products, arithmetic and copies ran while one was open for 0% of the time, Pallas kernels for 13%

profile of v5, /device:TPU:0, one launch (start us, length us, event | category | flops | bytes accessed | tf_op | source)
XLA Modules:
  0.0 36.3 jit_solution(3174619002915355327)
XLA Ops:
  0.7 2.0 %shard_map.86 = (f32[2,128,128]{2,1,0:T(8,128)S(1)}, f32[128,128]{1,0:T(8,128)S(1)}, f32[128,128]{1,0:T(8,128)S(1)}, f32[128,128]{1,0:T(8,128)S(1)}, f32[128,128]{1,0:T(8,128)S(1)}) custom-call(f32[1,128,128]{2,1,0:T(8,128)} %refs_2_.3, s32[1,2]{1,0:T(1,128)} %refs_1_.1, f32[1,2,128,128]{3,2,1,0:T(8,128)} %leaf_inv.1, f32[1,2,128,128]{3,2,1,0:T(8,128)} %refs_3_.1, ...), custom_call_target="tpu_custom_call" | custom-call | flops 50331648 | bytes 1048576 | tf_op jit(solution)/shard_map/pallas_call | solution.py:56
  2.6 0.5 %collective-permute-start.6 = (f32[128,128]{1,0:T(8,128)S(1)}, f32[128,128]{1,0:T(8,128)S(1)}, u32[]{:S(2)}, u32[]{:S(2)}) collective-permute-start(f32[128,128]{1,0:T(8,128)S(1)} %get-tuple-element.17), channel_id=1, source_target_pairs={{0,1},{1,0},{2,3},{3,2},{4,5},{5,4},{6,7},{7,6},{8,9},{9,8},{10,11... | collective-permute-start | bytes 196616 | tf_op jit(solution)/shard_map/ppermute | solution.py:215
  3.4 4.7 %collective-permute-start.2 = (f32[1,128,128]{2,1,0:T(8,128)S(1)}, f32[1,128,128]{2,1,0:T(8,128)S(1)}, u32[]{:S(2)}, u32[]{:S(2)}) collective-permute-start(f32[1,128,128]{2,1,0:T(8,128)S(1)} %shard_map.88.refs_0_), channel_id=1, source_target_pairs={{0,24},{4,28},{8,16},{12,20},{16,8},{20,12},{24,0},{28,4},{1,25},{... | collective-permute-start | bytes 196616 | tf_op jit(solution)/shard_map/ppermute | solution.py:215
  8.1 0.6 %collective-permute-start = (f32[1,128,128]{2,1,0:T(8,128)S(1)}, f32[1,128,128]{2,1,0:T(8,128)S(1)}, u32[]{:S(2)}, u32[]{:S(2)}) collective-permute-start(f32[1,128,128]{2,1,0:T(8,128)S(1)} %shard_map.88.refs_0_), channel_id=1, source_target_pairs={{0,8},{4,12},{8,0},{12,4},{16,24},{20,28},{24,16},{28,20},{1,9},{5... | collective-permute-start | bytes 196616 | tf_op jit(solution)/shard_map/ppermute | solution.py:215
  9.0 1.7 %collective-permute-start.7 = (f32[128,128]{1,0:T(8,128)S(1)}, f32[128,128]{1,0:T(8,128)S(1)}, u32[]{:S(2)}, u32[]{:S(2)}) collective-permute-start(f32[128,128]{1,0:T(8,128)S(1)} %add.13), channel_id=1, source_target_pairs={{0,2},{1,3},{2,0},{3,1},{4,6},{5,7},{6,4},{7,5},{8,10},{9,11},{10,... | collective-permute-start | bytes 196616 | tf_op jit(solution)/shard_map/ppermute | solution.py:215
  10.7 0.3 collective-permute-done.2.refs_3_
  11.0 3.2 %collective-permute-done.1.refs_2_ = f32[1,128,128]{2,1,0:T(8,128)S(1)} collective-permute-done((f32[1,128,128]{2,1,0:T(8,128)S(1)}, f32[1,128,128]{2,1,0:T(8,128)S(1)}, u32[]{:S(2)}, u32[]{:S(2)}) %collective-permute-start.1) | collective-permute-done | bytes 65568 | tf_op jit(solution)/shard_map/ppermute | solution.py:215
  14.2 1.6 %collective-permute-start.4 = (f32[2,128,128]{2,1,0:T(8,128)S(1)}, f32[2,128,128]{2,1,0:T(8,128)S(1)}, u32[]{:S(2)}, u32[]{:S(2)}) collective-permute-start(f32[2,128,128]{2,1,0:T(8,128)S(1)} %pad_maximum_fusion.1), channel_id=1, source_target_pairs={{0,4},{4,0},{8,12},{12,8},{16,20},{20,16},{24,28},{28,24},{1,5},{5... | collective-permute-start | bytes 393224 | tf_op jit(solution)/shard_map/ppermute | solution.py:215
  15.8 0.6 %collective-permute-start.3 = (f32[2,128,128]{2,1,0:T(8,128)S(1)}, f32[2,128,128]{2,1,0:T(8,128)S(1)}, u32[]{:S(2)}, u32[]{:S(2)}) collective-permute-start(f32[2,128,128]{2,1,0:T(8,128)S(1)} %pad_maximum_fusion), channel_id=1, source_target_pairs={{0,4},{4,0},{8,12},{12,8},{16,20},{20,16},{24,28},{28,24},{1,5},{5... | collective-permute-start | bytes 393224 | tf_op jit(solution)/shard_map/ppermute | solution.py:215
  16.4 2.5 %collective-permute-start.10 = (f32[1,128,128]{2,1,0:T(8,128)S(1)}, f32[1,128,128]{2,1,0:T(8,128)S(1)}, u32[]{:S(2)}, u32[]{:S(2)}) collective-permute-start(f32[1,128,128]{2,1,0:T(8,128)S(1)} %subtract_bitcast_fusion.refs_2_), channel_id=1, source_target_pairs={{0,24},{4,28},{8,16},{12,20},{16,8},{20,12},{24,0},{28,4},{1,25},{... | collective-permute-start | bytes 196616 | tf_op jit(solution)/shard_map/ppermute | solution.py:215
  18.9 1.9 %collective-permute-start.8 = (f32[1,128,128]{2,1,0:T(8,128)S(1)}, f32[1,128,128]{2,1,0:T(8,128)S(1)}, u32[]{:S(2)}, u32[]{:S(2)}) collective-permute-start(f32[1,128,128]{2,1,0:T(8,128)S(1)} %subtract_bitcast_fusion.refs_2_), channel_id=1, source_target_pairs={{0,8},{4,12},{8,0},{12,4},{16,24},{20,28},{24,16},{28,20},{1,9},{5... | collective-permute-start | bytes 196616 | tf_op jit(solution)/shard_map/ppermute | solution.py:215
  20.8 1.3 %collective-permute-done.3.refs_4_ = f32[2,128,128]{2,1,0:T(8,128)S(1)} collective-permute-done((f32[2,128,128]{2,1,0:T(8,128)S(1)}, f32[2,128,128]{2,1,0:T(8,128)S(1)}, u32[]{:S(2)}, u32[]{:S(2)}) %collective-permute-start.3) | collective-permute-done | bytes 131104 | tf_op jit(solution)/shard_map/ppermute | solution.py:215
  22.2 1.9 %shard_map.89.refs_0_ = f32[8,256,128]{2,1,0:T(8,128)S(1)} custom-call(f32[1,128,128]{2,1,0:T(8,128)S(1)} %shard_map.88.refs_0_, f32[1,128,128]{2,1,0:T(8,128)S(1)} %collective-permute-done.refs_1_, f32[1,128,128]{2,1,0:T(8,128)S(1)} %collective-permute-done.1.refs_2_, f32[1,128,128]{2,1,0:T(8,128)S(1)} %collective-permute-done.2.refs_3_, ...), custom_call_target="tpu_custom_call" | custom-call | flops 134217728 | bytes 2097152 | tf_op jit(solution)/shard_map/pallas_call | solution.py:56
  24.1 0.8 %collective-permute-done.9.refs_4_ = f32[1,128,128]{2,1,0:T(8,128)S(1)} collective-permute-done((f32[1,128,128]{2,1,0:T(8,128)S(1)}, f32[1,128,128]{2,1,0:T(8,128)S(1)}, u32[]{:S(2)}, u32[]{:S(2)}) %collective-permute-start.9) | collective-permute-done | bytes 65568 | tf_op jit(solution)/shard_map/ppermute | solution.py:215
  24.9 0.4 %shard_map.92 = f32[128,128]{1,0:T(8,128)S(1)} custom-call(f32[8,256,128]{2,1,0:T(8,128)S(1)} %shard_map.89.refs_0_, f32[2,128,128]{2,1,0:T(8,128)S(1)} %get-tuple-element.11.down.order_only.refs_1_, f32[1,128,128]{2,1,0:T(8,128)S(1)} %subtract_bitcast_fusion.refs_2_, f32[1,128,128]{2,1,0:T(8,128)S(1)} %collective-permute-done.8.refs_3_, ...), custom_call_target="tpu_custom_call" | custom-call | flops 16777216 | bytes 524288 | tf_op jit(solution)/shard_map/pallas_call | solution.py:56
  25.3 1.1 %collective-permute-start.11 = (f32[128,128]{1,0:T(8,128)S(1)}, f32[128,128]{1,0:T(8,128)S(1)}, u32[]{:S(2)}, u32[]{:S(2)}) collective-permute-start(f32[128,128]{1,0:T(8,128)S(1)} %shard_map.92), channel_id=1, source_target_pairs={{0,4},{4,0},{8,12},{12,8},{16,20},{20,16},{24,28},{28,24},{1,5},{5... | collective-permute-start | bytes 196616 | tf_op jit(solution)/shard_map/ppermute | solution.py:215
  26.4 1.1 %shard_map.87 = (f32[2,128,512]{2,1,0:T(8,128)S(1)}, bf16[256,384]{1,0:T(8,128)(2,1)S(1)}) custom-call(f32[1,2,128,512]{3,2,1,0:T(8,128)S(1)} %copy-done, f32[1,2,128,128]{3,2,1,0:T(8,128)S(1)} %copy-done.2, f32[2,128,128]{2,1,0:T(8,128)S(1)} %get-tuple-element.11.down.order_only.refs_1_), custom_call_target="tpu_custom_call" | custom-call | flops 41943040 | bytes 1572864 | tf_op jit(solution)/shard_map/pallas_call | solution.py:56
  27.4 0.4 %shard_map.91 = f32[128,128]{1,0:T(8,128)S(1)} custom-call(f32[8,256,128]{2,1,0:T(8,128)S(1)} %shard_map.89.refs_0_, bf16[256,384]{1,0:T(8,128)(2,1)S(1)} %get-tuple-element.13.refs_1_, f32[1,128,128]{2,1,0:T(8,128)S(1)} %subtract_bitcast_fusion.refs_2_, f32[1,128,128]{2,1,0:T(8,128)S(1)} %collective-permute-done.8.refs_3_, ...), custom_call_target="tpu_custom_call" | custom-call | flops 16777216 | bytes 524288 | tf_op jit(solution)/shard_map/pallas_call | solution.py:56
  27.8 1.8 %collective-permute-done.11 = f32[128,128]{1,0:T(8,128)S(1)} collective-permute-done((f32[128,128]{1,0:T(8,128)S(1)}, f32[128,128]{1,0:T(8,128)S(1)}, u32[]{:S(2)}, u32[]{:S(2)}) %collective-permute-start.11) | collective-permute-done | bytes 65568 | tf_op jit(solution)/shard_map/ppermute | solution.py:215
  29.6 1.6 %collective-permute-start.12 = (f32[1,128,128]{2,1,0:T(8,128)S(1)}, f32[1,128,128]{2,1,0:T(8,128)S(1)}, u32[]{:S(2)}, u32[]{:S(2)}) collective-permute-start(f32[1,128,128]{2,1,0:T(8,128)S(1)} %add_bitcast_fusion), channel_id=1, source_target_pairs={{0,2},{1,3},{2,0},{3,1},{4,6},{5,7},{6,4},{7,5},{8,10},{9,11},{10,... | collective-permute-start | bytes 196616 | tf_op jit(solution)/shard_map/ppermute | solution.py:215
  31.2 2.8 %collective-permute-done.12 = f32[1,128,128]{2,1,0:T(8,128)S(1)} collective-permute-done((f32[1,128,128]{2,1,0:T(8,128)S(1)}, f32[1,128,128]{2,1,0:T(8,128)S(1)}, u32[]{:S(2)}, u32[]{:S(2)}) %collective-permute-start.12) | collective-permute-done | bytes 65568 | tf_op jit(solution)/shard_map/ppermute | solution.py:215
  34.0 0.9 %shard_map.93 = (f32[2,2,128,128]{3,2,1,0:T(8,128)S(1)}, f32[1,128,128]{2,1,0:T(8,128)}) custom-call(f32[2,128,512]{2,1,0:T(8,128)S(1)} %get-tuple-element.12.refs_0_, bf16[256,384]{1,0:T(8,128)(2,1)S(1)} %get-tuple-element.13.refs_1_, f32[1,128,128]{2,1,0:T(8,128)S(1)} %copy-done.1, f32[2,128,128]{2,1,0:T(8,128)S(1)} %pad_maximum_fusion.2.refs_3_), custom_call_target="tpu_custom_call" | custom-call | flops 20971520 | bytes 524288 | tf_op jit(solution)/shard_map/pallas_call | solution.py:56
  35.0 0.4 %collective-permute-done.13.refs_2_ = f32[2,128,128]{2,1,0:T(8,128)S(1)} collective-permute-done((f32[2,128,128]{2,1,0:T(8,128)S(1)}, f32[2,128,128]{2,1,0:T(8,128)S(1)}, u32[]{:S(2)}, u32[]{:S(2)}) %collective-permute-start.13) | collective-permute-done | bytes 131104 | tf_op jit(solution)/shard_map/ppermute | solution.py:215
  35.4 1.0 %shard_map.94 = f32[1,2,128,512]{3,2,1,0:T(8,128)} custom-call(f32[2,128,512]{2,1,0:T(8,128)S(1)} %get-tuple-element.12.refs_0_, bf16[256,384]{1,0:T(8,128)(2,1)S(1)} %get-tuple-element.13.refs_1_, f32[2,128,128]{2,1,0:T(8,128)S(1)} %collective-permute-done.13.refs_2_, f32[2,2,128,128]{3,2,1,0:T(8,128)S(1)} %get-tuple-element.18.refs_3_), custom_call_target="tpu_custom_call" | custom-call | flops 16777216 | bytes 1048576 | tf_op jit(solution)/shard_map/pallas_call | solution.py:56
  (29 shorter events, 0.6 us)
Async XLA Ops:
  0.6 2.5 %copy-start.1 = (f32[1,128,128]{2,1,0:T(8,128)S(1)}, f32[1,128,128]{2,1,0:T(8,128)}, u32[]{:S(2)}) copy-start(f32[1,128,128]{2,1,0:T(8,128)} %refs_2_.3) | copy-start | bytes 196612
  0.6 2.5 %copy-start.4 = (f32[1,128,128]{2,1,0:T(8,128)S(1)}, f32[1,128,128]{2,1,0:T(8,128)}, u32[]{:S(2)}) copy-start(f32[1,128,128]{2,1,0:T(8,128)} %link.1) | copy-start | bytes 196612
  2.6 6.1 %copy-start.3 = (f32[1,128,512]{2,1,0:T(8,128)S(1)}, f32[1,128,512]{2,1,0:T(8,128)}, u32[]{:S(2)}) copy-start(f32[1,128,512]{2,1,0:T(8,128)} %rhs.3) | copy-start | bytes 786436
  2.6 6.3 %collective-permute-start.6 = (f32[128,128]{1,0:T(8,128)S(1)}, f32[128,128]{1,0:T(8,128)S(1)}, u32[]{:S(2)}, u32[]{:S(2)}) collective-permute-start(f32[128,128]{1,0:T(8,128)S(1)} %get-tuple-element.17), channel_id=1, source_target_pairs={{0,1},{1,0},{2,3},{3,2},{4,5},{5,4},{6,7},{7,6},{8,9},{9,8},{10,11... | collective-permute-start | bytes 196616 | tf_op jit(solution)/shard_map/ppermute | solution.py:215
  3.4 7.6 %collective-permute-start.2 = (f32[1,128,128]{2,1,0:T(8,128)S(1)}, f32[1,128,128]{2,1,0:T(8,128)S(1)}, u32[]{:S(2)}, u32[]{:S(2)}) collective-permute-start(f32[1,128,128]{2,1,0:T(8,128)S(1)} %shard_map.88.refs_0_), channel_id=1, source_target_pairs={{0,24},{4,28},{8,16},{12,20},{16,8},{20,12},{24,0},{28,4},{1,25},{... | collective-permute-start | bytes 196616 | tf_op jit(solution)/shard_map/ppermute | solution.py:215
  8.1 6.1 %collective-permute-start.1 = (f32[1,128,128]{2,1,0:T(8,128)S(1)}, f32[1,128,128]{2,1,0:T(8,128)S(1)}, u32[]{:S(2)}, u32[]{:S(2)}) collective-permute-start(f32[1,128,128]{2,1,0:T(8,128)S(1)} %shard_map.88.refs_0_), channel_id=1, source_target_pairs={{0,16},{4,20},{8,24},{12,28},{16,0},{20,4},{24,8},{28,12},{1,17},{... | collective-permute-start | bytes 196616 | tf_op jit(solution)/shard_map/ppermute | solution.py:215
  8.1 7.7 %collective-permute-start = (f32[1,128,128]{2,1,0:T(8,128)S(1)}, f32[1,128,128]{2,1,0:T(8,128)S(1)}, u32[]{:S(2)}, u32[]{:S(2)}) collective-permute-start(f32[1,128,128]{2,1,0:T(8,128)S(1)} %shard_map.88.refs_0_), channel_id=1, source_target_pairs={{0,8},{4,12},{8,0},{12,4},{16,24},{20,28},{24,16},{28,20},{1,9},{5... | collective-permute-start | bytes 196616 | tf_op jit(solution)/shard_map/ppermute | solution.py:215
  8.7 7.7 %collective-permute-start.5 = (f32[128,128]{1,0:T(8,128)S(1)}, f32[128,128]{1,0:T(8,128)S(1)}, u32[]{:S(2)}, u32[]{:S(2)}) collective-permute-start(f32[128,128]{1,0:T(8,128)S(1)} %get-tuple-element.15), channel_id=1, source_target_pairs={{0,1},{1,0},{2,3},{3,2},{4,5},{5,4},{6,7},{7,6},{8,9},{9,8},{10,11... | collective-permute-start | bytes 196616 | tf_op jit(solution)/shard_map/ppermute | solution.py:215
  9.0 7.4 %collective-permute-start.7 = (f32[128,128]{1,0:T(8,128)S(1)}, f32[128,128]{1,0:T(8,128)S(1)}, u32[]{:S(2)}, u32[]{:S(2)}) collective-permute-start(f32[128,128]{1,0:T(8,128)S(1)} %add.13), channel_id=1, source_target_pairs={{0,2},{1,3},{2,0},{3,1},{4,6},{5,7},{6,4},{7,5},{8,10},{9,11},{10,... | collective-permute-start | bytes 196616 | tf_op jit(solution)/shard_map/ppermute | solution.py:215
  14.2 6.7 %collective-permute-start.4 = (f32[2,128,128]{2,1,0:T(8,128)S(1)}, f32[2,128,128]{2,1,0:T(8,128)S(1)}, u32[]{:S(2)}, u32[]{:S(2)}) collective-permute-start(f32[2,128,128]{2,1,0:T(8,128)S(1)} %pad_maximum_fusion.1), channel_id=1, source_target_pairs={{0,4},{4,0},{8,12},{12,8},{16,20},{20,16},{24,28},{28,24},{1,5},{5... | collective-permute-start | bytes 393224 | tf_op jit(solution)/shard_map/ppermute | solution.py:215
  15.8 6.4 %collective-permute-start.3 = (f32[2,128,128]{2,1,0:T(8,128)S(1)}, f32[2,128,128]{2,1,0:T(8,128)S(1)}, u32[]{:S(2)}, u32[]{:S(2)}) collective-permute-start(f32[2,128,128]{2,1,0:T(8,128)S(1)} %pad_maximum_fusion), channel_id=1, source_target_pairs={{0,4},{4,0},{8,12},{12,8},{16,20},{20,16},{24,28},{28,24},{1,5},{5... | collective-permute-start | bytes 393224 | tf_op jit(solution)/shard_map/ppermute | solution.py:215
  16.4 7.7 %collective-permute-start.10 = (f32[1,128,128]{2,1,0:T(8,128)S(1)}, f32[1,128,128]{2,1,0:T(8,128)S(1)}, u32[]{:S(2)}, u32[]{:S(2)}) collective-permute-start(f32[1,128,128]{2,1,0:T(8,128)S(1)} %subtract_bitcast_fusion.refs_2_), channel_id=1, source_target_pairs={{0,24},{4,28},{8,16},{12,20},{16,8},{20,12},{24,0},{28,4},{1,25},{... | collective-permute-start | bytes 196616 | tf_op jit(solution)/shard_map/ppermute | solution.py:215
  18.9 6.0 %collective-permute-start.9 = (f32[1,128,128]{2,1,0:T(8,128)S(1)}, f32[1,128,128]{2,1,0:T(8,128)S(1)}, u32[]{:S(2)}, u32[]{:S(2)}) collective-permute-start(f32[1,128,128]{2,1,0:T(8,128)S(1)} %subtract_bitcast_fusion.refs_2_), channel_id=1, source_target_pairs={{0,16},{4,20},{8,24},{12,28},{16,0},{20,4},{24,8},{28,12},{1,17},{... | collective-permute-start | bytes 196616 | tf_op jit(solution)/shard_map/ppermute | solution.py:215
  18.9 6.0 %collective-permute-start.8 = (f32[1,128,128]{2,1,0:T(8,128)S(1)}, f32[1,128,128]{2,1,0:T(8,128)S(1)}, u32[]{:S(2)}, u32[]{:S(2)}) collective-permute-start(f32[1,128,128]{2,1,0:T(8,128)S(1)} %subtract_bitcast_fusion.refs_2_), channel_id=1, source_target_pairs={{0,8},{4,12},{8,0},{12,4},{16,24},{20,28},{24,16},{28,20},{1,9},{5... | collective-permute-start | bytes 196616 | tf_op jit(solution)/shard_map/ppermute | solution.py:215
  24.1 2.3 %copy-start = (f32[1,2,128,512]{3,2,1,0:T(8,128)S(1)}, f32[1,2,128,512]{3,2,1,0:T(8,128)}, u32[]{:S(2)}) copy-start(f32[1,2,128,512]{3,2,1,0:T(8,128)} %rhs.2) | copy-start | bytes 1572868
  24.1 2.3 %copy-start.2 = (f32[1,2,128,128]{3,2,1,0:T(8,128)S(1)}, f32[1,2,128,128]{3,2,1,0:T(8,128)}, u32[]{:S(2)}) copy-start(f32[1,2,128,128]{3,2,1,0:T(8,128)} %leaf_inv.1) | copy-start | bytes 393220
  25.3 4.3 %collective-permute-start.11 = (f32[128,128]{1,0:T(8,128)S(1)}, f32[128,128]{1,0:T(8,128)S(1)}, u32[]{:S(2)}, u32[]{:S(2)}) collective-permute-start(f32[128,128]{1,0:T(8,128)S(1)} %shard_map.92), channel_id=1, source_target_pairs={{0,4},{4,0},{8,12},{12,8},{16,20},{20,16},{24,28},{28,24},{1,5},{5... | collective-permute-start | bytes 196616 | tf_op jit(solution)/shard_map/ppermute | solution.py:215
  29.6 4.3 %collective-permute-start.12 = (f32[1,128,128]{2,1,0:T(8,128)S(1)}, f32[1,128,128]{2,1,0:T(8,128)S(1)}, u32[]{:S(2)}, u32[]{:S(2)}) collective-permute-start(f32[1,128,128]{2,1,0:T(8,128)S(1)} %add_bitcast_fusion), channel_id=1, source_target_pairs={{0,2},{1,3},{2,0},{3,1},{4,6},{5,7},{6,4},{7,5},{8,10},{9,11},{10,... | collective-permute-start | bytes 196616 | tf_op jit(solution)/shard_map/ppermute | solution.py:215
  34.0 1.4 %collective-permute-start.13 = (f32[2,128,128]{2,1,0:T(8,128)S(1)}, f32[2,128,128]{2,1,0:T(8,128)S(1)}, u32[]{:S(2)}, u32[]{:S(2)}) collective-permute-start(f32[2,128,128]{2,1,0:T(8,128)S(1)} %pad_maximum_fusion.2.refs_3_), channel_id=1, source_target_pairs={{0,1},{1,0},{2,3},{3,2},{4,5},{5,4},{6,7},{7,6},{8,9},{9,8},{10,11... | collective-permute-start | bytes 393224 | tf_op jit(solution)/shard_map/ppermute | solution.py:215

commit v6 on v5

--- a/solution.py
+++ b/solution.py
@@ -96,8 +96,8 @@
         copy.wait()
     for k in range(count):
         present = pattern[0, k].astype(F32)
-        mixed = dot(coupling[0, k] * present, leaf_inv[0, k])
-        down[k] = dot(inverse[0], mixed)
+        mixed = dot3(coupling[0, k] * present, leaf_inv[0, k])
+        down[k] = dot3(inverse[0], mixed)
     copies[4].wait()
     joined = left(jnp.concatenate([down[k] for k in range(count)], axis=1))
     for first in reversed(range(0, len(slots), 2)):
@@ -234,21 +234,21 @@
     cube = 2 * order**3
     block = shaped(order, width)
     block_bytes = order * width * 4
+    placed = (40 * sections * cube, 60 << 20)
 
     first = (sep_inv, pattern, leaf_inv, coupling, leaf_rhs)
     down, *slots = call(
         begin,
         (shaped(count, order, order),) + (block,) * groups,
-        (2 * count + groups * count) * cube,
-        2 * leaf_rhs.size * 4,
+        *placed,
         *first, held=landing(*first), far=5,
     )
     step = call(
-        section_map, shaped(1, order, order), cube, 3 * block_bytes,
+        section_map, shaped(1, order, order), *placed,
         sep_inv, chain_link, down,
     )
     slots = dict(enumerate(slots))
-    own = call(own_columns, block, cube, 3 * block_bytes, sep_rhs, sep_inv)
+    own = call(own_columns, block, *placed, sep_rhs, sep_inv)
     bit = 1
     while bit < groups:
         ahead = {
@@ -258,9 +258,8 @@
         slots = {0: slots[0] + swap(slots[bit], "grp", bit), **ahead}
         bit *= 2
     maps = gather_pairs(step)
-    middle = len(maps) // 2
     others = [
-        swap(jnp.concatenate(pair, axis=0), "leaf", 1) for pair in (maps[:middle], maps[middle:]) if pair
+        swap(jnp.concatenate(pair, axis=0), "leaf", 1) for pair in (maps[:-1], maps[-1:]) if pair
     ]
     offset = own - slots[0]
     offsets = gather_pairs(offset[None])
@@ -278,8 +277,7 @@
 
     def applied(which, order_only):
         return call(
-            lambda *refs: apply_rows(which, *refs), block, sections // 2 * cube,
-            sections * block_bytes, rows, order_only, *offsets,
+            lambda *refs: apply_rows(which, *refs), block, *placed, rows, order_only, *offsets,
         )
 
     theirs = swap(applied(1, down), "leaf", 1)

time: 36.5 us -> 35.8 us (0.981)
  waiting for transfers between devices: 10.6 us -> 8.83 us
  starting transfers between devices: 16.9 us -> 18 us
    ppermute x14, waiting for transfers between devices: 10.6 us -> 8.83 us  [swap(): return lax.ppermute(value, axis, [(i, i ^ bit) for i in range(count)])]
    ppermute x14, starting transfers between devices: 16.9 us -> 18 us  [swap(): return lax.ppermute(value, axis, [(i, i ^ bit) for i in range(count)])]
where the time goes in v6:
time: 35.8 us; the launch traced here: 35.7 us
  starting transfers between devices  18 us (50%)
  waiting for transfers between devices  8.83 us (25%)
  Pallas kernels  7.98 us (22%)
  between operations  0.79 us (2%)
    ppermute x14, starting transfers between devices, swap(): return lax.ppermute(value, axis, [(i, i ^ bit) for i in range(count)])  18 us
    ppermute x14, waiting for transfers between devices, swap(): return lax.ppermute(value, axis, [(i, i ^ bit) for i in range(count)])  8.83 us
    pallas_call x9, Pallas kernels, call(): pl.pallas_call(body, out_shape=outs, in_specs=[HBM] * far + [VMEM] * (len...  7.98 us
  transfers between devices with their start and end apart: 14, of which 7 were waited for; matrix products, arithmetic and copies ran while one was open for 0% of the time, Pallas kernels for 13%

profile of v6, /device:TPU:0, one launch (start us, length us, event | category | flops | bytes accessed | tf_op | source)
XLA Modules:
  0.0 35.7 jit_solution(16697744690522717995)
XLA Ops:
  0.7 2.0 %shard_map.86 = (f32[2,128,128]{2,1,0:T(8,128)S(1)}, f32[128,128]{1,0:T(8,128)S(1)}, f32[128,128]{1,0:T(8,128)S(1)}, f32[128,128]{1,0:T(8,128)S(1)}, f32[128,128]{1,0:T(8,128)S(1)}) custom-call(f32[1,128,128]{2,1,0:T(8,128)} %refs_2_.3, s32[1,2]{1,0:T(1,128)} %refs_1_.1, f32[1,2,128,128]{3,2,1,0:T(8,128)} %leaf_inv.1, f32[1,2,128,128]{3,2,1,0:T(8,128)} %refs_3_.1, ...), custom_call_target="tpu_custom_call" | custom-call | flops 1342177280 | bytes 62914560 | tf_op jit(solution)/shard_map/pallas_call | solution.py:56
  2.9 5.1 %collective-permute-start.2 = (f32[1,128,128]{2,1,0:T(8,128)S(1)}, f32[1,128,128]{2,1,0:T(8,128)S(1)}, u32[]{:S(2)}, u32[]{:S(2)}) collective-permute-start(f32[1,128,128]{2,1,0:T(8,128)S(1)} %shard_map.88.refs_0_), channel_id=1, source_target_pairs={{0,24},{4,28},{8,16},{12,20},{16,8},{20,12},{24,0},{28,4},{1,25},{... | collective-permute-start | bytes 196616 | tf_op jit(solution)/shard_map/ppermute | solution.py:215
  8.0 0.6 %collective-permute-start = (f32[1,128,128]{2,1,0:T(8,128)S(1)}, f32[1,128,128]{2,1,0:T(8,128)S(1)}, u32[]{:S(2)}, u32[]{:S(2)}) collective-permute-start(f32[1,128,128]{2,1,0:T(8,128)S(1)} %shard_map.88.refs_0_), channel_id=1, source_target_pairs={{0,8},{4,12},{8,0},{12,4},{16,24},{20,28},{24,16},{28,20},{1,9},{5... | collective-permute-start | bytes 196616 | tf_op jit(solution)/shard_map/ppermute | solution.py:215
  8.6 0.5 %collective-permute-start.6 = (f32[128,128]{1,0:T(8,128)S(1)}, f32[128,128]{1,0:T(8,128)S(1)}, u32[]{:S(2)}, u32[]{:S(2)}) collective-permute-start(f32[128,128]{1,0:T(8,128)S(1)} %get-tuple-element.17), channel_id=1, source_target_pairs={{0,1},{1,0},{2,3},{3,2},{4,5},{5,4},{6,7},{7,6},{8,9},{9,8},{10,11... | collective-permute-start | bytes 196616 | tf_op jit(solution)/shard_map/ppermute | solution.py:215
  9.3 0.7 %collective-permute-done.6 = f32[128,128]{1,0:T(8,128)S(1)} collective-permute-done((f32[128,128]{1,0:T(8,128)S(1)}, f32[128,128]{1,0:T(8,128)S(1)}, u32[]{:S(2)}, u32[]{:S(2)}) %collective-permute-start.6) | collective-permute-done | bytes 65568 | tf_op jit(solution)/shard_map/ppermute | solution.py:215
  10.0 1.7 %collective-permute-start.7 = (f32[128,128]{1,0:T(8,128)S(1)}, f32[128,128]{1,0:T(8,128)S(1)}, u32[]{:S(2)}, u32[]{:S(2)}) collective-permute-start(f32[128,128]{1,0:T(8,128)S(1)} %add.13), channel_id=1, source_target_pairs={{0,2},{1,3},{2,0},{3,1},{4,6},{5,7},{6,4},{7,5},{8,10},{9,11},{10,... | collective-permute-start | bytes 196616 | tf_op jit(solution)/shard_map/ppermute | solution.py:215
  11.7 1.8 %collective-permute-done.1.refs_2_ = f32[1,128,128]{2,1,0:T(8,128)S(1)} collective-permute-done((f32[1,128,128]{2,1,0:T(8,128)S(1)}, f32[1,128,128]{2,1,0:T(8,128)S(1)}, u32[]{:S(2)}, u32[]{:S(2)}) %collective-permute-start.1) | collective-permute-done | bytes 65568 | tf_op jit(solution)/shard_map/ppermute | solution.py:215
  13.6 1.6 %collective-permute-start.3 = (f32[3,128,128]{2,1,0:T(8,128)S(1)}, f32[3,128,128]{2,1,0:T(8,128)S(1)}, u32[]{:S(2)}, u32[]{:S(2)}) collective-permute-start(f32[3,128,128]{2,1,0:T(8,128)S(1)} %pad_maximum_fusion), channel_id=1, source_target_pairs={{0,4},{4,0},{8,12},{12,8},{16,20},{20,16},{24,28},{28,24},{1,5},{5... | collective-permute-start | bytes 589832 | tf_op jit(solution)/shard_map/ppermute | solution.py:215
  15.2 0.5 %collective-permute-start.4 = (f32[1,128,128]{2,1,0:T(8,128)S(1)}, f32[1,128,128]{2,1,0:T(8,128)S(1)}, u32[]{:S(2)}, u32[]{:S(2)}) collective-permute-start(f32[1,128,128]{2,1,0:T(8,128)S(1)} %collective-permute-done.2.refs_3_), channel_id=1, source_target_pairs={{0,4},{4,0},{8,12},{12,8},{16,20},{20,16},{24,28},{28,24},{1,5},{5... | collective-permute-start | bytes 196616 | tf_op jit(solution)/shard_map/ppermute | solution.py:215
  15.7 2.8 %collective-permute-start.10 = (f32[1,128,128]{2,1,0:T(8,128)S(1)}, f32[1,128,128]{2,1,0:T(8,128)S(1)}, u32[]{:S(2)}, u32[]{:S(2)}) collective-permute-start(f32[1,128,128]{2,1,0:T(8,128)S(1)} %subtract_bitcast_fusion.refs_2_), channel_id=1, source_target_pairs={{0,24},{4,28},{8,16},{12,20},{16,8},{20,12},{24,0},{28,4},{1,25},{... | collective-permute-start | bytes 196616 | tf_op jit(solution)/shard_map/ppermute | solution.py:215
  18.5 1.7 %collective-permute-start.8 = (f32[1,128,128]{2,1,0:T(8,128)S(1)}, f32[1,128,128]{2,1,0:T(8,128)S(1)}, u32[]{:S(2)}, u32[]{:S(2)}) collective-permute-start(f32[1,128,128]{2,1,0:T(8,128)S(1)} %subtract_bitcast_fusion.refs_2_), channel_id=1, source_target_pairs={{0,8},{4,12},{8,0},{12,4},{16,24},{20,28},{24,16},{28,20},{1,9},{5... | collective-permute-start | bytes 196616 | tf_op jit(solution)/shard_map/ppermute | solution.py:215
  20.2 1.1 %shard_map.87 = (f32[2,128,512]{2,1,0:T(8,128)S(1)}, bf16[256,384]{1,0:T(8,128)(2,1)S(1)}) custom-call(f32[1,2,128,512]{3,2,1,0:T(8,128)S(1)} %copy-done, f32[1,2,128,128]{3,2,1,0:T(8,128)S(1)} %copy-done.1, f32[2,128,128]{2,1,0:T(8,128)S(1)} %get-tuple-element.11.down.order_only.refs_1_), custom_call_target="tpu_custom_call" | custom-call | flops 41943040 | bytes 1572864 | tf_op jit(solution)/shard_map/pallas_call | solution.py:56
  21.3 0.3 collective-permute-done.4.refs_5_
  21.5 1.9 %shard_map.89.refs_0_ = f32[8,256,128]{2,1,0:T(8,128)S(1)} custom-call(f32[1,128,128]{2,1,0:T(8,128)S(1)} %shard_map.88.refs_0_, f32[1,128,128]{2,1,0:T(8,128)S(1)} %collective-permute-done.refs_1_, f32[1,128,128]{2,1,0:T(8,128)S(1)} %collective-permute-done.1.refs_2_, f32[1,128,128]{2,1,0:T(8,128)S(1)} %collective-permute-done.2.refs_3_, ...), custom_call_target="tpu_custom_call" | custom-call | flops 134217728 | bytes 2097152 | tf_op jit(solution)/shard_map/pallas_call | solution.py:56
  23.5 0.8 %collective-permute-done.9.refs_4_ = f32[1,128,128]{2,1,0:T(8,128)S(1)} collective-permute-done((f32[1,128,128]{2,1,0:T(8,128)S(1)}, f32[1,128,128]{2,1,0:T(8,128)S(1)}, u32[]{:S(2)}, u32[]{:S(2)}) %collective-permute-start.9) | collective-permute-done | bytes 65568 | tf_op jit(solution)/shard_map/ppermute | solution.py:215
  24.2 0.4 %shard_map.92 = f32[128,128]{1,0:T(8,128)S(1)} custom-call(f32[8,256,128]{2,1,0:T(8,128)S(1)} %shard_map.89.refs_0_, f32[2,128,128]{2,1,0:T(8,128)S(1)} %get-tuple-element.11.down.order_only.refs_1_, f32[1,128,128]{2,1,0:T(8,128)S(1)} %subtract_bitcast_fusion.refs_2_, f32[1,128,128]{2,1,0:T(8,128)S(1)} %collective-permute-done.8.refs_3_, ...), custom_call_target="tpu_custom_call" | custom-call | flops 1342177280 | bytes 62914560 | tf_op jit(solution)/shard_map/pallas_call | solution.py:56
  24.6 1.7 %collective-permute-start.11 = (f32[128,128]{1,0:T(8,128)S(1)}, f32[128,128]{1,0:T(8,128)S(1)}, u32[]{:S(2)}, u32[]{:S(2)}) collective-permute-start(f32[128,128]{1,0:T(8,128)S(1)} %shard_map.92), channel_id=1, source_target_pairs={{0,4},{4,0},{8,12},{12,8},{16,20},{20,16},{24,28},{28,24},{1,5},{5... | collective-permute-start | bytes 196616 | tf_op jit(solution)/shard_map/ppermute | solution.py:215
  26.4 0.4 %shard_map.91 = f32[128,128]{1,0:T(8,128)S(1)} custom-call(f32[8,256,128]{2,1,0:T(8,128)S(1)} %shard_map.89.refs_0_, bf16[256,384]{1,0:T(8,128)(2,1)S(1)} %get-tuple-element.13.refs_1_, f32[1,128,128]{2,1,0:T(8,128)S(1)} %subtract_bitcast_fusion.refs_2_, f32[1,128,128]{2,1,0:T(8,128)S(1)} %collective-permute-done.8.refs_3_, ...), custom_call_target="tpu_custom_call" | custom-call | flops 1342177280 | bytes 62914560 | tf_op jit(solution)/shard_map/pallas_call | solution.py:56
  26.7 2.2 %collective-permute-done.11 = f32[128,128]{1,0:T(8,128)S(1)} collective-permute-done((f32[128,128]{1,0:T(8,128)S(1)}, f32[128,128]{1,0:T(8,128)S(1)}, u32[]{:S(2)}, u32[]{:S(2)}) %collective-permute-start.11) | collective-permute-done | bytes 65568 | tf_op jit(solution)/shard_map/ppermute | solution.py:215
  29.0 1.7 %collective-permute-start.12 = (f32[1,128,128]{2,1,0:T(8,128)S(1)}, f32[1,128,128]{2,1,0:T(8,128)S(1)}, u32[]{:S(2)}, u32[]{:S(2)}) collective-permute-start(f32[1,128,128]{2,1,0:T(8,128)S(1)} %add_bitcast_fusion), channel_id=1, source_target_pairs={{0,2},{1,3},{2,0},{3,1},{4,6},{5,7},{6,4},{7,5},{8,10},{9,11},{10,... | collective-permute-start | bytes 196616 | tf_op jit(solution)/shard_map/ppermute | solution.py:215
  30.7 2.6 %collective-permute-done.12 = f32[1,128,128]{2,1,0:T(8,128)S(1)} collective-permute-done((f32[1,128,128]{2,1,0:T(8,128)S(1)}, f32[1,128,128]{2,1,0:T(8,128)S(1)}, u32[]{:S(2)}, u32[]{:S(2)}) %collective-permute-start.12) | collective-permute-done | bytes 65568 | tf_op jit(solution)/shard_map/ppermute | solution.py:215
  33.4 0.9 %shard_map.93 = (f32[2,2,128,128]{3,2,1,0:T(8,128)S(1)}, f32[1,128,128]{2,1,0:T(8,128)}) custom-call(f32[2,128,512]{2,1,0:T(8,128)S(1)} %get-tuple-element.12.refs_0_, bf16[256,384]{1,0:T(8,128)(2,1)S(1)} %get-tuple-element.13.refs_1_, f32[1,128,128]{2,1,0:T(8,128)S(1)} %copy-done.2, f32[2,128,128]{2,1,0:T(8,128)S(1)} %pad_maximum_fusion.1.refs_3_), custom_call_target="tpu_custom_call" | custom-call | flops 20971520 | bytes 524288 | tf_op jit(solution)/shard_map/pallas_call | solution.py:56
  34.3 0.4 %collective-permute-done.13.refs_2_ = f32[2,128,128]{2,1,0:T(8,128)S(1)} collective-permute-done((f32[2,128,128]{2,1,0:T(8,128)S(1)}, f32[2,128,128]{2,1,0:T(8,128)S(1)}, u32[]{:S(2)}, u32[]{:S(2)}) %collective-permute-start.13) | collective-permute-done | bytes 131104 | tf_op jit(solution)/shard_map/ppermute | solution.py:215
  34.7 1.0 %shard_map.94 = f32[1,2,128,512]{3,2,1,0:T(8,128)} custom-call(f32[2,128,512]{2,1,0:T(8,128)S(1)} %get-tuple-element.12.refs_0_, bf16[256,384]{1,0:T(8,128)(2,1)S(1)} %get-tuple-element.13.refs_1_, f32[2,128,128]{2,1,0:T(8,128)S(1)} %collective-permute-done.13.refs_2_, f32[2,2,128,128]{3,2,1,0:T(8,128)S(1)} %get-tuple-element.18.refs_3_), custom_call_target="tpu_custom_call" | custom-call | flops 16777216 | bytes 1048576 | tf_op jit(solution)/shard_map/pallas_call | solution.py:56
  (28 shorter events, 0.6 us)
Async XLA Ops:
  0.6 2.0 %copy-start.2 = (f32[1,128,128]{2,1,0:T(8,128)S(1)}, f32[1,128,128]{2,1,0:T(8,128)}, u32[]{:S(2)}) copy-start(f32[1,128,128]{2,1,0:T(8,128)} %refs_2_.3) | copy-start | bytes 196612
  0.6 2.0 %copy-start.4 = (f32[1,128,128]{2,1,0:T(8,128)S(1)}, f32[1,128,128]{2,1,0:T(8,128)}, u32[]{:S(2)}) copy-start(f32[1,128,128]{2,1,0:T(8,128)} %link.1) | copy-start | bytes 196612
  2.6 6.5 %copy-start.3 = (f32[1,128,512]{2,1,0:T(8,128)S(1)}, f32[1,128,512]{2,1,0:T(8,128)}, u32[]{:S(2)}) copy-start(f32[1,128,512]{2,1,0:T(8,128)} %rhs.3) | copy-start | bytes 786436
  2.9 12.3 %collective-permute-start.2 = (f32[1,128,128]{2,1,0:T(8,128)S(1)}, f32[1,128,128]{2,1,0:T(8,128)S(1)}, u32[]{:S(2)}, u32[]{:S(2)}) collective-permute-start(f32[1,128,128]{2,1,0:T(8,128)S(1)} %shard_map.88.refs_0_), channel_id=1, source_target_pairs={{0,24},{4,28},{8,16},{12,20},{16,8},{20,12},{24,0},{28,4},{1,25},{... | collective-permute-start | bytes 196616 | tf_op jit(solution)/shard_map/ppermute | solution.py:215
  8.0 5.6 %collective-permute-start.1 = (f32[1,128,128]{2,1,0:T(8,128)S(1)}, f32[1,128,128]{2,1,0:T(8,128)S(1)}, u32[]{:S(2)}, u32[]{:S(2)}) collective-permute-start(f32[1,128,128]{2,1,0:T(8,128)S(1)} %shard_map.88.refs_0_), channel_id=1, source_target_pairs={{0,16},{4,20},{8,24},{12,28},{16,0},{20,4},{24,8},{28,12},{1,17},{... | collective-permute-start | bytes 196616 | tf_op jit(solution)/shard_map/ppermute | solution.py:215
  8.0 5.6 %collective-permute-start = (f32[1,128,128]{2,1,0:T(8,128)S(1)}, f32[1,128,128]{2,1,0:T(8,128)S(1)}, u32[]{:S(2)}, u32[]{:S(2)}) collective-permute-start(f32[1,128,128]{2,1,0:T(8,128)S(1)} %shard_map.88.refs_0_), channel_id=1, source_target_pairs={{0,8},{4,12},{8,0},{12,4},{16,24},{20,28},{24,16},{28,20},{1,9},{5... | collective-permute-start | bytes 196616 | tf_op jit(solution)/shard_map/ppermute | solution.py:215
  8.6 7.1 %collective-permute-start.5 = (f32[128,128]{1,0:T(8,128)S(1)}, f32[128,128]{1,0:T(8,128)S(1)}, u32[]{:S(2)}, u32[]{:S(2)}) collective-permute-start(f32[128,128]{1,0:T(8,128)S(1)} %get-tuple-element.15), channel_id=1, source_target_pairs={{0,1},{1,0},{2,3},{3,2},{4,5},{5,4},{6,7},{7,6},{8,9},{9,8},{10,11... | collective-permute-start | bytes 196616 | tf_op jit(solution)/shard_map/ppermute | solution.py:215
  8.6 1.4 %collective-permute-start.6 = (f32[128,128]{1,0:T(8,128)S(1)}, f32[128,128]{1,0:T(8,128)S(1)}, u32[]{:S(2)}, u32[]{:S(2)}) collective-permute-start(f32[128,128]{1,0:T(8,128)S(1)} %get-tuple-element.17), channel_id=1, source_target_pairs={{0,1},{1,0},{2,3},{3,2},{4,5},{5,4},{6,7},{7,6},{8,9},{9,8},{10,11... | collective-permute-start | bytes 196616 | tf_op jit(solution)/shard_map/ppermute | solution.py:215
  9.3 10.8 %copy-start = (f32[1,2,128,512]{3,2,1,0:T(8,128)S(1)}, f32[1,2,128,512]{3,2,1,0:T(8,128)}, u32[]{:S(2)}) copy-start(f32[1,2,128,512]{3,2,1,0:T(8,128)} %rhs.2) | copy-start | bytes 1572868
  10.0 5.7 %collective-permute-start.7 = (f32[128,128]{1,0:T(8,128)S(1)}, f32[128,128]{1,0:T(8,128)S(1)}, u32[]{:S(2)}, u32[]{:S(2)}) collective-permute-start(f32[128,128]{1,0:T(8,128)S(1)} %add.13), channel_id=1, source_target_pairs={{0,2},{1,3},{2,0},{3,1},{4,6},{5,7},{6,4},{7,5},{8,10},{9,11},{10,... | collective-permute-start | bytes 196616 | tf_op jit(solution)/shard_map/ppermute | solution.py:215
  13.6 7.9 %collective-permute-start.3 = (f32[3,128,128]{2,1,0:T(8,128)S(1)}, f32[3,128,128]{2,1,0:T(8,128)S(1)}, u32[]{:S(2)}, u32[]{:S(2)}) collective-permute-start(f32[3,128,128]{2,1,0:T(8,128)S(1)} %pad_maximum_fusion), channel_id=1, source_target_pairs={{0,4},{4,0},{8,12},{12,8},{16,20},{20,16},{24,28},{28,24},{1,5},{5... | collective-permute-start | bytes 589832 | tf_op jit(solution)/shard_map/ppermute | solution.py:215
  15.2 6.4 %collective-permute-start.4 = (f32[1,128,128]{2,1,0:T(8,128)S(1)}, f32[1,128,128]{2,1,0:T(8,128)S(1)}, u32[]{:S(2)}, u32[]{:S(2)}) collective-permute-start(f32[1,128,128]{2,1,0:T(8,128)S(1)} %collective-permute-done.2.refs_3_), channel_id=1, source_target_pairs={{0,4},{4,0},{8,12},{12,8},{16,20},{20,16},{24,28},{28,24},{1,5},{5... | collective-permute-start | bytes 196616 | tf_op jit(solution)/shard_map/ppermute | solution.py:215
  15.7 4.5 %copy-start.1 = (f32[1,2,128,128]{3,2,1,0:T(8,128)S(1)}, f32[1,2,128,128]{3,2,1,0:T(8,128)}, u32[]{:S(2)}) copy-start(f32[1,2,128,128]{3,2,1,0:T(8,128)} %leaf_inv.1) | copy-start | bytes 393220
  15.7 7.7 %collective-permute-start.10 = (f32[1,128,128]{2,1,0:T(8,128)S(1)}, f32[1,128,128]{2,1,0:T(8,128)S(1)}, u32[]{:S(2)}, u32[]{:S(2)}) collective-permute-start(f32[1,128,128]{2,1,0:T(8,128)S(1)} %subtract_bitcast_fusion.refs_2_), channel_id=1, source_target_pairs={{0,24},{4,28},{8,16},{12,20},{16,8},{20,12},{24,0},{28,4},{1,25},{... | collective-permute-start | bytes 196616 | tf_op jit(solution)/shard_map/ppermute | solution.py:215
  18.5 5.7 %collective-permute-start.9 = (f32[1,128,128]{2,1,0:T(8,128)S(1)}, f32[1,128,128]{2,1,0:T(8,128)S(1)}, u32[]{:S(2)}, u32[]{:S(2)}) collective-permute-start(f32[1,128,128]{2,1,0:T(8,128)S(1)} %subtract_bitcast_fusion.refs_2_), channel_id=1, source_target_pairs={{0,16},{4,20},{8,24},{12,28},{16,0},{20,4},{24,8},{28,12},{1,17},{... | collective-permute-start | bytes 196616 | tf_op jit(solution)/shard_map/ppermute | solution.py:215
  18.5 5.7 %collective-permute-start.8 = (f32[1,128,128]{2,1,0:T(8,128)S(1)}, f32[1,128,128]{2,1,0:T(8,128)S(1)}, u32[]{:S(2)}, u32[]{:S(2)}) collective-permute-start(f32[1,128,128]{2,1,0:T(8,128)S(1)} %subtract_bitcast_fusion.refs_2_), channel_id=1, source_target_pairs={{0,8},{4,12},{8,0},{12,4},{16,24},{20,28},{24,16},{28,20},{1,9},{5... | collective-permute-start | bytes 196616 | tf_op jit(solution)/shard_map/ppermute | solution.py:215
  24.6 4.3 %collective-permute-start.11 = (f32[128,128]{1,0:T(8,128)S(1)}, f32[128,128]{1,0:T(8,128)S(1)}, u32[]{:S(2)}, u32[]{:S(2)}) collective-permute-start(f32[128,128]{1,0:T(8,128)S(1)} %shard_map.92), channel_id=1, source_target_pairs={{0,4},{4,0},{8,12},{12,8},{16,20},{20,16},{24,28},{28,24},{1,5},{5... | collective-permute-start | bytes 196616 | tf_op jit(solution)/shard_map/ppermute | solution.py:215
  29.0 4.3 %collective-permute-start.12 = (f32[1,128,128]{2,1,0:T(8,128)S(1)}, f32[1,128,128]{2,1,0:T(8,128)S(1)}, u32[]{:S(2)}, u32[]{:S(2)}) collective-permute-start(f32[1,128,128]{2,1,0:T(8,128)S(1)} %add_bitcast_fusion), channel_id=1, source_target_pairs={{0,2},{1,3},{2,0},{3,1},{4,6},{5,7},{6,4},{7,5},{8,10},{9,11},{10,... | collective-permute-start | bytes 196616 | tf_op jit(solution)/shard_map/ppermute | solution.py:215
  33.3 1.4 %collective-permute-start.13 = (f32[2,128,128]{2,1,0:T(8,128)S(1)}, f32[2,128,128]{2,1,0:T(8,128)S(1)}, u32[]{:S(2)}, u32[]{:S(2)}) collective-permute-start(f32[2,128,128]{2,1,0:T(8,128)S(1)} %pad_maximum_fusion.1.refs_3_), channel_id=1, source_target_pairs={{0,1},{1,0},{2,3},{3,2},{4,5},{5,4},{6,7},{7,6},{8,9},{9,8},{10,11... | collective-permute-start | bytes 393224 | tf_op jit(solution)/shard_map/ppermute | solution.py:215

commit v7 on v6

--- a/solution.py
+++ b/solution.py
@@ -168,7 +168,7 @@
     total = None
     for p, part in enumerate(parts):
         for i in range(size):
-            piece = dot(held[2 * (p * size + i) ^ me, rows], part[i])
+            piece = dot3(held[2 * (p * size + i) ^ me, rows], part[i])
             total = piece if total is None else total + piece
     out[...] = total
 
@@ -192,20 +192,22 @@
     solved[0] = dot_ta(inverse[0], spread[0])
 
 
-def late_blocks(early, late, base, factors, spread, done, leaves, fresh, sems):
+def late_blocks(early, late, base, factors, spread, *refs):
+    done, (leaves, fresh, sems) = refs[:-3], refs[-3:]
     width = spread.shape[2]
 
-    def put(i, slot, source):
+    def put(slot, source):
         target = leaves.at[0, :, :, columns_of(lax.axis_index("grp") ^ slot, width)]
-        return pltpu.make_async_copy(source, target, sems.at[i])
-
-    copies = [put(i, slot, done.at[i]) for i, slot in enumerate(early)]
+        return pltpu.make_async_copy(source, target, sems.at[slot])
+
+    copies = [
+        put(slot, blocks.at[i]) for slots, blocks in zip(early, done) for i, slot in enumerate(slots)
+    ]
     for copy in copies:
         copy.start()
-    leaf_blocks(late, base, factors, spread, fresh)
-    for i, slot in enumerate(late):
-        copies.append(put(len(early) + i, slot, fresh.at[i]))
-        copies[-1].start()
+    leaf_blocks([late], base, factors, spread, fresh)
+    copies.append(put(late, fresh.at[0]))
+    copies[-1].start()
     for copy in copies:
         copy.wait()
 
@@ -282,25 +284,27 @@
 
     theirs = swap(applied(1, down), "leaf", 1)
     carried = applied(0, factors) + theirs
-    spread, slots, bit = carried[None], [0], groups // 2
-    while bit > 1:
-        spread = jnp.concatenate([spread, swap(spread, "grp", bit)], axis=0)
-        slots = slots + [slot ^ bit for slot in slots]
-        bit //= 2
-    late = [slot ^ 1 for slot in slots]
-    arrived = swap(spread, "grp", 1)
-    done, solved = call(
-        lambda *refs: early_blocks(slots, *refs),
-        (shaped(len(slots), count, order, width), shaped(1, order, width)),
-        (len(slots) * count + 1) * cube, 4 * leaf_rhs.size, base, factors, sep_inv, spread,
-    )
+    blocks = {0: carried[None]}
+    for m in sorted(range(1, groups), key=lambda m: (m & (m - 1) != 0, -m)):
+        blocks[m] = swap(blocks[m & (m - 1)], "grp", m & -m)
+    early, solved = call(
+        lambda *refs: early_blocks([0, 1], *refs),
+        (shaped(2, count, order, width), shaped(1, order, width)),
+        (2 * count + 1) * cube, 4 * leaf_rhs.size, base, factors, sep_inv, jnp.concatenate([blocks[0], blocks[1]], axis=0),
+    )
+    done, slots = [early], [[0, 1]]
+    for m in range(2, groups - 1):
+        slots.append([m])
+        done.append(
+            call(
+                lambda *refs, m=m: leaf_blocks([m], *refs), shaped(1, count, order, width),
+                count * cube, 2 * leaf_rhs.size, base, factors, blocks[m],
+            )
+        )
     leaves = call(
-        lambda *refs: late_blocks(slots, late, *refs), shaped(1, count, order, columns),
-        len(late) * count * cube, 8 * leaf_rhs.size, base, factors, arrived, done,
-        held=[
-            pltpu.VMEM((len(late), count, order, width), F32),
-            pltpu.SemaphoreType.DMA((groups,)),
-        ],
+        lambda *refs: late_blocks(slots, groups - 1, *refs), shaped(1, count, order, columns),
+        count * cube, 8 * leaf_rhs.size, base, factors, blocks[groups - 1], *done,
+        held=[pltpu.VMEM((1, count, order, width), F32), pltpu.SemaphoreType.DMA((groups,))],
         out_specs=HBM,
     )
     return leaves, solved

time: 35.8 us -> 35.5 us (level)
    ppermute x14 -> x15, waiting for transfers between devices: 8.83 us -> 8.63 us  [swap(): return lax.ppermute(value, axis, [(i, i ^ bit) for i in range(count)])]
    pallas_call x9 -> x10, Pallas kernels: 7.98 us -> 7.87 us  [call(): pl.pallas_call(body, out_shape=outs, in_specs=[HBM] * far + [VMEM] * (len...]
    ppermute x14 -> x15, starting transfers between devices: 18 us -> 17.9 us  [swap(): return lax.ppermute(value, axis, [(i, i ^ bit) for i in range(count)])]
  transfers between devices with their start and end apart: 14 -> 15, of which waited for: 7 -> 7; matrix products, arithmetic and copies ran while one was open for 0% -> 0% of each run, Pallas kernels for 13% -> 13%
where the time goes in v7:
time: 35.5 us; the launch traced here: 35.3 us
  starting transfers between devices  17.9 us (50%)
  waiting for transfers between devices  8.63 us (24%)
  Pallas kernels  7.87 us (22%)
  between operations  0.8 us (2%)
    ppermute x15, starting transfers between devices, swap(): return lax.ppermute(value, axis, [(i, i ^ bit) for i in range(count)])  17.9 us
    ppermute x15, waiting for transfers between devices, swap(): return lax.ppermute(value, axis, [(i, i ^ bit) for i in range(count)])  8.63 us
    pallas_call x10, Pallas kernels, call(): pl.pallas_call(body, out_shape=outs, in_specs=[HBM] * far + [VMEM] * (len...  7.87 us
  transfers between devices with their start and end apart: 15, of which 7 were waited for; matrix products, arithmetic and copies ran while one was open for 0% of the time, Pallas kernels for 13%

profile of v7, /device:TPU:0, one launch (start us, length us, event | category | flops | bytes accessed | tf_op | source)
XLA Modules:
  0.0 35.3 jit_solution(4439593933671366774)
XLA Ops:
  0.7 2.0 %shard_map.86 = (f32[2,128,128]{2,1,0:T(8,128)S(1)}, f32[128,128]{1,0:T(8,128)S(1)}, f32[128,128]{1,0:T(8,128)S(1)}, f32[128,128]{1,0:T(8,128)S(1)}, f32[128,128]{1,0:T(8,128)S(1)}) custom-call(f32[1,128,128]{2,1,0:T(8,128)} %refs_2_.3, s32[1,2]{1,0:T(1,128)} %refs_1_.1, f32[1,2,128,128]{3,2,1,0:T(8,128)} %leaf_inv.1, f32[1,2,128,128]{3,2,1,0:T(8,128)} %refs_3_.1, ...), custom_call_target="tpu_custom_call" | custom-call | flops 1342177280 | bytes 62914560 | tf_op jit(solution)/shard_map/pallas_call | solution.py:56
  2.9 5.1 %collective-permute-start.2 = (f32[1,128,128]{2,1,0:T(8,128)S(1)}, f32[1,128,128]{2,1,0:T(8,128)S(1)}, u32[]{:S(2)}, u32[]{:S(2)}) collective-permute-start(f32[1,128,128]{2,1,0:T(8,128)S(1)} %shard_map.88.refs_0_), channel_id=1, source_target_pairs={{0,24},{4,28},{8,16},{12,20},{16,8},{20,12},{24,0},{28,4},{1,25},{... | collective-permute-start | bytes 196616 | tf_op jit(solution)/shard_map/ppermute | solution.py:217
  8.0 0.6 %collective-permute-start = (f32[1,128,128]{2,1,0:T(8,128)S(1)}, f32[1,128,128]{2,1,0:T(8,128)S(1)}, u32[]{:S(2)}, u32[]{:S(2)}) collective-permute-start(f32[1,128,128]{2,1,0:T(8,128)S(1)} %shard_map.88.refs_0_), channel_id=1, source_target_pairs={{0,8},{4,12},{8,0},{12,4},{16,24},{20,28},{24,16},{28,20},{1,9},{5... | collective-permute-start | bytes 196616 | tf_op jit(solution)/shard_map/ppermute | solution.py:217
  8.6 0.5 %collective-permute-start.6 = (f32[128,128]{1,0:T(8,128)S(1)}, f32[128,128]{1,0:T(8,128)S(1)}, u32[]{:S(2)}, u32[]{:S(2)}) collective-permute-start(f32[128,128]{1,0:T(8,128)S(1)} %get-tuple-element.17), channel_id=1, source_target_pairs={{0,1},{1,0},{2,3},{3,2},{4,5},{5,4},{6,7},{7,6},{8,9},{9,8},{10,11... | collective-permute-start | bytes 196616 | tf_op jit(solution)/shard_map/ppermute | solution.py:217
  9.1 0.2 shard_map.90
  9.3 0.7 %collective-permute-done.6 = f32[128,128]{1,0:T(8,128)S(1)} collective-permute-done((f32[128,128]{1,0:T(8,128)S(1)}, f32[128,128]{1,0:T(8,128)S(1)}, u32[]{:S(2)}, u32[]{:S(2)}) %collective-permute-start.6) | collective-permute-done | bytes 65568 | tf_op jit(solution)/shard_map/ppermute | solution.py:217
  10.0 1.7 %collective-permute-start.7 = (f32[128,128]{1,0:T(8,128)S(1)}, f32[128,128]{1,0:T(8,128)S(1)}, u32[]{:S(2)}, u32[]{:S(2)}) collective-permute-start(f32[128,128]{1,0:T(8,128)S(1)} %add.13), channel_id=1, source_target_pairs={{0,2},{1,3},{2,0},{3,1},{4,6},{5,7},{6,4},{7,5},{8,10},{9,11},{10,... | collective-permute-start | bytes 196616 | tf_op jit(solution)/shard_map/ppermute | solution.py:217
  11.7 1.8 %collective-permute-done.1.refs_2_ = f32[1,128,128]{2,1,0:T(8,128)S(1)} collective-permute-done((f32[1,128,128]{2,1,0:T(8,128)S(1)}, f32[1,128,128]{2,1,0:T(8,128)S(1)}, u32[]{:S(2)}, u32[]{:S(2)}) %collective-permute-start.1) | collective-permute-done | bytes 65568 | tf_op jit(solution)/shard_map/ppermute | solution.py:217
  13.6 1.6 %collective-permute-start.3 = (f32[3,128,128]{2,1,0:T(8,128)S(1)}, f32[3,128,128]{2,1,0:T(8,128)S(1)}, u32[]{:S(2)}, u32[]{:S(2)}) collective-permute-start(f32[3,128,128]{2,1,0:T(8,128)S(1)} %pad_maximum_fusion), channel_id=1, source_target_pairs={{0,4},{4,0},{8,12},{12,8},{16,20},{20,16},{24,28},{28,24},{1,5},{5... | collective-permute-start | bytes 589832 | tf_op jit(solution)/shard_map/ppermute | solution.py:217
  15.2 0.5 %collective-permute-start.4 = (f32[1,128,128]{2,1,0:T(8,128)S(1)}, f32[1,128,128]{2,1,0:T(8,128)S(1)}, u32[]{:S(2)}, u32[]{:S(2)}) collective-permute-start(f32[1,128,128]{2,1,0:T(8,128)S(1)} %collective-permute-done.2.refs_3_), channel_id=1, source_target_pairs={{0,4},{4,0},{8,12},{12,8},{16,20},{20,16},{24,28},{28,24},{1,5},{5... | collective-permute-start | bytes 196616 | tf_op jit(solution)/shard_map/ppermute | solution.py:217
  15.7 2.8 %collective-permute-start.10 = (f32[1,128,128]{2,1,0:T(8,128)S(1)}, f32[1,128,128]{2,1,0:T(8,128)S(1)}, u32[]{:S(2)}, u32[]{:S(2)}) collective-permute-start(f32[1,128,128]{2,1,0:T(8,128)S(1)} %subtract_bitcast_fusion.refs_2_), channel_id=1, source_target_pairs={{0,24},{4,28},{8,16},{12,20},{16,8},{20,12},{24,0},{28,4},{1,25},{... | collective-permute-start | bytes 196616 | tf_op jit(solution)/shard_map/ppermute | solution.py:217
  18.5 1.7 %collective-permute-start.8 = (f32[1,128,128]{2,1,0:T(8,128)S(1)}, f32[1,128,128]{2,1,0:T(8,128)S(1)}, u32[]{:S(2)}, u32[]{:S(2)}) collective-permute-start(f32[1,128,128]{2,1,0:T(8,128)S(1)} %subtract_bitcast_fusion.refs_2_), channel_id=1, source_target_pairs={{0,8},{4,12},{8,0},{12,4},{16,24},{20,28},{24,16},{28,20},{1,9},{5... | collective-permute-start | bytes 196616 | tf_op jit(solution)/shard_map/ppermute | solution.py:217
  20.2 1.1 %shard_map.87 = (f32[2,128,512]{2,1,0:T(8,128)S(1)}, bf16[256,384]{1,0:T(8,128)(2,1)S(1)}) custom-call(f32[1,2,128,512]{3,2,1,0:T(8,128)S(1)} %copy-done, f32[1,2,128,128]{3,2,1,0:T(8,128)S(1)} %copy-done.1, f32[2,128,128]{2,1,0:T(8,128)S(1)} %get-tuple-element.11.down.order_only.refs_1_), custom_call_target="tpu_custom_call" | custom-call | flops 41943040 | bytes 1572864 | tf_op jit(solution)/shard_map/pallas_call | solution.py:56
  21.3 0.3 collective-permute-done.4.refs_5_
  21.5 1.9 %shard_map.89.refs_0_ = f32[8,256,128]{2,1,0:T(8,128)S(1)} custom-call(f32[1,128,128]{2,1,0:T(8,128)S(1)} %shard_map.88.refs_0_, f32[1,128,128]{2,1,0:T(8,128)S(1)} %collective-permute-done.refs_1_, f32[1,128,128]{2,1,0:T(8,128)S(1)} %collective-permute-done.1.refs_2_, f32[1,128,128]{2,1,0:T(8,128)S(1)} %collective-permute-done.2.refs_3_, ...), custom_call_target="tpu_custom_call" | custom-call | flops 134217728 | bytes 2097152 | tf_op jit(solution)/shard_map/pallas_call | solution.py:56
  23.5 0.8 %collective-permute-done.9.refs_4_ = f32[1,128,128]{2,1,0:T(8,128)S(1)} collective-permute-done((f32[1,128,128]{2,1,0:T(8,128)S(1)}, f32[1,128,128]{2,1,0:T(8,128)S(1)}, u32[]{:S(2)}, u32[]{:S(2)}) %collective-permute-start.9) | collective-permute-done | bytes 65568 | tf_op jit(solution)/shard_map/ppermute | solution.py:217
  24.2 0.3 shard_map.92
  24.5 1.7 %collective-permute-start.11 = (f32[128,128]{1,0:T(8,128)S(1)}, f32[128,128]{1,0:T(8,128)S(1)}, u32[]{:S(2)}, u32[]{:S(2)}) collective-permute-start(f32[128,128]{1,0:T(8,128)S(1)} %shard_map.92), channel_id=1, source_target_pairs={{0,4},{4,0},{8,12},{12,8},{16,20},{20,16},{24,28},{28,24},{1,5},{5... | collective-permute-start | bytes 196616 | tf_op jit(solution)/shard_map/ppermute | solution.py:217
  26.2 0.3 shard_map.91
  26.5 2.3 %collective-permute-done.11 = f32[128,128]{1,0:T(8,128)S(1)} collective-permute-done((f32[128,128]{1,0:T(8,128)S(1)}, f32[128,128]{1,0:T(8,128)S(1)}, u32[]{:S(2)}, u32[]{:S(2)}) %collective-permute-start.11) | collective-permute-done | bytes 65568 | tf_op jit(solution)/shard_map/ppermute | solution.py:217
  28.9 1.7 %collective-permute-start.12 = (f32[1,128,128]{2,1,0:T(8,128)S(1)}, f32[1,128,128]{2,1,0:T(8,128)S(1)}, u32[]{:S(2)}, u32[]{:S(2)}) collective-permute-start(f32[1,128,128]{2,1,0:T(8,128)S(1)} %add_bitcast_fusion), channel_id=1, source_target_pairs={{0,2},{1,3},{2,0},{3,1},{4,6},{5,7},{6,4},{7,5},{8,10},{9,11},{10,... | collective-permute-start | bytes 196616 | tf_op jit(solution)/shard_map/ppermute | solution.py:217
  30.6 2.6 %collective-permute-done.12.refs_2_ = f32[1,128,128]{2,1,0:T(8,128)S(1)} collective-permute-done((f32[1,128,128]{2,1,0:T(8,128)S(1)}, f32[1,128,128]{2,1,0:T(8,128)S(1)}, u32[]{:S(2)}, u32[]{:S(2)}) %collective-permute-start.12) | collective-permute-done | bytes 65568 | tf_op jit(solution)/shard_map/ppermute | solution.py:217
  33.4 0.9 %shard_map.93 = (f32[2,2,128,128]{3,2,1,0:T(8,128)S(1)}, f32[1,128,128]{2,1,0:T(8,128)}) custom-call(f32[2,128,512]{2,1,0:T(8,128)S(1)} %get-tuple-element.12.refs_0_, bf16[256,384]{1,0:T(8,128)(2,1)S(1)} %get-tuple-element.13.refs_1_, f32[1,128,128]{2,1,0:T(8,128)S(1)} %copy-done.2, f32[2,128,128]{2,1,0:T(8,128)S(1)} %pad_maximum_fusion.1.refs_3_), custom_call_target="tpu_custom_call" | custom-call | flops 20971520 | bytes 524288 | tf_op jit(solution)/shard_map/pallas_call | solution.py:56
  34.4 0.9 %shard_map.95 = f32[1,2,128,512]{3,2,1,0:T(8,128)} custom-call(f32[2,128,512]{2,1,0:T(8,128)S(1)} %get-tuple-element.12.refs_0_, bf16[256,384]{1,0:T(8,128)(2,1)S(1)} %get-tuple-element.13.refs_1_, f32[1,128,128]{2,1,0:T(8,128)S(1)} %collective-permute-done.13.refs_2_, f32[2,2,128,128]{3,2,1,0:T(8,128)S(1)} %get-tuple-element.18.refs_3_, ...), custom_call_target="tpu_custom_call" | custom-call | flops 8388608 | bytes 1048576 | tf_op jit(solution)/shard_map/pallas_call | solution.py:56
  (31 shorter events, 0.6 us)
Async XLA Ops:
  0.6 2.0 %copy-start.2 = (f32[1,128,128]{2,1,0:T(8,128)S(1)}, f32[1,128,128]{2,1,0:T(8,128)}, u32[]{:S(2)}) copy-start(f32[1,128,128]{2,1,0:T(8,128)} %refs_2_.3) | copy-start | bytes 196612
  0.6 2.0 %copy-start.4 = (f32[1,128,128]{2,1,0:T(8,128)S(1)}, f32[1,128,128]{2,1,0:T(8,128)}, u32[]{:S(2)}) copy-start(f32[1,128,128]{2,1,0:T(8,128)} %link.1) | copy-start | bytes 196612
  2.6 6.5 %copy-start.3 = (f32[1,128,512]{2,1,0:T(8,128)S(1)}, f32[1,128,512]{2,1,0:T(8,128)}, u32[]{:S(2)}) copy-start(f32[1,128,512]{2,1,0:T(8,128)} %rhs.3) | copy-start | bytes 786436
  2.9 12.3 %collective-permute-start.2 = (f32[1,128,128]{2,1,0:T(8,128)S(1)}, f32[1,128,128]{2,1,0:T(8,128)S(1)}, u32[]{:S(2)}, u32[]{:S(2)}) collective-permute-start(f32[1,128,128]{2,1,0:T(8,128)S(1)} %shard_map.88.refs_0_), channel_id=1, source_target_pairs={{0,24},{4,28},{8,16},{12,20},{16,8},{20,12},{24,0},{28,4},{1,25},{... | collective-permute-start | bytes 196616 | tf_op jit(solution)/shard_map/ppermute | solution.py:217
  8.0 5.6 %collective-permute-start.1 = (f32[1,128,128]{2,1,0:T(8,128)S(1)}, f32[1,128,128]{2,1,0:T(8,128)S(1)}, u32[]{:S(2)}, u32[]{:S(2)}) collective-permute-start(f32[1,128,128]{2,1,0:T(8,128)S(1)} %shard_map.88.refs_0_), channel_id=1, source_target_pairs={{0,16},{4,20},{8,24},{12,28},{16,0},{20,4},{24,8},{28,12},{1,17},{... | collective-permute-start | bytes 196616 | tf_op jit(solution)/shard_map/ppermute | solution.py:217
  8.0 5.6 %collective-permute-start = (f32[1,128,128]{2,1,0:T(8,128)S(1)}, f32[1,128,128]{2,1,0:T(8,128)S(1)}, u32[]{:S(2)}, u32[]{:S(2)}) collective-permute-start(f32[1,128,128]{2,1,0:T(8,128)S(1)} %shard_map.88.refs_0_), channel_id=1, source_target_pairs={{0,8},{4,12},{8,0},{12,4},{16,24},{20,28},{24,16},{28,20},{1,9},{5... | collective-permute-start | bytes 196616 | tf_op jit(solution)/shard_map/ppermute | solution.py:217
  8.6 7.1 %collective-permute-start.5 = (f32[128,128]{1,0:T(8,128)S(1)}, f32[128,128]{1,0:T(8,128)S(1)}, u32[]{:S(2)}, u32[]{:S(2)}) collective-permute-start(f32[128,128]{1,0:T(8,128)S(1)} %get-tuple-element.15), channel_id=1, source_target_pairs={{0,1},{1,0},{2,3},{3,2},{4,5},{5,4},{6,7},{7,6},{8,9},{9,8},{10,11... | collective-permute-start | bytes 196616 | tf_op jit(solution)/shard_map/ppermute | solution.py:217
  8.6 1.4 %collective-permute-start.6 = (f32[128,128]{1,0:T(8,128)S(1)}, f32[128,128]{1,0:T(8,128)S(1)}, u32[]{:S(2)}, u32[]{:S(2)}) collective-permute-start(f32[128,128]{1,0:T(8,128)S(1)} %get-tuple-element.17), channel_id=1, source_target_pairs={{0,1},{1,0},{2,3},{3,2},{4,5},{5,4},{6,7},{7,6},{8,9},{9,8},{10,11... | collective-permute-start | bytes 196616 | tf_op jit(solution)/shard_map/ppermute | solution.py:217
  9.3 10.8 %copy-start = (f32[1,2,128,512]{3,2,1,0:T(8,128)S(1)}, f32[1,2,128,512]{3,2,1,0:T(8,128)}, u32[]{:S(2)}) copy-start(f32[1,2,128,512]{3,2,1,0:T(8,128)} %rhs.2) | copy-start | bytes 1572868
  10.0 5.7 %collective-permute-start.7 = (f32[128,128]{1,0:T(8,128)S(1)}, f32[128,128]{1,0:T(8,128)S(1)}, u32[]{:S(2)}, u32[]{:S(2)}) collective-permute-start(f32[128,128]{1,0:T(8,128)S(1)} %add.13), channel_id=1, source_target_pairs={{0,2},{1,3},{2,0},{3,1},{4,6},{5,7},{6,4},{7,5},{8,10},{9,11},{10,... | collective-permute-start | bytes 196616 | tf_op jit(solution)/shard_map/ppermute | solution.py:217
  13.6 7.9 %collective-permute-start.3 = (f32[3,128,128]{2,1,0:T(8,128)S(1)}, f32[3,128,128]{2,1,0:T(8,128)S(1)}, u32[]{:S(2)}, u32[]{:S(2)}) collective-permute-start(f32[3,128,128]{2,1,0:T(8,128)S(1)} %pad_maximum_fusion), channel_id=1, source_target_pairs={{0,4},{4,0},{8,12},{12,8},{16,20},{20,16},{24,28},{28,24},{1,5},{5... | collective-permute-start | bytes 589832 | tf_op jit(solution)/shard_map/ppermute | solution.py:217
  15.2 6.4 %collective-permute-start.4 = (f32[1,128,128]{2,1,0:T(8,128)S(1)}, f32[1,128,128]{2,1,0:T(8,128)S(1)}, u32[]{:S(2)}, u32[]{:S(2)}) collective-permute-start(f32[1,128,128]{2,1,0:T(8,128)S(1)} %collective-permute-done.2.refs_3_), channel_id=1, source_target_pairs={{0,4},{4,0},{8,12},{12,8},{16,20},{20,16},{24,28},{28,24},{1,5},{5... | collective-permute-start | bytes 196616 | tf_op jit(solution)/shard_map/ppermute | solution.py:217
  15.7 4.5 %copy-start.1 = (f32[1,2,128,128]{3,2,1,0:T(8,128)S(1)}, f32[1,2,128,128]{3,2,1,0:T(8,128)}, u32[]{:S(2)}) copy-start(f32[1,2,128,128]{3,2,1,0:T(8,128)} %leaf_inv.1) | copy-start | bytes 393220
  15.7 7.7 %collective-permute-start.10 = (f32[1,128,128]{2,1,0:T(8,128)S(1)}, f32[1,128,128]{2,1,0:T(8,128)S(1)}, u32[]{:S(2)}, u32[]{:S(2)}) collective-permute-start(f32[1,128,128]{2,1,0:T(8,128)S(1)} %subtract_bitcast_fusion.refs_2_), channel_id=1, source_target_pairs={{0,24},{4,28},{8,16},{12,20},{16,8},{20,12},{24,0},{28,4},{1,25},{... | collective-permute-start | bytes 196616 | tf_op jit(solution)/shard_map/ppermute | solution.py:217
  18.5 5.7 %collective-permute-start.9 = (f32[1,128,128]{2,1,0:T(8,128)S(1)}, f32[1,128,128]{2,1,0:T(8,128)S(1)}, u32[]{:S(2)}, u32[]{:S(2)}) collective-permute-start(f32[1,128,128]{2,1,0:T(8,128)S(1)} %subtract_bitcast_fusion.refs_2_), channel_id=1, source_target_pairs={{0,16},{4,20},{8,24},{12,28},{16,0},{20,4},{24,8},{28,12},{1,17},{... | collective-permute-start | bytes 196616 | tf_op jit(solution)/shard_map/ppermute | solution.py:217
  18.5 5.7 %collective-permute-start.8 = (f32[1,128,128]{2,1,0:T(8,128)S(1)}, f32[1,128,128]{2,1,0:T(8,128)S(1)}, u32[]{:S(2)}, u32[]{:S(2)}) collective-permute-start(f32[1,128,128]{2,1,0:T(8,128)S(1)} %subtract_bitcast_fusion.refs_2_), channel_id=1, source_target_pairs={{0,8},{4,12},{8,0},{12,4},{16,24},{20,28},{24,16},{28,20},{1,9},{5... | collective-permute-start | bytes 196616 | tf_op jit(solution)/shard_map/ppermute | solution.py:217
  24.5 4.3 %collective-permute-start.11 = (f32[128,128]{1,0:T(8,128)S(1)}, f32[128,128]{1,0:T(8,128)S(1)}, u32[]{:S(2)}, u32[]{:S(2)}) collective-permute-start(f32[128,128]{1,0:T(8,128)S(1)} %shard_map.92), channel_id=1, source_target_pairs={{0,4},{4,0},{8,12},{12,8},{16,20},{20,16},{24,28},{28,24},{1,5},{5... | collective-permute-start | bytes 196616 | tf_op jit(solution)/shard_map/ppermute | solution.py:217
  28.9 4.3 %collective-permute-start.12 = (f32[1,128,128]{2,1,0:T(8,128)S(1)}, f32[1,128,128]{2,1,0:T(8,128)S(1)}, u32[]{:S(2)}, u32[]{:S(2)}) collective-permute-start(f32[1,128,128]{2,1,0:T(8,128)S(1)} %add_bitcast_fusion), channel_id=1, source_target_pairs={{0,2},{1,3},{2,0},{3,1},{4,6},{5,7},{6,4},{7,5},{8,10},{9,11},{10,... | collective-permute-start | bytes 196616 | tf_op jit(solution)/shard_map/ppermute | solution.py:217
  30.6 2.8 %collective-permute-start.14 = (f32[1,128,128]{2,1,0:T(8,128)S(1)}, f32[1,128,128]{2,1,0:T(8,128)S(1)}, u32[]{:S(2)}, u32[]{:S(2)}) collective-permute-start(f32[1,128,128]{2,1,0:T(8,128)S(1)} %add_bitcast_fusion), channel_id=1, source_target_pairs={{0,1},{1,0},{2,3},{3,2},{4,5},{5,4},{6,7},{7,6},{8,9},{9,8},{10,11... | collective-permute-start | bytes 196616 | tf_op jit(solution)/shard_map/ppermute | solution.py:217
  33.2 1.3 %collective-permute-start.13 = (f32[1,128,128]{2,1,0:T(8,128)S(1)}, f32[1,128,128]{2,1,0:T(8,128)S(1)}, u32[]{:S(2)}, u32[]{:S(2)}) collective-permute-start(f32[1,128,128]{2,1,0:T(8,128)S(1)} %collective-permute-done.12.refs_2_), channel_id=1, source_target_pairs={{0,1},{1,0},{2,3},{3,2},{4,5},{5,4},{6,7},{7,6},{8,9},{9,8},{10,11... | collective-permute-start | bytes 196616 | tf_op jit(solution)/shard_map/ppermute | solution.py:217

commit v8 on v7

--- a/solution.py
+++ b/solution.py
@@ -112,19 +112,19 @@
 
 
 def section_map(inverse, link, order_only, out):
-    out[0] = -dot(inverse[0], link[0])
+    out[0] = -dot3(inverse[0], link[0])
 
 
 def leaf_base(rhs, leaf_inv, down, base, factors):
     order = down.shape[1]
     for k in range(base.shape[0]):
         gram = dot_ta(leaf_inv[0, k], leaf_inv[0, k])
-        base[k] = dot(gram, rhs[0, k])
+        base[k] = dot3(gram, rhs[0, k])
         factors[k * order : (k + 1) * order] = left(down[k].T)
 
 
 def own_columns(rhs, inverse, out):
-    out[...] = dot(inverse[0], rhs[0, :, columns_of(lax.axis_index("grp"), out.shape[1])])
+    out[...] = dot3(inverse[0], rhs[0, :, columns_of(lax.axis_index("grp"), out.shape[1])])
 
 
 def operator_rows(*refs):

time: 35.5 us -> 35.4 us (level)
  Pallas kernels: 7.87 us -> 7.38 us
  waiting for transfers between devices: 8.63 us -> 9.09 us
    pallas_call x10, Pallas kernels: 7.87 us -> 7.38 us  [call(): pl.pallas_call(body, out_shape=outs, in_specs=[HBM] * far + [VMEM] * (len...]
    ppermute x15, waiting for transfers between devices: 8.63 us -> 9.09 us  [swap(): return lax.ppermute(value, axis, [(i, i ^ bit) for i in range(count)])]
  transfers between devices with their start and end apart: 15 -> 15, of which waited for: 7 -> 7; matrix products, arithmetic and copies ran while one was open for 0% -> 0% of each run, Pallas kernels for 13% -> 12%
where the time goes in v8:
time: 35.4 us; the launch traced here: 35.3 us
  starting transfers between devices  17.9 us (51%)
  waiting for transfers between devices  9.09 us (26%)
  Pallas kernels  7.38 us (21%)
  between operations  0.8 us (2%)
    ppermute x15, starting transfers between devices, swap(): return lax.ppermute(value, axis, [(i, i ^ bit) for i in range(count)])  17.9 us
    ppermute x15, waiting for transfers between devices, swap(): return lax.ppermute(value, axis, [(i, i ^ bit) for i in range(count)])  9.09 us
    pallas_call x10, Pallas kernels, call(): pl.pallas_call(body, out_shape=outs, in_specs=[HBM] * far + [VMEM] * (len...  7.38 us
  transfers between devices with their start and end apart: 15, of which 7 were waited for; matrix products, arithmetic and copies ran while one was open for 0% of the time, Pallas kernels for 12%

profile of v8, /device:TPU:0, one launch (start us, length us, event | category | flops | bytes accessed | tf_op | source)
XLA Modules:
  0.0 35.3 jit_solution(6570119723579205132)
XLA Ops:
  0.7 2.0 %shard_map.86 = (f32[2,128,128]{2,1,0:T(8,128)S(1)}, f32[128,128]{1,0:T(8,128)S(1)}, f32[128,128]{1,0:T(8,128)S(1)}, f32[128,128]{1,0:T(8,128)S(1)}, f32[128,128]{1,0:T(8,128)S(1)}) custom-call(f32[1,128,128]{2,1,0:T(8,128)} %refs_2_.3, s32[1,2]{1,0:T(1,128)} %refs_1_.1, f32[1,2,128,128]{3,2,1,0:T(8,128)} %leaf_inv.1, f32[1,2,128,128]{3,2,1,0:T(8,128)} %refs_3_.1, ...), custom_call_target="tpu_custom_call" | custom-call | flops 1342177280 | bytes 62914560 | tf_op jit(solution)/shard_map/pallas_call | solution.py:56
  2.8 5.1 %collective-permute-start.2 = (f32[1,128,128]{2,1,0:T(8,128)S(1)}, f32[1,128,128]{2,1,0:T(8,128)S(1)}, u32[]{:S(2)}, u32[]{:S(2)}) collective-permute-start(f32[1,128,128]{2,1,0:T(8,128)S(1)} %shard_map.88.refs_0_), channel_id=1, source_target_pairs={{0,24},{4,28},{8,16},{12,20},{16,8},{20,12},{24,0},{28,4},{1,25},{... | collective-permute-start | bytes 196616 | tf_op jit(solution)/shard_map/ppermute | solution.py:217
  7.9 0.6 %collective-permute-start = (f32[1,128,128]{2,1,0:T(8,128)S(1)}, f32[1,128,128]{2,1,0:T(8,128)S(1)}, u32[]{:S(2)}, u32[]{:S(2)}) collective-permute-start(f32[1,128,128]{2,1,0:T(8,128)S(1)} %shard_map.88.refs_0_), channel_id=1, source_target_pairs={{0,8},{4,12},{8,0},{12,4},{16,24},{20,28},{24,16},{28,20},{1,9},{5... | collective-permute-start | bytes 196616 | tf_op jit(solution)/shard_map/ppermute | solution.py:217
  8.6 0.5 %collective-permute-start.6 = (f32[128,128]{1,0:T(8,128)S(1)}, f32[128,128]{1,0:T(8,128)S(1)}, u32[]{:S(2)}, u32[]{:S(2)}) collective-permute-start(f32[128,128]{1,0:T(8,128)S(1)} %get-tuple-element.17), channel_id=1, source_target_pairs={{0,1},{1,0},{2,3},{3,2},{4,5},{5,4},{6,7},{7,6},{8,9},{9,8},{10,11... | collective-permute-start | bytes 196616 | tf_op jit(solution)/shard_map/ppermute | solution.py:217
  9.3 0.7 %collective-permute-done.6 = f32[128,128]{1,0:T(8,128)S(1)} collective-permute-done((f32[128,128]{1,0:T(8,128)S(1)}, f32[128,128]{1,0:T(8,128)S(1)}, u32[]{:S(2)}, u32[]{:S(2)}) %collective-permute-start.6) | collective-permute-done | bytes 65568 | tf_op jit(solution)/shard_map/ppermute | solution.py:217
  10.0 1.7 %collective-permute-start.7 = (f32[128,128]{1,0:T(8,128)S(1)}, f32[128,128]{1,0:T(8,128)S(1)}, u32[]{:S(2)}, u32[]{:S(2)}) collective-permute-start(f32[128,128]{1,0:T(8,128)S(1)} %add.13), channel_id=1, source_target_pairs={{0,2},{1,3},{2,0},{3,1},{4,6},{5,7},{6,4},{7,5},{8,10},{9,11},{10,... | collective-permute-start | bytes 196616 | tf_op jit(solution)/shard_map/ppermute | solution.py:217
  11.7 1.8 %collective-permute-done.1.refs_2_ = f32[1,128,128]{2,1,0:T(8,128)S(1)} collective-permute-done((f32[1,128,128]{2,1,0:T(8,128)S(1)}, f32[1,128,128]{2,1,0:T(8,128)S(1)}, u32[]{:S(2)}, u32[]{:S(2)}) %collective-permute-start.1) | collective-permute-done | bytes 65568 | tf_op jit(solution)/shard_map/ppermute | solution.py:217
  13.6 1.6 %collective-permute-start.3 = (f32[3,128,128]{2,1,0:T(8,128)S(1)}, f32[3,128,128]{2,1,0:T(8,128)S(1)}, u32[]{:S(2)}, u32[]{:S(2)}) collective-permute-start(f32[3,128,128]{2,1,0:T(8,128)S(1)} %pad_maximum_fusion), channel_id=1, source_target_pairs={{0,4},{4,0},{8,12},{12,8},{16,20},{20,16},{24,28},{28,24},{1,5},{5... | collective-permute-start | bytes 589832 | tf_op jit(solution)/shard_map/ppermute | solution.py:217
  15.1 0.5 %collective-permute-start.4 = (f32[1,128,128]{2,1,0:T(8,128)S(1)}, f32[1,128,128]{2,1,0:T(8,128)S(1)}, u32[]{:S(2)}, u32[]{:S(2)}) collective-permute-start(f32[1,128,128]{2,1,0:T(8,128)S(1)} %collective-permute-done.2.refs_3_), channel_id=1, source_target_pairs={{0,4},{4,0},{8,12},{12,8},{16,20},{20,16},{24,28},{28,24},{1,5},{5... | collective-permute-start | bytes 196616 | tf_op jit(solution)/shard_map/ppermute | solution.py:217
  15.7 2.8 %collective-permute-start.10 = (f32[1,128,128]{2,1,0:T(8,128)S(1)}, f32[1,128,128]{2,1,0:T(8,128)S(1)}, u32[]{:S(2)}, u32[]{:S(2)}) collective-permute-start(f32[1,128,128]{2,1,0:T(8,128)S(1)} %subtract_bitcast_fusion.refs_2_), channel_id=1, source_target_pairs={{0,24},{4,28},{8,16},{12,20},{16,8},{20,12},{24,0},{28,4},{1,25},{... | collective-permute-start | bytes 196616 | tf_op jit(solution)/shard_map/ppermute | solution.py:217
  18.5 1.7 %collective-permute-start.8 = (f32[1,128,128]{2,1,0:T(8,128)S(1)}, f32[1,128,128]{2,1,0:T(8,128)S(1)}, u32[]{:S(2)}, u32[]{:S(2)}) collective-permute-start(f32[1,128,128]{2,1,0:T(8,128)S(1)} %subtract_bitcast_fusion.refs_2_), channel_id=1, source_target_pairs={{0,8},{4,12},{8,0},{12,4},{16,24},{20,28},{24,16},{28,20},{1,9},{5... | collective-permute-start | bytes 196616 | tf_op jit(solution)/shard_map/ppermute | solution.py:217
  20.2 0.6 %shard_map.87 = (f32[2,128,512]{2,1,0:T(8,128)S(1)}, bf16[256,384]{1,0:T(8,128)(2,1)S(1)}) custom-call(f32[1,2,128,512]{3,2,1,0:T(8,128)S(1)} %copy-done, f32[1,2,128,128]{3,2,1,0:T(8,128)S(1)} %copy-done.1, f32[2,128,128]{2,1,0:T(8,128)S(1)} %get-tuple-element.11.down.order_only.refs_1_), custom_call_target="tpu_custom_call" | custom-call | flops 41943040 | bytes 1572864 | tf_op jit(solution)/shard_map/pallas_call | solution.py:56
  20.8 0.7 %collective-permute-done.4.refs_5_ = f32[1,128,128]{2,1,0:T(8,128)S(1)} collective-permute-done((f32[1,128,128]{2,1,0:T(8,128)S(1)}, f32[1,128,128]{2,1,0:T(8,128)S(1)}, u32[]{:S(2)}, u32[]{:S(2)}) %collective-permute-start.4) | collective-permute-done | bytes 65568 | tf_op jit(solution)/shard_map/ppermute | solution.py:217
  21.5 1.9 %shard_map.89.refs_0_ = f32[8,256,128]{2,1,0:T(8,128)S(1)} custom-call(f32[1,128,128]{2,1,0:T(8,128)S(1)} %shard_map.88.refs_0_, f32[1,128,128]{2,1,0:T(8,128)S(1)} %collective-permute-done.refs_1_, f32[1,128,128]{2,1,0:T(8,128)S(1)} %collective-permute-done.1.refs_2_, f32[1,128,128]{2,1,0:T(8,128)S(1)} %collective-permute-done.2.refs_3_, ...), custom_call_target="tpu_custom_call" | custom-call | flops 134217728 | bytes 2097152 | tf_op jit(solution)/shard_map/pallas_call | solution.py:56
  23.4 0.8 %collective-permute-done.9.refs_4_ = f32[1,128,128]{2,1,0:T(8,128)S(1)} collective-permute-done((f32[1,128,128]{2,1,0:T(8,128)S(1)}, f32[1,128,128]{2,1,0:T(8,128)S(1)}, u32[]{:S(2)}, u32[]{:S(2)}) %collective-permute-start.9) | collective-permute-done | bytes 65568 | tf_op jit(solution)/shard_map/ppermute | solution.py:217
  24.2 0.3 shard_map.92
  24.5 1.7 %collective-permute-start.11 = (f32[128,128]{1,0:T(8,128)S(1)}, f32[128,128]{1,0:T(8,128)S(1)}, u32[]{:S(2)}, u32[]{:S(2)}) collective-permute-start(f32[128,128]{1,0:T(8,128)S(1)} %shard_map.92), channel_id=1, source_target_pairs={{0,4},{4,0},{8,12},{12,8},{16,20},{20,16},{24,28},{28,24},{1,5},{5... | collective-permute-start | bytes 196616 | tf_op jit(solution)/shard_map/ppermute | solution.py:217
  26.2 0.3 shard_map.91
  26.5 2.3 %collective-permute-done.11 = f32[128,128]{1,0:T(8,128)S(1)} collective-permute-done((f32[128,128]{1,0:T(8,128)S(1)}, f32[128,128]{1,0:T(8,128)S(1)}, u32[]{:S(2)}, u32[]{:S(2)}) %collective-permute-start.11) | collective-permute-done | bytes 65568 | tf_op jit(solution)/shard_map/ppermute | solution.py:217
  28.8 1.7 %collective-permute-start.12 = (f32[1,128,128]{2,1,0:T(8,128)S(1)}, f32[1,128,128]{2,1,0:T(8,128)S(1)}, u32[]{:S(2)}, u32[]{:S(2)}) collective-permute-start(f32[1,128,128]{2,1,0:T(8,128)S(1)} %add_bitcast_fusion), channel_id=1, source_target_pairs={{0,2},{1,3},{2,0},{3,1},{4,6},{5,7},{6,4},{7,5},{8,10},{9,11},{10,... | collective-permute-start | bytes 196616 | tf_op jit(solution)/shard_map/ppermute | solution.py:217
  30.5 2.6 %collective-permute-done.12.refs_2_ = f32[1,128,128]{2,1,0:T(8,128)S(1)} collective-permute-done((f32[1,128,128]{2,1,0:T(8,128)S(1)}, f32[1,128,128]{2,1,0:T(8,128)S(1)}, u32[]{:S(2)}, u32[]{:S(2)}) %collective-permute-start.12) | collective-permute-done | bytes 65568 | tf_op jit(solution)/shard_map/ppermute | solution.py:217
  33.2 0.2 shard_map.94.refs_4_
  33.4 0.9 %shard_map.93 = (f32[2,2,128,128]{3,2,1,0:T(8,128)S(1)}, f32[1,128,128]{2,1,0:T(8,128)}) custom-call(f32[2,128,512]{2,1,0:T(8,128)S(1)} %get-tuple-element.12.refs_0_, bf16[256,384]{1,0:T(8,128)(2,1)S(1)} %get-tuple-element.13.refs_1_, f32[1,128,128]{2,1,0:T(8,128)S(1)} %copy-done.2, f32[2,128,128]{2,1,0:T(8,128)S(1)} %pad_maximum_fusion.1.refs_3_), custom_call_target="tpu_custom_call" | custom-call | flops 20971520 | bytes 524288 | tf_op jit(solution)/shard_map/pallas_call | solution.py:56
  34.4 0.9 %shard_map.95 = f32[1,2,128,512]{3,2,1,0:T(8,128)} custom-call(f32[2,128,512]{2,1,0:T(8,128)S(1)} %get-tuple-element.12.refs_0_, bf16[256,384]{1,0:T(8,128)(2,1)S(1)} %get-tuple-element.13.refs_1_, f32[1,128,128]{2,1,0:T(8,128)S(1)} %collective-permute-done.13.refs_2_, f32[2,2,128,128]{3,2,1,0:T(8,128)S(1)} %get-tuple-element.18.refs_3_, ...), custom_call_target="tpu_custom_call" | custom-call | flops 8388608 | bytes 1048576 | tf_op jit(solution)/shard_map/pallas_call | solution.py:56
  (31 shorter events, 0.5 us)
Async XLA Ops:
  0.6 2.0 %copy-start.2 = (f32[1,128,128]{2,1,0:T(8,128)S(1)}, f32[1,128,128]{2,1,0:T(8,128)}, u32[]{:S(2)}) copy-start(f32[1,128,128]{2,1,0:T(8,128)} %refs_2_.3) | copy-start | bytes 196612
  0.6 2.0 %copy-start.4 = (f32[1,128,128]{2,1,0:T(8,128)S(1)}, f32[1,128,128]{2,1,0:T(8,128)}, u32[]{:S(2)}) copy-start(f32[1,128,128]{2,1,0:T(8,128)} %link.1) | copy-start | bytes 196612
  2.6 6.5 %copy-start.3 = (f32[1,128,512]{2,1,0:T(8,128)S(1)}, f32[1,128,512]{2,1,0:T(8,128)}, u32[]{:S(2)}) copy-start(f32[1,128,512]{2,1,0:T(8,128)} %rhs.3) | copy-start | bytes 786436
  2.8 12.3 %collective-permute-start.2 = (f32[1,128,128]{2,1,0:T(8,128)S(1)}, f32[1,128,128]{2,1,0:T(8,128)S(1)}, u32[]{:S(2)}, u32[]{:S(2)}) collective-permute-start(f32[1,128,128]{2,1,0:T(8,128)S(1)} %shard_map.88.refs_0_), channel_id=1, source_target_pairs={{0,24},{4,28},{8,16},{12,20},{16,8},{20,12},{24,0},{28,4},{1,25},{... | collective-permute-start | bytes 196616 | tf_op jit(solution)/shard_map/ppermute | solution.py:217
  7.9 5.6 %collective-permute-start.1 = (f32[1,128,128]{2,1,0:T(8,128)S(1)}, f32[1,128,128]{2,1,0:T(8,128)S(1)}, u32[]{:S(2)}, u32[]{:S(2)}) collective-permute-start(f32[1,128,128]{2,1,0:T(8,128)S(1)} %shard_map.88.refs_0_), channel_id=1, source_target_pairs={{0,16},{4,20},{8,24},{12,28},{16,0},{20,4},{24,8},{28,12},{1,17},{... | collective-permute-start | bytes 196616 | tf_op jit(solution)/shard_map/ppermute | solution.py:217
  7.9 5.6 %collective-permute-start = (f32[1,128,128]{2,1,0:T(8,128)S(1)}, f32[1,128,128]{2,1,0:T(8,128)S(1)}, u32[]{:S(2)}, u32[]{:S(2)}) collective-permute-start(f32[1,128,128]{2,1,0:T(8,128)S(1)} %shard_map.88.refs_0_), channel_id=1, source_target_pairs={{0,8},{4,12},{8,0},{12,4},{16,24},{20,28},{24,16},{28,20},{1,9},{5... | collective-permute-start | bytes 196616 | tf_op jit(solution)/shard_map/ppermute | solution.py:217
  8.6 7.1 %collective-permute-start.5 = (f32[128,128]{1,0:T(8,128)S(1)}, f32[128,128]{1,0:T(8,128)S(1)}, u32[]{:S(2)}, u32[]{:S(2)}) collective-permute-start(f32[128,128]{1,0:T(8,128)S(1)} %get-tuple-element.15), channel_id=1, source_target_pairs={{0,1},{1,0},{2,3},{3,2},{4,5},{5,4},{6,7},{7,6},{8,9},{9,8},{10,11... | collective-permute-start | bytes 196616 | tf_op jit(solution)/shard_map/ppermute | solution.py:217
  8.6 1.4 %collective-permute-start.6 = (f32[128,128]{1,0:T(8,128)S(1)}, f32[128,128]{1,0:T(8,128)S(1)}, u32[]{:S(2)}, u32[]{:S(2)}) collective-permute-start(f32[128,128]{1,0:T(8,128)S(1)} %get-tuple-element.17), channel_id=1, source_target_pairs={{0,1},{1,0},{2,3},{3,2},{4,5},{5,4},{6,7},{7,6},{8,9},{9,8},{10,11... | collective-permute-start | bytes 196616 | tf_op jit(solution)/shard_map/ppermute | solution.py:217
  9.3 10.9 %copy-start = (f32[1,2,128,512]{3,2,1,0:T(8,128)S(1)}, f32[1,2,128,512]{3,2,1,0:T(8,128)}, u32[]{:S(2)}) copy-start(f32[1,2,128,512]{3,2,1,0:T(8,128)} %rhs.2) | copy-start | bytes 1572868
  10.0 5.7 %collective-permute-start.7 = (f32[128,128]{1,0:T(8,128)S(1)}, f32[128,128]{1,0:T(8,128)S(1)}, u32[]{:S(2)}, u32[]{:S(2)}) collective-permute-start(f32[128,128]{1,0:T(8,128)S(1)} %add.13), channel_id=1, source_target_pairs={{0,2},{1,3},{2,0},{3,1},{4,6},{5,7},{6,4},{7,5},{8,10},{9,11},{10,... | collective-permute-start | bytes 196616 | tf_op jit(solution)/shard_map/ppermute | solution.py:217
  13.6 7.9 %collective-permute-start.3 = (f32[3,128,128]{2,1,0:T(8,128)S(1)}, f32[3,128,128]{2,1,0:T(8,128)S(1)}, u32[]{:S(2)}, u32[]{:S(2)}) collective-permute-start(f32[3,128,128]{2,1,0:T(8,128)S(1)} %pad_maximum_fusion), channel_id=1, source_target_pairs={{0,4},{4,0},{8,12},{12,8},{16,20},{20,16},{24,28},{28,24},{1,5},{5... | collective-permute-start | bytes 589832 | tf_op jit(solution)/shard_map/ppermute | solution.py:217
  15.1 6.4 %collective-permute-start.4 = (f32[1,128,128]{2,1,0:T(8,128)S(1)}, f32[1,128,128]{2,1,0:T(8,128)S(1)}, u32[]{:S(2)}, u32[]{:S(2)}) collective-permute-start(f32[1,128,128]{2,1,0:T(8,128)S(1)} %collective-permute-done.2.refs_3_), channel_id=1, source_target_pairs={{0,4},{4,0},{8,12},{12,8},{16,20},{20,16},{24,28},{28,24},{1,5},{5... | collective-permute-start | bytes 196616 | tf_op jit(solution)/shard_map/ppermute | solution.py:217
  15.7 4.5 %copy-start.1 = (f32[1,2,128,128]{3,2,1,0:T(8,128)S(1)}, f32[1,2,128,128]{3,2,1,0:T(8,128)}, u32[]{:S(2)}) copy-start(f32[1,2,128,128]{3,2,1,0:T(8,128)} %leaf_inv.1) | copy-start | bytes 393220
  15.7 7.7 %collective-permute-start.10 = (f32[1,128,128]{2,1,0:T(8,128)S(1)}, f32[1,128,128]{2,1,0:T(8,128)S(1)}, u32[]{:S(2)}, u32[]{:S(2)}) collective-permute-start(f32[1,128,128]{2,1,0:T(8,128)S(1)} %subtract_bitcast_fusion.refs_2_), channel_id=1, source_target_pairs={{0,24},{4,28},{8,16},{12,20},{16,8},{20,12},{24,0},{28,4},{1,25},{... | collective-permute-start | bytes 196616 | tf_op jit(solution)/shard_map/ppermute | solution.py:217
  18.5 5.7 %collective-permute-start.9 = (f32[1,128,128]{2,1,0:T(8,128)S(1)}, f32[1,128,128]{2,1,0:T(8,128)S(1)}, u32[]{:S(2)}, u32[]{:S(2)}) collective-permute-start(f32[1,128,128]{2,1,0:T(8,128)S(1)} %subtract_bitcast_fusion.refs_2_), channel_id=1, source_target_pairs={{0,16},{4,20},{8,24},{12,28},{16,0},{20,4},{24,8},{28,12},{1,17},{... | collective-permute-start | bytes 196616 | tf_op jit(solution)/shard_map/ppermute | solution.py:217
  18.5 5.7 %collective-permute-start.8 = (f32[1,128,128]{2,1,0:T(8,128)S(1)}, f32[1,128,128]{2,1,0:T(8,128)S(1)}, u32[]{:S(2)}, u32[]{:S(2)}) collective-permute-start(f32[1,128,128]{2,1,0:T(8,128)S(1)} %subtract_bitcast_fusion.refs_2_), channel_id=1, source_target_pairs={{0,8},{4,12},{8,0},{12,4},{16,24},{20,28},{24,16},{28,20},{1,9},{5... | collective-permute-start | bytes 196616 | tf_op jit(solution)/shard_map/ppermute | solution.py:217
  24.5 4.3 %collective-permute-start.11 = (f32[128,128]{1,0:T(8,128)S(1)}, f32[128,128]{1,0:T(8,128)S(1)}, u32[]{:S(2)}, u32[]{:S(2)}) collective-permute-start(f32[128,128]{1,0:T(8,128)S(1)} %shard_map.92), channel_id=1, source_target_pairs={{0,4},{4,0},{8,12},{12,8},{16,20},{20,16},{24,28},{28,24},{1,5},{5... | collective-permute-start | bytes 196616 | tf_op jit(solution)/shard_map/ppermute | solution.py:217
  28.8 4.3 %collective-permute-start.12 = (f32[1,128,128]{2,1,0:T(8,128)S(1)}, f32[1,128,128]{2,1,0:T(8,128)S(1)}, u32[]{:S(2)}, u32[]{:S(2)}) collective-permute-start(f32[1,128,128]{2,1,0:T(8,128)S(1)} %add_bitcast_fusion), channel_id=1, source_target_pairs={{0,2},{1,3},{2,0},{3,1},{4,6},{5,7},{6,4},{7,5},{8,10},{9,11},{10,... | collective-permute-start | bytes 196616 | tf_op jit(solution)/shard_map/ppermute | solution.py:217
  30.5 2.8 %collective-permute-start.14 = (f32[1,128,128]{2,1,0:T(8,128)S(1)}, f32[1,128,128]{2,1,0:T(8,128)S(1)}, u32[]{:S(2)}, u32[]{:S(2)}) collective-permute-start(f32[1,128,128]{2,1,0:T(8,128)S(1)} %add_bitcast_fusion), channel_id=1, source_target_pairs={{0,1},{1,0},{2,3},{3,2},{4,5},{5,4},{6,7},{7,6},{8,9},{9,8},{10,11... | collective-permute-start | bytes 196616 | tf_op jit(solution)/shard_map/ppermute | solution.py:217
  33.2 1.3 %collective-permute-start.13 = (f32[1,128,128]{2,1,0:T(8,128)S(1)}, f32[1,128,128]{2,1,0:T(8,128)S(1)}, u32[]{:S(2)}, u32[]{:S(2)}) collective-permute-start(f32[1,128,128]{2,1,0:T(8,128)S(1)} %collective-permute-done.12.refs_2_), channel_id=1, source_target_pairs={{0,1},{1,0},{2,3},{3,2},{4,5},{5,4},{6,7},{7,6},{8,9},{9,8},{10,11... | collective-permute-start | bytes 196616 | tf_op jit(solution)/shard_map/ppermute | solution.py:217
